TPU v7x, 128 devices: a whole 4x4x4 slice. The times are simulated.
128 devices in a mesh: dp: 8 (over z, core), expert: 16 (over y, x).
Axes of the slice: x: 4, y: 4, z: 4, core: 2. Of those that a mesh axis runs over, the one named last changes fastest.
Arguments:
- tokens: bfloat16 [16384, 4096], P(('dp', 'expert')), may hold values from -24 to 24
- cotangent: bfloat16 [16384, 4096], P(('dp', 'expert')), may hold values from -6 to 6
- expert_ids: int32 [16384, 8], P(('dp', 'expert')), may hold values from 0 to 15, all different within a row; in each aligned block of 128 rows (0 to 127, 128 to 255, ...) at most 72 rows name the same one
- route_weight: float32 [16384, 8], P(('dp', 'expert')), may hold values from 0.02 to 0.5
- up_weight: bfloat16 [16, 4096, 768], P('expert'), may hold values from -0.09375 to 0.09375
- down_weight: bfloat16 [16, 768, 4096], P('expert'), may hold values from -0.21875 to 0.21875
Outputs:
- token_grad: bfloat16 [16384, 4096], P(('dp', 'expert'))
- up_grad: float32 [16, 4096, 768], P('expert', 'dp')
- down_grad: float32 [16, 768, 4096], P('expert', 'dp')
Inputs may be any that keep to these rules, and one draw needn't show every extreme that they name: `expert_ids`: each row names 8 different experts. Among the 128 tokens of one device (aligned blocks) no expert is named more than 72 times, a bound that some block reaches.
All inputs are finite; a program needn't handle non-finite values.
Results may differ from a plain program's by a relative error of at most 0.017.
Values may be sent and summed in bfloat16 or wider, within the bound.
No kernel may reach another device: no remote copies, remote signals or barrier semaphores. Data moves between devices by JAX's collectives and lax.ppermute only.
A program may use at most 192 MiB of HBM per device.

v0:
```python
import functools

import jax
import jax.numpy as jnp
from jax import lax
from jax.experimental import pallas as pl
from jax.experimental.pallas import tpu as pltpu
from jax.sharding import PartitionSpec as P

SIDE = 4
OFFSETS = (0, 1, 3, 2)
SLOTS = 72
BOTH = ("dp", "expert")
TILE = 1024
ROWS = SIDE * SLOTS
WIDE = 3 * ROWS
COLS_LAST = (((1,), (1,)), ((), ()))
ROWS_FIRST = (((0,), (0,)), ((), ()))
VMEM_LIMIT = 58 * 1024 * 1024


def cost(m, k, n):
    return pl.CostEstimate(
        flops=2 * m * k * n, bytes_accessed=2 * (m * k + k * n + m * n), transcendentals=0
    )


HEAVY = pl.CostEstimate(flops=30_000_000_000, bytes_accessed=1, transcendentals=0)
LIGHT = pl.CostEstimate(flops=1_000_000, bytes_accessed=1, transcendentals=0)
PARAMS = pltpu.CompilerParams(vmem_limit_bytes=VMEM_LIMIT)


def ring(first, shift):
    pairs = []
    for dp in range(8):
        along_x = first == (dp % 2 == 0)
        for y in range(SIDE):
            for x in range(SIDE):
                to = y * SIDE + (x + shift) % SIDE if along_x else ((y + shift) % SIDE) * SIDE + x
                pairs.append((dp * 16 + y * SIDE + x, dp * 16 + to))
    return pairs


def send(value, first, shift):
    shift = shift % SIDE
    return value if shift == 0 else lax.ppermute(value, BOTH, ring(first, shift))


def route_kernel(dest_ref, m0, m1, m2, m3, pick_ref, put_ref, weight_ref):
    rows = lax.broadcasted_iota(jnp.int32, (16, 128), 0)
    masks = jnp.zeros((16, 128), jnp.float32)
    weights = []
    for i, meta in enumerate((m0, m1, m2, m3)):
        packed = meta[...].astype(jnp.float32)
        ids = packed[:, 0:128]
        route = packed[:, 128:256] + packed[:, 256:384] + packed[:, 384:512]
        for j in range(SIDE):
            hit = ids == dest_ref[j].astype(jnp.float32)
            mask = jnp.sum(jnp.where(hit, 1.0, 0.0), axis=0, keepdims=True)
            weights.append(jnp.sum(jnp.where(hit, route, 0.0), axis=0, keepdims=True))
            masks = jnp.where(rows == i * SIDE + j, mask, masks)
    before = lax.broadcasted_iota(jnp.int32, (128, 128), 0) < lax.broadcasted_iota(
        jnp.int32, (128, 128), 1
    )
    rank = jnp.dot(
        masks.astype(jnp.bfloat16),
        before.astype(jnp.float32).astype(jnp.bfloat16),
        preferred_element_type=jnp.float32,
    )
    rank = jnp.where(masks > 0.5, rank, -1.0)
    slot = lax.broadcasted_iota(jnp.int32, (SLOTS, 128), 0).astype(jnp.float32)
    for i in range(SIDE):
        for j in range(SIDE):
            n = i * SIDE + j
            pick = jnp.where(slot == rank[n : n + 1, :], 1.0, 0.0)
            pick_ref[i, j * SLOTS : (j + 1) * SLOTS, :] = pick.astype(jnp.bfloat16)
            put_ref[i, j, :, :] = pick.T.astype(jnp.bfloat16)
            column = jnp.sum(pick * weights[n], axis=1, keepdims=True)
            weight_ref[i, j * SLOTS : (j + 1) * SLOTS, :] = jnp.broadcast_to(column, (SLOTS, 128))


def route(dest, blocks):
    return pl.pallas_call(
        route_kernel,
        out_shape=(
            jax.ShapeDtypeStruct((SIDE, SIDE * SLOTS, 128), jnp.bfloat16),
            jax.ShapeDtypeStruct((SIDE, SIDE, 128, SLOTS), jnp.bfloat16),
            jax.ShapeDtypeStruct((SIDE, SIDE * SLOTS, 128), jnp.float32),
        ),
        grid=(1,),
        in_specs=[pl.BlockSpec(memory_space=pltpu.SMEM)]
        + [pl.BlockSpec((8, 512), lambda c: (16, 0))] * SIDE,
        out_specs=(
            pl.BlockSpec((SIDE, ROWS, 128), lambda c: (0, 0, 0)),
            pl.BlockSpec((SIDE, SIDE, 128, SLOTS), lambda c: (0, 0, 0, 0)),
            pl.BlockSpec((SIDE, ROWS, 128), lambda c: (0, 0, 0)),
        ),
        cost_estimate=LIGHT,
        name="route",
    )(dest, *blocks)


def select_kernel(scaled, pick_ref, weight_ref, b0, b1, b2, b3, o0, o1, o2, o3):
    outs = (o0, o1, o2, o3)
    for i, block in enumerate((b0, b1, b2, b3)):
        rows = jnp.dot(pick_ref[i], block[...], preferred_element_type=jnp.float32)
        if scaled:
            rows = rows * weight_ref[i][:, 0:1]
        rows = rows.astype(jnp.bfloat16)
        for j in range(SIDE):
            outs[j][i, :, :] = rows[j * SLOTS : (j + 1) * SLOTS, :]


def select(pick, weight, blocks, scaled):
    width = blocks[0].shape[1]
    tile = TILE
    return pl.pallas_call(
        functools.partial(select_kernel, scaled),
        out_shape=(jax.ShapeDtypeStruct((SIDE, SLOTS, width), jnp.bfloat16),) * SIDE,
        grid=(width // tile,),
        in_specs=[
            pl.BlockSpec((SIDE, SIDE * SLOTS, 128), lambda c: (0, 0, 0)),
            pl.BlockSpec((SIDE, SIDE * SLOTS, 128), lambda c: (0, 0, 0)),
        ]
        + [pl.BlockSpec((128, tile), lambda c: (0, c))] * SIDE,
        out_specs=(pl.BlockSpec((SIDE, SLOTS, tile), lambda c: (0, 0, c)),) * SIDE,
        compiler_params=PARAMS,
        cost_estimate=HEAVY,
        name="select_scaled" if scaled else "select",
    )(pick, weight, *blocks)


def combine_kernel(put_ref, r0, r1, r2, r3, o0, o1, o2, o3):
    returned = (r0, r1, r2, r3)
    for i, out in enumerate((o0, o1, o2, o3)):
        total = jnp.dot(put_ref[i, 0], r0[i], preferred_element_type=jnp.float32)
        for j in range(1, SIDE):
            total += jnp.dot(put_ref[i, j], returned[j][i], preferred_element_type=jnp.float32)
        out[...] = total.astype(jnp.bfloat16)


def combine(put, returned):
    width = returned[0].shape[2]
    tile = TILE
    return pl.pallas_call(
        combine_kernel,
        out_shape=(jax.ShapeDtypeStruct((128, width), jnp.bfloat16),) * SIDE,
        grid=(width // tile,),
        in_specs=[pl.BlockSpec((SIDE, SIDE, 128, SLOTS), lambda c: (0, 0, 0, 0))]
        + [pl.BlockSpec((SIDE, SLOTS, tile), lambda c: (0, 0, c))] * SIDE,
        out_specs=(pl.BlockSpec((128, tile), lambda c: (0, c)),) * SIDE,
        compiler_params=PARAMS,
        cost_estimate=LIGHT,
        name="combine",
    )(put, *returned)


def dot(a, b, dims=(((1,), (0,)), ((), ()))):
    return lax.dot_general(a, b, dims, preferred_element_type=jnp.float32)


def stacked(refs):
    return jnp.concatenate([r[...] for r in refs], axis=0)


def pre_kernel(*refs):
    xs, up, pre, wide, last = refs[:SIDE], refs[SIDE], *refs[SIDE + 1 :]
    step = pl.program_id(0)
    part = dot(stacked(xs), up[...])

    @pl.when(step == 0)
    def _():
        pre[...] = part

    @pl.when(step > 0)
    def _():
        pre[...] += part

    @pl.when(step == pl.num_programs(0) - 1)
    def _():
        for rows, out in ((slice(0, WIDE), wide), (slice(WIDE, WIDE + ROWS), last)):
            value = pre[rows, :]
            out[...] = (value * jax.nn.sigmoid(value)).T.astype(jnp.bfloat16)


def expert_pre(xs, up):
    width, hidden = up.shape
    return pl.pallas_call(
        pre_kernel,
        out_shape=(
            jax.ShapeDtypeStruct((WIDE + ROWS, hidden), jnp.float32),
            jax.ShapeDtypeStruct((hidden, WIDE), jnp.bfloat16),
            jax.ShapeDtypeStruct((hidden, ROWS), jnp.bfloat16),
        ),
        grid=(width // TILE,),
        in_specs=[pl.BlockSpec((ROWS, TILE), lambda c: (0, c))] * SIDE
        + [pl.BlockSpec((TILE, hidden), lambda c: (c, 0))],
        out_specs=(
            pl.BlockSpec((WIDE + ROWS, hidden), lambda c: (0, 0)),
            pl.BlockSpec((hidden, WIDE), lambda c: (0, 0)),
            pl.BlockSpec((hidden, ROWS), lambda c: (0, 0)),
        ),
        compiler_params=PARAMS,
        cost_estimate=cost(WIDE + ROWS, width, hidden),
        name="expert_pre",
    )(*xs, up)


def back_kernel(n, *refs):
    gs, pre, down, up, grad, rows, back = refs[:n], *refs[n : n + 4], refs[n + 4 : -1], refs[-1]
    step = pl.program_id(0)
    half = pl.num_programs(0) // 2

    @pl.when(step == 0)
    def _():
        back[...] = dot(stacked(gs), down[...], COLS_LAST)

    @pl.when(jnp.logical_and(step > 0, step < half))
    def _():
        back[...] += dot(stacked(gs), down[...], COLS_LAST)

    @pl.when(step == half - 1)
    def _():
        value = pre[...]
        sigma = jax.nn.sigmoid(value)
        grad[...] = (back[...] * sigma * (1.0 + value * (1.0 - sigma))).astype(jnp.bfloat16)

    @pl.when(step >= half)
    def _():
        out = dot(grad[...], up[...], COLS_LAST).astype(jnp.bfloat16)
        for i in range(n):
            rows[i][...] = out[i * ROWS : (i + 1) * ROWS, :]


def expert_back(gs, pre, place, down, up):
    n, (width, hidden) = len(gs), up.shape
    tiles = width // TILE
    out = pl.pallas_call(
        functools.partial(back_kernel, n),
        out_shape=(jax.ShapeDtypeStruct((n * ROWS, hidden), jnp.bfloat16),)
        + (jax.ShapeDtypeStruct((ROWS, width), jnp.bfloat16),) * n,
        grid=(2 * tiles,),
        in_specs=[pl.BlockSpec((ROWS, TILE), lambda c: (0, jnp.minimum(c, tiles - 1)))] * n
        + [
            pl.BlockSpec((n * ROWS, hidden), lambda c: (place, 0)),
            pl.BlockSpec((hidden, TILE), lambda c: (0, jnp.minimum(c, tiles - 1))),
            pl.BlockSpec((TILE, hidden), lambda c: (jnp.maximum(c - tiles, 0), 0)),
        ],
        out_specs=(pl.BlockSpec((n * ROWS, hidden), lambda c: (0, 0)),)
        + (pl.BlockSpec((ROWS, TILE), lambda c: (0, jnp.maximum(c - tiles, 0))),) * n,
        scratch_shapes=[pltpu.VMEM((n * ROWS, hidden), jnp.float32)],
        compiler_params=PARAMS,
        cost_estimate=cost(2 * n * ROWS, width, hidden) if n > 1 else LIGHT,
        name="expert_back",
    )(*gs, pre, down, up)
    return out[0], list(out[1:])


def up_first_kernel(x0, x1, x2, grad, out):
    out[...] = dot(stacked((x0, x1, x2)), grad[...], ROWS_FIRST)


def up_first(xs, grad):
    width, hidden = xs[0].shape[1], grad.shape[1]
    return pl.pallas_call(
        up_first_kernel,
        out_shape=jax.ShapeDtypeStruct((width, hidden), jnp.float32),
        grid=(width // TILE,),
        in_specs=[pl.BlockSpec((ROWS, TILE), lambda c: (0, c))] * 3
        + [pl.BlockSpec((WIDE, hidden), lambda c: (0, 0))],
        out_specs=pl.BlockSpec((TILE, hidden), lambda c: (c, 0)),
        compiler_params=PARAMS,
        cost_estimate=cost(width, WIDE, hidden),
        name="up_first",
    )(*xs, grad)


def down_first_kernel(act, g0, g1, g2, out):
    out[...] = dot(act[...], stacked((g0, g1, g2)))


def down_first(act, gs):
    width, hidden = gs[0].shape[1], act.shape[0]
    return pl.pallas_call(
        down_first_kernel,
        out_shape=jax.ShapeDtypeStruct((hidden, width), jnp.float32),
        grid=(width // TILE,),
        in_specs=[pl.BlockSpec((hidden, WIDE), lambda c: (0, 0))]
        + [pl.BlockSpec((ROWS, TILE), lambda c: (0, c))] * 3,
        out_specs=pl.BlockSpec((hidden, TILE), lambda c: (0, c)),
        compiler_params=PARAMS,
        cost_estimate=cost(hidden, WIDE, width),
        name="down_first",
    )(act, *gs)


def up_last_kernel(idx, x, grad, acc, give, keep):
    total = (acc[...] + dot(x[...], grad[...], ROWS_FIRST)).astype(jnp.bfloat16)
    half = total.shape[0] // 2

    @pl.when(idx[SIDE] == 0)
    def _():
        keep[0], give[0] = total[:half], total[half:]

    @pl.when(idx[SIDE] == 1)
    def _():
        give[0], keep[0] = total[:half], total[half:]


def up_last(idx, x, grad, acc):
    width, hidden = acc.shape
    tile = width // SIDE
    slab = pl.BlockSpec((1, tile // 2, hidden), lambda s, idx: (s, 0, 0))
    return pl.pallas_call(
        up_last_kernel,
        out_shape=(jax.ShapeDtypeStruct((SIDE, tile // 2, hidden), jnp.bfloat16),) * 2,
        grid_spec=pltpu.PrefetchScalarGridSpec(
            num_scalar_prefetch=1,
            grid=(SIDE,),
            in_specs=[
                pl.BlockSpec((ROWS, tile), lambda s, idx: (0, idx[s])),
                pl.BlockSpec((ROWS, hidden), lambda s, idx: (0, 0)),
                pl.BlockSpec((tile, hidden), lambda s, idx: (idx[s], 0)),
            ],
            out_specs=(slab, slab),
        ),
        compiler_params=PARAMS,
        cost_estimate=LIGHT,
        name="up_last",
    )(idx, x, grad, acc)


def down_last_kernel(idx, act, g, acc, give, keep, total):
    value = acc[...] + dot(act[...], g[...])
    total[...] = value.reshape(total.shape)
    core = idx[SIDE]
    for s in range(SIDE):
        keep[s] = total[2 * idx[s] + core].astype(jnp.bfloat16)
        give[s] = total[2 * idx[s] + 1 - core].astype(jnp.bfloat16)


def down_last(idx, act, g, acc):
    hidden, width = acc.shape
    part = hidden // 8
    slab = pl.BlockSpec((SIDE, part, TILE), lambda c, idx: (0, 0, c))
    return pl.pallas_call(
        down_last_kernel,
        out_shape=(jax.ShapeDtypeStruct((SIDE, part, width), jnp.bfloat16),) * 2,
        grid_spec=pltpu.PrefetchScalarGridSpec(
            num_scalar_prefetch=1,
            grid=(width // TILE,),
            in_specs=[
                pl.BlockSpec((hidden, ROWS), lambda c, idx: (0, 0)),
                pl.BlockSpec((ROWS, TILE), lambda c, idx: (0, c)),
                pl.BlockSpec((hidden, TILE), lambda c, idx: (0, c)),
            ],
            out_specs=(slab, slab),
            scratch_shapes=[pltpu.VMEM((8, part, TILE), jnp.float32)],
        ),
        compiler_params=PARAMS,
        cost_estimate=LIGHT,
        name="down_last",
    )(idx, act, g, acc)


def swap_cores(value):
    return lax.ppermute(value, "dp", [(d, d ^ 1) for d in range(8)])


def send_z(value, shift):
    pairs = [(z * 2 + c, (z + shift) % SIDE * 2 + c) for z in range(SIDE) for c in range(2)]
    return value if shift == 0 else lax.ppermute(value, "dp", pairs)


def pairs_kernel(own, other, *outs):
    total = own[...].astype(jnp.float32) + other[...].astype(jnp.float32)
    for i, out in enumerate(outs):
        out[...] = total[i].astype(jnp.bfloat16)


def sum_pairs(own, other, dim):
    _, rows, columns = own.shape
    tile = (rows // SIDE, columns) if dim == 0 else (rows, columns // SIDE)

    def index(c):
        return (c, 0) if dim == 0 else (0, c)

    return pl.pallas_call(
        pairs_kernel,
        out_shape=(jax.ShapeDtypeStruct((rows, columns), jnp.bfloat16),) * SIDE,
        grid=(SIDE,),
        in_specs=[pl.BlockSpec((SIDE, *tile), lambda c: (0, *index(c)))] * 2,
        out_specs=(pl.BlockSpec(tile, index),) * SIDE,
        compiler_params=PARAMS,
        cost_estimate=LIGHT,
        name="sum_pairs",
    )(own, other)


def after(value, *earlier):
    return lax.optimization_barrier((value, *earlier))[0]


def body(tokens, cotangent, expert_ids, route_weight, up_weight, down_weight):
    width = tokens.shape[1]
    up_matrix = up_weight[0]
    down_matrix = down_weight[0]
    dp = lax.axis_index("dp")
    core, z = dp & 1, dp >> 1
    place = lax.axis_index("expert")
    y, x = place >> 2, place & 3
    shifts = jnp.array(OFFSETS, jnp.int32)
    dest = jnp.where(core == 1, y * SIDE + ((x + shifts) & 3), ((y + shifts) & 3) * SIDE + x)
    pieces = jnp.concatenate([(z + shifts) & 3, core[None]])
    high = lax.reduce_precision(route_weight, 8, 7)
    middle = lax.reduce_precision(route_weight - high, 8, 7)
    low = route_weight - high - middle
    meta = jnp.concatenate(
        [m.astype(jnp.bfloat16).T for m in (expert_ids, high, middle, low)], axis=1
    )
    message = jnp.concatenate([tokens, jnp.pad(meta, ((0, 0), (0, width - 512)))], axis=0)

    with jax.named_scope("p1x"):
        token_blocks = [send(message, True, o) for o in OFFSETS]
    cotangent = after(cotangent, *token_blocks)
    with jax.named_scope("p1g"):
        cot_blocks = [send(cotangent, True, o) for o in OFFSETS]
    pick, put, weight = route(dest, token_blocks)

    out_x = select(pick, weight, token_blocks, False)
    with jax.named_scope("p2x"):
        rx = [send(r, False, o).reshape(ROWS, width) for r, o in zip(out_x, OFFSETS)]
    out_g = select(pick, weight, cot_blocks, True)
    with jax.named_scope("p2g"):
        rg = [send(r, False, o).reshape(ROWS, width) for r, o in zip(out_g[:3], OFFSETS)]
    pre, act, act_last = expert_pre(rx, up_matrix)
    with jax.named_scope("p2g2"):
        last = send(after(out_g[3], *rx), False, OFFSETS[3]).reshape(ROWS, width)

    grad, rows = expert_back(rg, pre, 0, down_matrix, up_matrix)
    with jax.named_scope("r2"):
        returned = [send(r.reshape(SIDE, SLOTS, width), False, -o) for r, o in zip(rows, OFFSETS)]
    down_acc = down_first(act, rg)
    up_acc = up_first(rx[:3], grad)
    last, act_last, _ = lax.optimization_barrier((last, act_last, (rows, down_acc, up_acc)))

    down_give, down_keep = down_last(pieces, act_last, last, down_acc)
    with jax.named_scope("swap"):
        down_other = swap_cores(down_give)
    last = after(last, down_give)
    grad_last, rows_last = expert_back([last], pre, 3, down_matrix, up_matrix)
    with jax.named_scope("r2"):
        returned.append(send(rows_last[0].reshape(SIDE, SLOTS, width), False, -OFFSETS[3]))
    down_pairs = sum_pairs(down_keep, down_other, 1)
    grad_last = after(grad_last, rows_last[0], *down_pairs, *returned[:3])
    up_give, up_keep = up_last(pieces, rx[3], grad_last, up_acc)
    with jax.named_scope("swap"):
        up_other = swap_cores(up_give)
    up_pairs = sum_pairs(up_keep, up_other, 0)

    with jax.named_scope("zd"):
        down_sum = [send_z(p, o).astype(jnp.float32) for p, o in zip(down_pairs, OFFSETS)]
    with jax.named_scope("zu"):
        up_sum = [send_z(p, o).astype(jnp.float32) for p, o in zip(up_pairs, OFFSETS)]

    parts = combine(after(put, *up_pairs), returned)
    with jax.named_scope("r1"):
        parts = [send(p, True, -o) for p, o in zip(parts, OFFSETS)]
    token_grad = sum(p.astype(jnp.float32) for p in parts).astype(jnp.bfloat16)
    return token_grad, sum(up_sum)[None], sum(down_sum)[None]


def solution(mesh):
    rows = P(("dp", "expert"), None)
    weights = P("expert", None, None)
    return jax.shard_map(
        body,
        mesh=mesh,
        in_specs=(rows, rows, rows, rows, weights, weights),
        out_specs=(rows, P("expert", "dp", None), P("expert", "dp", None)),
        check_vma=False,
    )
```

profile of v0, /device:TPU:0, one launch (start us, length us, event | category | flops | bytes accessed | tf_op | source)
XLA Modules:
  0.0 339.9 jit_solution(9771865598046936696)
XLA Ops:
  9.1 11.1 %collective-permute-done.m1.b1 = bf16[136,4096]{1,0:T(8,128)(2,1)S(1)} collective-permute-done((bf16[136,4096]{1,0:T(8,128)(2,1)S(1)}, bf16[136,4096]{1,0:T(8,128)(2,1)S(1)}, u32[]{:S(2)}, u32[]{:S(2)}) %collective-permute-start) | collective-permute-done | bytes 1114144 | tf_op jit(solution)/shard_map/p1x/ppermute | solution.py:46
  20.5 12.7 %collective-permute-done.2.m3.b3 = bf16[136,4096]{1,0:T(8,128)(2,1)} collective-permute-done((bf16[136,4096]{1,0:T(8,128)(2,1)S(1)}, bf16[136,4096]{1,0:T(8,128)(2,1)}, u32[]{:S(2)}, u32[]{:S(2)}) %collective-permute-start.2) | collective-permute-done | bytes 1114144 | tf_op jit(solution)/shard_map/p1x/ppermute | solution.py:46
  38.9 7.7 %select.22 = (bf16[4,72,4096]{2,1,0:T(8,128)(2,1)}, bf16[4,72,4096]{2,1,0:T(8,128)(2,1)}, bf16[4,72,4096]{2,1,0:T(8,128)(2,1)}, bf16[4,72,4096]{2,1,0:T(8,128)(2,1)}) custom-call(bf16[4,288,128]{2,1,0:T(8,128)(2,1)} %get-tuple-element.47.pick_ref, f32[4,288,128]{2,1,0:T(8,128)} %get-tuple-element.48.weight_ref, bf16[136,4096]{1,0:T(8,128)(2,1)} %copy-done.1, ...), custom_call_target="tpu_custom_call" | custom-call | flops 30000001024 | bytes 1 | tf_op jit(solution)/shard_map/select/pallas_call | solution.py:117
  53.3 32.4 %collective-permute-done.5.b2 = bf16[128,4096]{1,0:T(8,128)(2,1)} collective-permute-done((bf16[128,4096]{1,0:T(8,128)(2,1)}, bf16[128,4096]{1,0:T(8,128)(2,1)}, u32[]{:S(2)}, u32[]{:S(2)}) %collective-permute-start.5) | collective-permute-done | bytes 1048608 | tf_op jit(solution)/shard_map/p1g/ppermute | solution.py:46
  85.7 7.8 %select_scaled.1 = (bf16[4,72,4096]{2,1,0:T(8,128)(2,1)}, bf16[4,72,4096]{2,1,0:T(8,128)(2,1)}, bf16[4,72,4096]{2,1,0:T(8,128)(2,1)}, bf16[4,72,4096]{2,1,0:T(8,128)(2,1)}) custom-call(bf16[4,288,128]{2,1,0:T(8,128)(2,1)} %get-tuple-element.47.pick_ref, f32[4,288,128]{2,1,0:T(8,128)} %get-tuple-element.48.weight_ref, bf16[128,4096]{1,0:T(8,128)(2,1)} %b0, ...), custom_call_target="tpu_custom_call" | custom-call | flops 30000001024 | bytes 1 | tf_op jit(solution)/shard_map/select_scaled/pallas_call | solution.py:117
  97.3 12.3 %collective-permute-done.7 = bf16[4,72,4096]{2,1,0:T(8,128)(2,1)S(1)} collective-permute-done((bf16[4,72,4096]{2,1,0:T(8,128)(2,1)}, bf16[4,72,4096]{2,1,0:T(8,128)(2,1)S(1)}, u32[]{:S(2)}, u32[]{:S(2)}) %collective-permute-start.7) | collective-permute-done | bytes 2359328 | tf_op jit(solution)/shard_map/p2x/ppermute | solution.py:46
  113.1 14.7 %expert_pre.1 = (f32[1152,768]{1,0:T(8,128)}, bf16[768,864]{1,0:T(8,128)(2,1)}, bf16[768,288]{1,0:T(8,128)(2,1)}) custom-call(bf16[288,4096]{1,0:T(8,128)(2,1)} %bitcast.34, bf16[288,4096]{1,0:T(8,128)(2,1)} %bitcast.36, bf16[288,4096]{1,0:T(8,128)(2,1)} %bitcast.38, bf16[288,4096]{1,0:T(8,128)(2,1)} %bitcast.5.refs_3_.x, bf16[4096,768]{1,0:T(8,128)(2,1)} %bitcast.29), custom_call_target="tpu_custom_call" | custom-call | flops 7247757312 | bytes 17498112 | tf_op jit(solution)/shard_map/expert_pre/pallas_call | solution.py:188
  127.8 7.2 %collective-permute-done.10 = bf16[4,72,4096]{2,1,0:T(8,128)(2,1)} collective-permute-done((bf16[4,72,4096]{2,1,0:T(8,128)(2,1)}, bf16[4,72,4096]{2,1,0:T(8,128)(2,1)}, u32[]{:S(2)}, u32[]{:S(2)}) %collective-permute-start.10) | collective-permute-done | bytes 2359328 | tf_op jit(solution)/shard_map/p2g/ppermute | solution.py:46
  135.0 24.5 %collective-permute-done.11 = bf16[4,72,4096]{2,1,0:T(8,128)(2,1)} collective-permute-done((bf16[4,72,4096]{2,1,0:T(8,128)(2,1)}, bf16[4,72,4096]{2,1,0:T(8,128)(2,1)}, u32[]{:S(2)}, u32[]{:S(2)}) %collective-permute-start.11) | collective-permute-done | bytes 2359328 | tf_op jit(solution)/shard_map/p2g/ppermute | solution.py:46
  159.5 11.7 %down_first.1.acc = f32[768,4096]{1,0:T(8,128)} custom-call(bf16[768,864]{1,0:T(8,128)(2,1)} %get-tuple-element.64.act, bf16[288,4096]{1,0:T(8,128)(2,1)} %bitcast.40, bf16[288,4096]{1,0:T(8,128)(2,1)} %bitcast.12.refs_1_.g1, bf16[288,4096]{1,0:T(8,128)(2,1)} %bitcast.13.refs_2_.g2), custom_call_target="tpu_custom_call" | custom-call | flops 5435817984 | bytes 14696448 | tf_op jit(solution)/shard_map/down_first/pallas_call | solution.py:284
  171.2 20.4 %expert_back.2 = (bf16[864,768]{1,0:T(8,128)(2,1)}, bf16[288,4096]{1,0:T(8,128)(2,1)}, bf16[288,4096]{1,0:T(8,128)(2,1)}, bf16[288,4096]{1,0:T(8,128)(2,1)}) custom-call(bf16[288,4096]{1,0:T(8,128)(2,1)} %bitcast.41, bf16[288,4096]{1,0:T(8,128)(2,1)} %bitcast.12.refs_1_.g1, bf16[288,4096]{1,0:T(8,128)(2,1)} %bitcast.13.refs_2_.g2, ...), custom_call_target="tpu_custom_call" | custom-call | flops 10871635968 | bytes 23101440 | tf_op jit(solution)/shard_map/expert_back/pallas_call | solution.py:238
  191.6 12.1 %up_first.1.acc = f32[4096,768]{1,0:T(8,128)} custom-call(bf16[288,4096]{1,0:T(8,128)(2,1)} %bitcast.35, bf16[288,4096]{1,0:T(8,128)(2,1)} %bitcast.37, bf16[288,4096]{1,0:T(8,128)(2,1)} %bitcast.39, bf16[864,768]{1,0:T(8,128)(2,1)} %get-tuple-element.65.grad), custom_call_target="tpu_custom_call" | custom-call | flops 5435817984 | bytes 14696448 | tf_op jit(solution)/shard_map/up_first/pallas_call | solution.py:265
  205.1 10.6 %down_last.1 = (bf16[4,96,4096]{2,1,0:T(8,128)(2,1)}, bf16[4,96,4096]{2,1,0:T(8,128)(2,1)}) custom-call(s32[5]{0:T(128)} %pad_add_fusion.idx, bf16[768,288]{1,0:T(8,128)(2,1)} %get-tuple-element.67.act, bf16[288,4096]{1,0:T(8,128)(2,1)} %bitcast.27, f32[768,4096]{1,0:T(8,128)} %down_first.1.acc), custom_call_target="tpu_custom_call" | custom-call | flops 1000000 | bytes 1 | tf_op jit(solution)/shard_map/down_last/pallas_call | solution.py:346
  220.9 12.3 %expert_back.3 = (bf16[288,768]{1,0:T(8,128)(2,1)}, bf16[288,4096]{1,0:T(8,128)(2,1)}) custom-call(bf16[288,4096]{1,0:T(8,128)(2,1)} %bitcast.28, f32[1152,768]{1,0:T(8,128)} %get-tuple-element.60.refs_3_.refs_1_, bf16[768,4096]{1,0:T(8,128)(2,1)} %bitcast.33, bf16[4096,768]{1,0:T(8,128)(2,1)} %bitcast.31), custom_call_target="tpu_custom_call" | custom-call | flops 1000000 | bytes 1 | tf_op jit(solution)/shard_map/expert_back/pallas_call | solution.py:238
  234.8 5.0 %sum_pairs.2 = (bf16[96,4096]{1,0:T(8,128)(2,1)}, bf16[96,4096]{1,0:T(8,128)(2,1)}, bf16[96,4096]{1,0:T(8,128)(2,1)}, bf16[96,4096]{1,0:T(8,128)(2,1)}) custom-call(bf16[4,96,4096]{2,1,0:T(8,128)(2,1)} %get-tuple-element.72.own, bf16[4,96,4096]{2,1,0:T(8,128)(2,1)} %copy-done.3), custom_call_target="tpu_custom_call" | custom-call | flops 1000000 | bytes 1 | tf_op jit(solution)/shard_map/sum_pairs/pallas_call | solution.py:388
  239.8 7.7 %collective-permute-done.13.r1 = bf16[4,72,4096]{2,1,0:T(8,128)(2,1)S(1)} collective-permute-done((bf16[4,72,4096]{2,1,0:T(8,128)(2,1)}, bf16[4,72,4096]{2,1,0:T(8,128)(2,1)S(1)}, u32[]{:S(2)}, u32[]{:S(2)}) %collective-permute-start.13) | collective-permute-done | bytes 2359328 | tf_op jit(solution)/shard_map/r2/ppermute | solution.py:46
  251.2 10.8 %up_last.1 = (bf16[4,512,768]{2,1,0:T(8,128)(2,1)}, bf16[4,512,768]{2,1,0:T(8,128)(2,1)}) custom-call(s32[5]{0:T(128)} %pad_add_fusion.idx, bf16[288,4096]{1,0:T(8,128)(2,1)} %bitcast.5.refs_3_.x, bf16[288,768]{1,0:T(8,128)(2,1)} %get-tuple-element.77.grad, f32[4096,768]{1,0:T(8,128)} %up_first.1.acc), custom_call_target="tpu_custom_call" | custom-call | flops 1000000 | bytes 1 | tf_op jit(solution)/shard_map/up_last/pallas_call | solution.py:314
  264.1 3.9 %collective-permute-start.25 = (bf16[96,4096]{1,0:T(8,128)(2,1)}, bf16[96,4096]{1,0:T(8,128)(2,1)}, u32[]{:S(2)}, u32[]{:S(2)}) collective-permute-start(bf16[96,4096]{1,0:T(8,128)(2,1)} %get-tuple-element.76), channel_id=1, source_target_pairs={{0,64},{16,80},{32,96},{48,112},{64,0},{80,16},{96,32},{112,48},{1... | collective-permute-start | bytes 2359304 | tf_op jit(solution)/shard_map/zd/ppermute | solution.py:372
  271.7 4.9 %sum_pairs.3 = (bf16[512,768]{1,0:T(8,128)(2,1)}, bf16[512,768]{1,0:T(8,128)(2,1)}, bf16[512,768]{1,0:T(8,128)(2,1)}, bf16[512,768]{1,0:T(8,128)(2,1)}) custom-call(bf16[4,512,768]{2,1,0:T(8,128)(2,1)} %get-tuple-element.78.own, bf16[4,512,768]{2,1,0:T(8,128)(2,1)} %copy-done.2), custom_call_target="tpu_custom_call" | custom-call | flops 1000000 | bytes 1 | tf_op jit(solution)/shard_map/sum_pairs/pallas_call | solution.py:388
  278.4 14.3 %collective-permute-done.16.r3 = bf16[4,72,4096]{2,1,0:T(8,128)(2,1)S(1)} collective-permute-done((bf16[4,72,4096]{2,1,0:T(8,128)(2,1)}, bf16[4,72,4096]{2,1,0:T(8,128)(2,1)S(1)}, u32[]{:S(2)}, u32[]{:S(2)}) %collective-permute-start.16) | collective-permute-done | bytes 2359328 | tf_op jit(solution)/shard_map/r2/ppermute | solution.py:46
  292.7 4.0 %collective-permute-start.21 = (bf16[512,768]{1,0:T(8,128)(2,1)}, bf16[512,768]{1,0:T(8,128)(2,1)S(1)}, u32[]{:S(2)}, u32[]{:S(2)}) collective-permute-start(bf16[512,768]{1,0:T(8,128)(2,1)} %get-tuple-element.82), channel_id=1, source_target_pairs={{0,96},{16,112},{32,0},{48,16},{64,32},{80,48},{96,64},{112,80},{1... | collective-permute-start | bytes 2359304 | tf_op jit(solution)/shard_map/zu/ppermute | solution.py:372
  296.7 8.2 %combine.1 = (bf16[128,4096]{1,0:T(8,128)(2,1)}, bf16[128,4096]{1,0:T(8,128)(2,1)}, bf16[128,4096]{1,0:T(8,128)(2,1)}, bf16[128,4096]{1,0:T(8,128)(2,1)}) custom-call(bf16[4,4,128,72]{3,2,1,0:T(8,128)(2,1)} %get-tuple-element.84.put_ref, bf16[4,72,4096]{2,1,0:T(8,128)(2,1)} %bitcast.42, bf16[4,72,4096]{2,1,0:T(8,128)(2,1)} %copy-done.6, ...), custom_call_target="tpu_custom_call" | custom-call | flops 1000000 | bytes 1 | tf_op jit(solution)/shard_map/combine/pallas_call | solution.py:145
  309.3 11.1 %collective-permute-done.22 = bf16[512,768]{1,0:T(8,128)(2,1)S(1)} collective-permute-done((bf16[512,768]{1,0:T(8,128)(2,1)}, bf16[512,768]{1,0:T(8,128)(2,1)S(1)}, u32[]{:S(2)}, u32[]{:S(2)}) %collective-permute-start.22) | collective-permute-done | bytes 786464 | tf_op jit(solution)/shard_map/zu/ppermute | solution.py:372
  324.9 11.8 %collective-permute-done.21 = bf16[512,768]{1,0:T(8,128)(2,1)S(1)} collective-permute-done((bf16[512,768]{1,0:T(8,128)(2,1)}, bf16[512,768]{1,0:T(8,128)(2,1)S(1)}, u32[]{:S(2)}, u32[]{:S(2)}) %collective-permute-start.21) | collective-permute-done | bytes 786464 | tf_op jit(solution)/shard_map/zu/ppermute | solution.py:372
  (80 shorter events, 59.9 us)
Async XLA Ops:
  3.4 16.8 %collective-permute-start = (bf16[136,4096]{1,0:T(8,128)(2,1)S(1)}, bf16[136,4096]{1,0:T(8,128)(2,1)S(1)}, u32[]{:S(2)}, u32[]{:S(2)}) collective-permute-start(bf16[136,4096]{1,0:T(8,128)(2,1)S(1)} %pad_maximum_fusion.m0.b0), channel_id=1, source_target_pairs={{0,1},{1,2},{2,3},{3,0},{4,5},{5,6},{6,7},{7,4},{8,9},{9,10},{10,1... | collective-permute-start | bytes 3342344 | tf_op jit(solution)/shard_map/p1x/ppermute | solution.py:46
  6.7 26.6 %collective-permute-start.2 = (bf16[136,4096]{1,0:T(8,128)(2,1)S(1)}, bf16[136,4096]{1,0:T(8,128)(2,1)}, u32[]{:S(2)}, u32[]{:S(2)}) collective-permute-start(bf16[136,4096]{1,0:T(8,128)(2,1)S(1)} %pad_maximum_fusion.m0.b0), channel_id=1, source_target_pairs={{0,2},{1,3},{2,0},{3,1},{4,6},{5,7},{6,4},{7,5},{8,10},{9,11},{10,... | collective-permute-start | bytes 3342344 | tf_op jit(solution)/shard_map/p1x/ppermute | solution.py:46
  33.2 17.4 %collective-permute-start.4 = (bf16[128,4096]{1,0:T(8,128)(2,1)}, bf16[128,4096]{1,0:T(8,128)(2,1)}, u32[]{:S(2)}, u32[]{:S(2)}) collective-permute-start(bf16[128,4096]{1,0:T(8,128)(2,1)} %b0), channel_id=1, source_target_pairs={{0,1},{1,2},{2,3},{3,0},{4,5},{5,6},{6,7},{7,4},{8,9},{9,10},{10,1... | collective-permute-start | bytes 3145736 | tf_op jit(solution)/shard_map/p1g/ppermute | solution.py:46
  34.7 51.0 %collective-permute-start.5 = (bf16[128,4096]{1,0:T(8,128)(2,1)}, bf16[128,4096]{1,0:T(8,128)(2,1)}, u32[]{:S(2)}, u32[]{:S(2)}) collective-permute-start(bf16[128,4096]{1,0:T(8,128)(2,1)} %b0), channel_id=1, source_target_pairs={{0,3},{1,0},{2,1},{3,2},{4,7},{5,4},{6,5},{7,6},{8,11},{9,8},{10,9... | collective-permute-start | bytes 3145736 | tf_op jit(solution)/shard_map/p1g/ppermute | solution.py:46
  36.5 49.2 %collective-permute-start.6 = (bf16[128,4096]{1,0:T(8,128)(2,1)}, bf16[128,4096]{1,0:T(8,128)(2,1)}, u32[]{:S(2)}, u32[]{:S(2)}) collective-permute-start(bf16[128,4096]{1,0:T(8,128)(2,1)} %b0), channel_id=1, source_target_pairs={{0,2},{1,3},{2,0},{3,1},{4,6},{5,7},{6,4},{7,5},{8,10},{9,11},{10,... | collective-permute-start | bytes 3145736 | tf_op jit(solution)/shard_map/p1g/ppermute | solution.py:46
  46.7 50.6 %collective-permute-start.3 = (bf16[4,72,4096]{2,1,0:T(8,128)(2,1)}, bf16[4,72,4096]{2,1,0:T(8,128)(2,1)}, u32[]{:S(2)}, u32[]{:S(2)}) collective-permute-start(bf16[4,72,4096]{2,1,0:T(8,128)(2,1)} %get-tuple-element.49), channel_id=1, source_target_pairs={{0,8},{1,9},{2,10},{3,11},{4,12},{5,13},{6,14},{7,15},{8,0},{9,1},... | collective-permute-start | bytes 7077896 | tf_op jit(solution)/shard_map/p2x/ppermute | solution.py:46
  50.0 59.6 %collective-permute-start.7 = (bf16[4,72,4096]{2,1,0:T(8,128)(2,1)}, bf16[4,72,4096]{2,1,0:T(8,128)(2,1)S(1)}, u32[]{:S(2)}, u32[]{:S(2)}) collective-permute-start(bf16[4,72,4096]{2,1,0:T(8,128)(2,1)} %get-tuple-element.53), channel_id=1, source_target_pairs={{0,4},{1,5},{2,6},{3,7},{4,8},{5,9},{6,10},{7,11},{8,12},{9,13},{1... | collective-permute-start | bytes 7077896 | tf_op jit(solution)/shard_map/p2x/ppermute | solution.py:46
  50.6 59.0 %collective-permute-start.8 = (bf16[4,72,4096]{2,1,0:T(8,128)(2,1)}, bf16[4,72,4096]{2,1,0:T(8,128)(2,1)S(1)}, u32[]{:S(2)}, u32[]{:S(2)}) collective-permute-start(bf16[4,72,4096]{2,1,0:T(8,128)(2,1)} %get-tuple-element.54), channel_id=1, source_target_pairs={{0,12},{1,13},{2,14},{3,15},{4,0},{5,1},{6,2},{7,3},{8,4},{9,5},{1... | collective-permute-start | bytes 7077896 | tf_op jit(solution)/shard_map/p2x/ppermute | solution.py:46
  93.4 41.6 %collective-permute-start.10 = (bf16[4,72,4096]{2,1,0:T(8,128)(2,1)}, bf16[4,72,4096]{2,1,0:T(8,128)(2,1)}, u32[]{:S(2)}, u32[]{:S(2)}) collective-permute-start(bf16[4,72,4096]{2,1,0:T(8,128)(2,1)} %get-tuple-element.58), channel_id=1, source_target_pairs={{0,4},{1,5},{2,6},{3,7},{4,8},{5,9},{6,10},{7,11},{8,12},{9,13},{1... | collective-permute-start | bytes 7077896 | tf_op jit(solution)/shard_map/p2g/ppermute | solution.py:46
  95.0 64.5 %collective-permute-start.11 = (bf16[4,72,4096]{2,1,0:T(8,128)(2,1)}, bf16[4,72,4096]{2,1,0:T(8,128)(2,1)}, u32[]{:S(2)}, u32[]{:S(2)}) collective-permute-start(bf16[4,72,4096]{2,1,0:T(8,128)(2,1)} %get-tuple-element.59), channel_id=1, source_target_pairs={{0,12},{1,13},{2,14},{3,15},{4,0},{5,1},{6,2},{7,3},{8,4},{9,5},{1... | collective-permute-start | bytes 7077896 | tf_op jit(solution)/shard_map/p2g/ppermute | solution.py:46
  111.1 92.6 %collective-permute-start.9 = (bf16[4,72,4096]{2,1,0:T(8,128)(2,1)}, bf16[4,72,4096]{2,1,0:T(8,128)(2,1)S(1)}, u32[]{:S(2)}, u32[]{:S(2)}) collective-permute-start(bf16[4,72,4096]{2,1,0:T(8,128)(2,1)} %get-tuple-element.55), channel_id=1, source_target_pairs={{0,8},{1,9},{2,10},{3,11},{4,12},{5,13},{6,14},{7,15},{8,0},{9,1},... | collective-permute-start | bytes 7077896 | tf_op jit(solution)/shard_map/p2g2/ppermute | solution.py:46
  215.7 17.5 %collective-permute-start.12 = (bf16[4,96,4096]{2,1,0:T(8,128)(2,1)}, bf16[4,96,4096]{2,1,0:T(8,128)(2,1)S(1)}, u32[]{:S(2)}, u32[]{:S(2)}) collective-permute-start(bf16[4,96,4096]{2,1,0:T(8,128)(2,1)} %get-tuple-element.68), channel_id=1, source_target_pairs={{0,16},{16,0},{32,48},{48,32},{64,80},{80,64},{96,112},{112,96},{1... | collective-permute-start | bytes 9437192 | tf_op jit(solution)/shard_map/swap/ppermute | solution.py:367
  217.8 29.7 %collective-permute-start.13 = (bf16[4,72,4096]{2,1,0:T(8,128)(2,1)}, bf16[4,72,4096]{2,1,0:T(8,128)(2,1)S(1)}, u32[]{:S(2)}, u32[]{:S(2)}) collective-permute-start(bf16[4,72,4096]{2,1,0:T(8,128)(2,1)} %bitcast.45), channel_id=1, source_target_pairs={{0,12},{1,13},{2,14},{3,15},{4,0},{5,1},{6,2},{7,3},{8,4},{9,5},{1... | collective-permute-start | bytes 7077896 | tf_op jit(solution)/shard_map/r2/ppermute | solution.py:46
  220.9 30.4 %collective-permute-start.14 = (bf16[4,72,4096]{2,1,0:T(8,128)(2,1)}, bf16[4,72,4096]{2,1,0:T(8,128)(2,1)}, u32[]{:S(2)}, u32[]{:S(2)}) collective-permute-start(bf16[4,72,4096]{2,1,0:T(8,128)(2,1)} %bitcast.44), channel_id=1, source_target_pairs={{0,4},{1,5},{2,6},{3,7},{4,8},{5,9},{6,10},{7,11},{8,12},{9,13},{1... | collective-permute-start | bytes 7077896 | tf_op jit(solution)/shard_map/r2/ppermute | solution.py:46
  262.0 30.6 %collective-permute-start.16 = (bf16[4,72,4096]{2,1,0:T(8,128)(2,1)}, bf16[4,72,4096]{2,1,0:T(8,128)(2,1)S(1)}, u32[]{:S(2)}, u32[]{:S(2)}) collective-permute-start(bf16[4,72,4096]{2,1,0:T(8,128)(2,1)} %bitcast.43), channel_id=1, source_target_pairs={{0,8},{1,9},{2,10},{3,11},{4,12},{5,13},{6,14},{7,15},{8,0},{9,1},... | collective-permute-start | bytes 7077896 | tf_op jit(solution)/shard_map/r2/ppermute | solution.py:46
  264.1 40.8 %collective-permute-start.25 = (bf16[96,4096]{1,0:T(8,128)(2,1)}, bf16[96,4096]{1,0:T(8,128)(2,1)}, u32[]{:S(2)}, u32[]{:S(2)}) collective-permute-start(bf16[96,4096]{1,0:T(8,128)(2,1)} %get-tuple-element.76), channel_id=1, source_target_pairs={{0,64},{16,80},{32,96},{48,112},{64,0},{80,16},{96,32},{112,48},{1... | collective-permute-start | bytes 2359304 | tf_op jit(solution)/shard_map/zd/ppermute | solution.py:372
  268.0 37.0 %collective-permute-start.24 = (bf16[96,4096]{1,0:T(8,128)(2,1)}, bf16[96,4096]{1,0:T(8,128)(2,1)}, u32[]{:S(2)}, u32[]{:S(2)}) collective-permute-start(bf16[96,4096]{1,0:T(8,128)(2,1)} %get-tuple-element.75), channel_id=1, source_target_pairs={{0,96},{16,112},{32,0},{48,16},{64,32},{80,48},{96,64},{112,80},{1... | collective-permute-start | bytes 2359304 | tf_op jit(solution)/shard_map/zd/ppermute | solution.py:372
  268.7 37.7 %collective-permute-start.23 = (bf16[96,4096]{1,0:T(8,128)(2,1)}, bf16[96,4096]{1,0:T(8,128)(2,1)}, u32[]{:S(2)}, u32[]{:S(2)}) collective-permute-start(bf16[96,4096]{1,0:T(8,128)(2,1)} %get-tuple-element.74), channel_id=1, source_target_pairs={{0,32},{16,48},{32,64},{48,80},{64,96},{80,112},{96,0},{112,16},{1... | collective-permute-start | bytes 2359304 | tf_op jit(solution)/shard_map/zd/ppermute | solution.py:372
  276.6 43.8 %collective-permute-start.22 = (bf16[512,768]{1,0:T(8,128)(2,1)}, bf16[512,768]{1,0:T(8,128)(2,1)S(1)}, u32[]{:S(2)}, u32[]{:S(2)}) collective-permute-start(bf16[512,768]{1,0:T(8,128)(2,1)} %get-tuple-element.83), channel_id=1, source_target_pairs={{0,64},{16,80},{32,96},{48,112},{64,0},{80,16},{96,32},{112,48},{1... | collective-permute-start | bytes 2359304 | tf_op jit(solution)/shard_map/zu/ppermute | solution.py:372
  292.7 44.0 %collective-permute-start.21 = (bf16[512,768]{1,0:T(8,128)(2,1)}, bf16[512,768]{1,0:T(8,128)(2,1)S(1)}, u32[]{:S(2)}, u32[]{:S(2)}) collective-permute-start(bf16[512,768]{1,0:T(8,128)(2,1)} %get-tuple-element.82), channel_id=1, source_target_pairs={{0,96},{16,112},{32,0},{48,16},{64,32},{80,48},{96,64},{112,80},{1... | collective-permute-start | bytes 2359304 | tf_op jit(solution)/shard_map/zu/ppermute | solution.py:372
  304.9 31.7 %collective-permute-start.20 = (bf16[512,768]{1,0:T(8,128)(2,1)S(1)}, bf16[512,768]{1,0:T(8,128)(2,1)S(1)}, u32[]{:S(2)}, u32[]{:S(2)}) collective-permute-start(bf16[512,768]{1,0:T(8,128)(2,1)S(1)} %copy-done.14), channel_id=1, source_target_pairs={{0,32},{16,48},{32,64},{48,80},{64,96},{80,112},{96,0},{112,16},{1... | collective-permute-start | bytes 2359304 | tf_op jit(solution)/shard_map/zu/ppermute | solution.py:372
  305.0 33.2 %collective-permute-start.19 = (bf16[128,4096]{1,0:T(8,128)(2,1)}, bf16[128,4096]{1,0:T(8,128)(2,1)S(1)}, u32[]{:S(2)}, u32[]{:S(2)}) collective-permute-start(bf16[128,4096]{1,0:T(8,128)(2,1)} %get-tuple-element.88), channel_id=1, source_target_pairs={{0,2},{1,3},{2,0},{3,1},{4,6},{5,7},{6,4},{7,5},{8,10},{9,11},{10,... | collective-permute-start | bytes 3145736 | tf_op jit(solution)/shard_map/r1/ppermute | solution.py:46
  306.4 31.8 %collective-permute-start.18 = (bf16[128,4096]{1,0:T(8,128)(2,1)}, bf16[128,4096]{1,0:T(8,128)(2,1)S(1)}, u32[]{:S(2)}, u32[]{:S(2)}) collective-permute-start(bf16[128,4096]{1,0:T(8,128)(2,1)} %get-tuple-element.87), channel_id=1, source_target_pairs={{0,1},{1,2},{2,3},{3,0},{4,5},{5,6},{6,7},{7,4},{8,9},{9,10},{10,1... | collective-permute-start | bytes 3145736 | tf_op jit(solution)/shard_map/r1/ppermute | solution.py:46
  320.4 17.8 %collective-permute-start.17 = (bf16[128,4096]{1,0:T(8,128)(2,1)}, bf16[128,4096]{1,0:T(8,128)(2,1)S(1)}, u32[]{:S(2)}, u32[]{:S(2)}) collective-permute-start(bf16[128,4096]{1,0:T(8,128)(2,1)} %get-tuple-element.86), channel_id=1, source_target_pairs={{0,3},{1,0},{2,1},{3,2},{4,7},{5,4},{6,5},{7,6},{8,11},{9,8},{10,9... | collective-permute-start | bytes 3145736 | tf_op jit(solution)/shard_map/r1/ppermute | solution.py:46
  (17 other events, 225.5 us)
where the time goes:
time: 341 us; the launch traced here: 340 us
  waiting for transfers between devices  149 us (44%)
  Pallas kernels  128 us (38%)
  starting transfers between devices  45.2 us (13%)
  other arithmetic  10.1 us (3%)
  local copies, waits for them, and re-layouts  6.22 us (2%)
    ppermute x18, waiting for transfers between devices, send(): lax.ppermute(value, BOTH, ring(first, shift))  126 us
    pallas_call x2, Pallas kernels, expert_back(): pl.pallas_call(functools.partial(back_kernel, n), out_shape=(jax.ShapeDty...  32.7 us
    ppermute x18, starting transfers between devices, send(): lax.ppermute(value, BOTH, ring(first, shift))  31.3 us
    ppermute x6, waiting for transfers between devices, send_z(): return value if shift == 0 else lax.ppermute(value, 'dp', pairs)  22.8 us
    pallas_call x2, Pallas kernels, select(): pl.pallas_call(functools.partial(select_kernel, scaled), out_shape=(jax.S...  15.5 us
    pallas_call x1, Pallas kernels, expert_pre(): pl.pallas_call(pre_kernel, out_shape=(jax.ShapeDtypeStruct((WIDE + ROWS,...  14.7 us
    pallas_call x1, Pallas kernels, up_first(): pl.pallas_call(up_first_kernel, out_shape=jax.ShapeDtypeStruct((width, hi...  12.1 us
    pallas_call x1, Pallas kernels, down_first(): pl.pallas_call(down_first_kernel, out_shape=jax.ShapeDtypeStruct((hidden,...  11.7 us
  transfers between devices with their start and end apart: 26, of which 12 were waited for; matrix products, arithmetic and copies ran while one was open for 2% of the time, Pallas kernels for 32%

commit v1 on v0

--- a/solution.py
+++ b/solution.py
@@ -26,6 +26,7 @@
 
 
 HEAVY = pl.CostEstimate(flops=30_000_000_000, bytes_accessed=1, transcendentals=0)
+LONGEST = pl.CostEstimate(flops=300_000_000_000, bytes_accessed=1, transcendentals=0)
 LIGHT = pl.CostEstimate(flops=1_000_000, bytes_accessed=1, transcendentals=0)
 PARAMS = pltpu.CompilerParams(vmem_limit_bytes=VMEM_LIMIT)
 
@@ -164,7 +165,7 @@
 
 
 def pre_kernel(*refs):
-    xs, up, pre, wide, last = refs[:SIDE], refs[SIDE], *refs[SIDE + 1 :]
+    xs, up, pre, act = refs[:SIDE], refs[SIDE], *refs[SIDE + 1 :]
     step = pl.program_id(0)
     part = dot(stacked(xs), up[...])
 
@@ -178,9 +179,8 @@
 
     @pl.when(step == pl.num_programs(0) - 1)
     def _():
-        for rows, out in ((slice(0, WIDE), wide), (slice(WIDE, WIDE + ROWS), last)):
-            value = pre[rows, :]
-            out[...] = (value * jax.nn.sigmoid(value)).T.astype(jnp.bfloat16)
+        value = pre[...]
+        act[...] = (value * jax.nn.sigmoid(value)).T.astype(jnp.bfloat16)
 
 
 def expert_pre(xs, up):
@@ -189,16 +189,14 @@
         pre_kernel,
         out_shape=(
             jax.ShapeDtypeStruct((WIDE + ROWS, hidden), jnp.float32),
-            jax.ShapeDtypeStruct((hidden, WIDE), jnp.bfloat16),
-            jax.ShapeDtypeStruct((hidden, ROWS), jnp.bfloat16),
+            jax.ShapeDtypeStruct((hidden, WIDE + ROWS), jnp.bfloat16),
         ),
         grid=(width // TILE,),
         in_specs=[pl.BlockSpec((ROWS, TILE), lambda c: (0, c))] * SIDE
         + [pl.BlockSpec((TILE, hidden), lambda c: (c, 0))],
         out_specs=(
             pl.BlockSpec((WIDE + ROWS, hidden), lambda c: (0, 0)),
-            pl.BlockSpec((hidden, WIDE), lambda c: (0, 0)),
-            pl.BlockSpec((hidden, ROWS), lambda c: (0, 0)),
+            pl.BlockSpec((hidden, WIDE + ROWS), lambda c: (0, 0)),
         ),
         compiler_params=PARAMS,
         cost_estimate=cost(WIDE + ROWS, width, hidden),
@@ -256,145 +254,64 @@
     return out[0], list(out[1:])
 
 
-def up_first_kernel(x0, x1, x2, grad, out):
-    out[...] = dot(stacked((x0, x1, x2)), grad[...], ROWS_FIRST)
-
-
-def up_first(xs, grad):
-    width, hidden = xs[0].shape[1], grad.shape[1]
-    return pl.pallas_call(
-        up_first_kernel,
-        out_shape=jax.ShapeDtypeStruct((width, hidden), jnp.float32),
+def up_kernel(x0, x1, x2, x3, grad, grad_last, out):
+    total = dot(stacked((x0, x1, x2, x3)), stacked((grad, grad_last)), ROWS_FIRST)
+    out[...] = total.astype(jnp.bfloat16)
+
+
+def up_partial(xs, grads):
+    width, hidden = xs[0].shape[1], grads[0].shape[1]
+    return pl.pallas_call(
+        up_kernel,
+        out_shape=jax.ShapeDtypeStruct((width, hidden), jnp.bfloat16),
         grid=(width // TILE,),
-        in_specs=[pl.BlockSpec((ROWS, TILE), lambda c: (0, c))] * 3
-        + [pl.BlockSpec((WIDE, hidden), lambda c: (0, 0))],
+        in_specs=[pl.BlockSpec((ROWS, TILE), lambda c: (0, c))] * SIDE
+        + [pl.BlockSpec(g.shape, lambda c: (0, 0)) for g in grads],
         out_specs=pl.BlockSpec((TILE, hidden), lambda c: (c, 0)),
         compiler_params=PARAMS,
-        cost_estimate=cost(width, WIDE, hidden),
-        name="up_first",
-    )(*xs, grad)
-
-
-def down_first_kernel(act, g0, g1, g2, out):
-    out[...] = dot(act[...], stacked((g0, g1, g2)))
-
-
-def down_first(act, gs):
-    width, hidden = gs[0].shape[1], act.shape[0]
-    return pl.pallas_call(
-        down_first_kernel,
-        out_shape=jax.ShapeDtypeStruct((hidden, width), jnp.float32),
+        cost_estimate=LIGHT,
+        name="up_partial",
+    )(*xs, *grads)
+
+
+def down_kernel(act, g0, g1, g2, g3, out):
+    out[...] = dot(act[...], stacked((g0, g1, g2, g3))).astype(jnp.bfloat16)
+
+
+def down_partial(act, gs):
+    hidden, rows = act.shape
+    width = gs[0].shape[1]
+    return pl.pallas_call(
+        down_kernel,
+        out_shape=jax.ShapeDtypeStruct((hidden, width), jnp.bfloat16),
         grid=(width // TILE,),
-        in_specs=[pl.BlockSpec((hidden, WIDE), lambda c: (0, 0))]
-        + [pl.BlockSpec((ROWS, TILE), lambda c: (0, c))] * 3,
+        in_specs=[pl.BlockSpec((hidden, rows), lambda c: (0, 0))]
+        + [pl.BlockSpec((ROWS, TILE), lambda c: (0, c))] * SIDE,
         out_specs=pl.BlockSpec((hidden, TILE), lambda c: (0, c)),
         compiler_params=PARAMS,
-        cost_estimate=cost(hidden, WIDE, width),
-        name="down_first",
+        cost_estimate=LIGHT,
+        name="down_partial",
     )(act, *gs)
 
 
-def up_last_kernel(idx, x, grad, acc, give, keep):
-    total = (acc[...] + dot(x[...], grad[...], ROWS_FIRST)).astype(jnp.bfloat16)
-    half = total.shape[0] // 2
-
-    @pl.when(idx[SIDE] == 0)
-    def _():
-        keep[0], give[0] = total[:half], total[half:]
-
-    @pl.when(idx[SIDE] == 1)
-    def _():
-        give[0], keep[0] = total[:half], total[half:]
-
-
-def up_last(idx, x, grad, acc):
-    width, hidden = acc.shape
-    tile = width // SIDE
-    slab = pl.BlockSpec((1, tile // 2, hidden), lambda s, idx: (s, 0, 0))
-    return pl.pallas_call(
-        up_last_kernel,
-        out_shape=(jax.ShapeDtypeStruct((SIDE, tile // 2, hidden), jnp.bfloat16),) * 2,
-        grid_spec=pltpu.PrefetchScalarGridSpec(
-            num_scalar_prefetch=1,
-            grid=(SIDE,),
-            in_specs=[
-                pl.BlockSpec((ROWS, tile), lambda s, idx: (0, idx[s])),
-                pl.BlockSpec((ROWS, hidden), lambda s, idx: (0, 0)),
-                pl.BlockSpec((tile, hidden), lambda s, idx: (idx[s], 0)),
-            ],
-            out_specs=(slab, slab),
-        ),
-        compiler_params=PARAMS,
-        cost_estimate=LIGHT,
-        name="up_last",
-    )(idx, x, grad, acc)
-
-
-def down_last_kernel(idx, act, g, acc, give, keep, total):
-    value = acc[...] + dot(act[...], g[...])
-    total[...] = value.reshape(total.shape)
-    core = idx[SIDE]
-    for s in range(SIDE):
-        keep[s] = total[2 * idx[s] + core].astype(jnp.bfloat16)
-        give[s] = total[2 * idx[s] + 1 - core].astype(jnp.bfloat16)
-
-
-def down_last(idx, act, g, acc):
-    hidden, width = acc.shape
-    part = hidden // 8
-    slab = pl.BlockSpec((SIDE, part, TILE), lambda c, idx: (0, 0, c))
-    return pl.pallas_call(
-        down_last_kernel,
-        out_shape=(jax.ShapeDtypeStruct((SIDE, part, width), jnp.bfloat16),) * 2,
-        grid_spec=pltpu.PrefetchScalarGridSpec(
-            num_scalar_prefetch=1,
-            grid=(width // TILE,),
-            in_specs=[
-                pl.BlockSpec((hidden, ROWS), lambda c, idx: (0, 0)),
-                pl.BlockSpec((ROWS, TILE), lambda c, idx: (0, c)),
-                pl.BlockSpec((hidden, TILE), lambda c, idx: (0, c)),
-            ],
-            out_specs=(slab, slab),
-            scratch_shapes=[pltpu.VMEM((8, part, TILE), jnp.float32)],
-        ),
-        compiler_params=PARAMS,
-        cost_estimate=LIGHT,
-        name="down_last",
-    )(idx, act, g, acc)
-
-
-def swap_cores(value):
-    return lax.ppermute(value, "dp", [(d, d ^ 1) for d in range(8)])
-
-
-def send_z(value, shift):
-    pairs = [(z * 2 + c, (z + shift) % SIDE * 2 + c) for z in range(SIDE) for c in range(2)]
-    return value if shift == 0 else lax.ppermute(value, "dp", pairs)
-
-
-def pairs_kernel(own, other, *outs):
-    total = own[...].astype(jnp.float32) + other[...].astype(jnp.float32)
-    for i, out in enumerate(outs):
-        out[...] = total[i].astype(jnp.bfloat16)
-
-
-def sum_pairs(own, other, dim):
-    _, rows, columns = own.shape
-    tile = (rows // SIDE, columns) if dim == 0 else (rows, columns // SIDE)
-
-    def index(c):
-        return (c, 0) if dim == 0 else (0, c)
-
-    return pl.pallas_call(
-        pairs_kernel,
-        out_shape=(jax.ShapeDtypeStruct((rows, columns), jnp.bfloat16),) * SIDE,
+def parts_kernel(p0, p1, p2, p3, out):
+    total = sum(p[...].astype(jnp.float32) for p in (p0, p1, p2, p3))
+    out[...] = total.astype(jnp.bfloat16)
+
+
+def sum_parts(parts):
+    rows, width = parts[0].shape
+    spec = pl.BlockSpec((rows // SIDE, width), lambda c: (c, 0))
+    return pl.pallas_call(
+        parts_kernel,
+        out_shape=jax.ShapeDtypeStruct((rows, width), jnp.bfloat16),
         grid=(SIDE,),
-        in_specs=[pl.BlockSpec((SIDE, *tile), lambda c: (0, *index(c)))] * 2,
-        out_specs=(pl.BlockSpec(tile, index),) * SIDE,
-        compiler_params=PARAMS,
-        cost_estimate=LIGHT,
-        name="sum_pairs",
-    )(own, other)
+        in_specs=[spec] * SIDE,
+        out_specs=spec,
+        compiler_params=PARAMS,
+        cost_estimate=LONGEST,
+        name="sum_parts",
+    )(*parts)
 
 
 def after(value, *earlier):
@@ -406,12 +323,11 @@
     up_matrix = up_weight[0]
     down_matrix = down_weight[0]
     dp = lax.axis_index("dp")
-    core, z = dp & 1, dp >> 1
+    core = dp & 1
     place = lax.axis_index("expert")
     y, x = place >> 2, place & 3
     shifts = jnp.array(OFFSETS, jnp.int32)
     dest = jnp.where(core == 1, y * SIDE + ((x + shifts) & 3), ((y + shifts) & 3) * SIDE + x)
-    pieces = jnp.concatenate([(z + shifts) & 3, core[None]])
     high = lax.reduce_precision(route_weight, 8, 7)
     middle = lax.reduce_precision(route_weight - high, 8, 7)
     low = route_weight - high - middle
@@ -433,41 +349,31 @@
     out_g = select(pick, weight, cot_blocks, True)
     with jax.named_scope("p2g"):
         rg = [send(r, False, o).reshape(ROWS, width) for r, o in zip(out_g[:3], OFFSETS)]
-    pre, act, act_last = expert_pre(rx, up_matrix)
+    pre, act = expert_pre(rx, up_matrix)
     with jax.named_scope("p2g2"):
-        last = send(after(out_g[3], *rx), False, OFFSETS[3]).reshape(ROWS, width)
+        last = send(after(out_g[3], *rx, *rg), False, OFFSETS[3]).reshape(ROWS, width)
 
     grad, rows = expert_back(rg, pre, 0, down_matrix, up_matrix)
     with jax.named_scope("r2"):
         returned = [send(r.reshape(SIDE, SLOTS, width), False, -o) for r, o in zip(rows, OFFSETS)]
-    down_acc = down_first(act, rg)
-    up_acc = up_first(rx[:3], grad)
-    last, act_last, _ = lax.optimization_barrier((last, act_last, (rows, down_acc, up_acc)))
-
-    down_give, down_keep = down_last(pieces, act_last, last, down_acc)
-    with jax.named_scope("swap"):
-        down_other = swap_cores(down_give)
-    last = after(last, down_give)
+
+    last = after(last, *rows)
+    down_part = down_partial(act, [*rg, last])
+    down_grad = lax.psum_scatter(down_part, "dp", scatter_dimension=0, tiled=True)
+    last = after(last, down_part)
     grad_last, rows_last = expert_back([last], pre, 3, down_matrix, up_matrix)
     with jax.named_scope("r2"):
         returned.append(send(rows_last[0].reshape(SIDE, SLOTS, width), False, -OFFSETS[3]))
-    down_pairs = sum_pairs(down_keep, down_other, 1)
-    grad_last = after(grad_last, rows_last[0], *down_pairs, *returned[:3])
-    up_give, up_keep = up_last(pieces, rx[3], grad_last, up_acc)
-    with jax.named_scope("swap"):
-        up_other = swap_cores(up_give)
-    up_pairs = sum_pairs(up_keep, up_other, 0)
-
-    with jax.named_scope("zd"):
-        down_sum = [send_z(p, o).astype(jnp.float32) for p, o in zip(down_pairs, OFFSETS)]
-    with jax.named_scope("zu"):
-        up_sum = [send_z(p, o).astype(jnp.float32) for p, o in zip(up_pairs, OFFSETS)]
-
-    parts = combine(after(put, *up_pairs), returned)
+    grad_last = after(grad_last, rows_last[0], *returned[:3])
+    up_part = up_partial(rx, [grad, grad_last])
+    up_grad = lax.psum_scatter(up_part, "dp", scatter_dimension=0, tiled=True)
+
+    parts = combine(after(put, up_part), returned)
     with jax.named_scope("r1"):
         parts = [send(p, True, -o) for p, o in zip(parts, OFFSETS)]
-    token_grad = sum(p.astype(jnp.float32) for p in parts).astype(jnp.bfloat16)
-    return token_grad, sum(up_sum)[None], sum(down_sum)[None]
+    token_grad = sum_parts(parts)
+    token_grad, up_grad, down_grad = lax.optimization_barrier((token_grad, up_grad, down_grad))
+    return token_grad, up_grad.astype(jnp.float32)[None], down_grad.astype(jnp.float32)[None]
 
 
 def solution(mesh):

time: 341 us -> 332 us (0.974)
  Pallas kernels: 128 us -> 103 us
  waiting for transfers between devices: 149 us -> 169 us
  between operations: 0.75 us -> 14.1 us
  starting transfers between devices: 45.2 us -> 31.9 us
    ppermute x18, waiting for transfers between devices: 126 us -> 157 us  [send(): lax.ppermute(value, BOTH, ring(first, shift))]
    pallas_call x6 -> x3, Pallas kernels: 55.2 us -> 30.2 us  [the longest x1 13.6 us: up_partial(): pl.pallas_call(up_kernel, out_shape=jax.ShapeDtypeStruct((width, hidden),...]
    ppermute x8 -> x0, waiting for transfers between devices: 22.9 us -> none  [the longest x6 22.8 us: send_z(): return value if shift == 0 else lax.ppermute(value, 'dp', pairs)]
    ppermute x8 -> x0, starting transfers between devices: 13.9 us -> none  [the longest x6 11.7 us: send_z(): return value if shift == 0 else lax.ppermute(value, 'dp', pairs)]
    reduce_scatter x0 -> x2, waiting for transfers between devices: none -> 12.7 us  [the longest x1 12.7 us: body(): up_grad = lax.psum_scatter(up_part, 'dp', scatter_dimension=0, tiled=True)]
  transfers between devices with their start and end apart: 26 -> 20, of which waited for: 12 -> 11; matrix products, arithmetic and copies ran while one was open for 2% -> 0% of each run, Pallas kernels for 32% -> 28%
where the time goes in v1:
time: 332 us; the launch traced here: 331 us
  waiting for transfers between devices  169 us (51%)
  Pallas kernels  103 us (31%)
  starting transfers between devices  31.9 us (10%)
  between operations  14.1 us (4%)
  other arithmetic  7.59 us (2%)
  local copies, waits for them, and re-layouts  4.17 us (1%)
    ppermute x18, waiting for transfers between devices, send(): lax.ppermute(value, BOTH, ring(first, shift))  157 us
    pallas_call x2, Pallas kernels, expert_back(): pl.pallas_call(functools.partial(back_kernel, n), out_shape=(jax.ShapeDty...  32.8 us
    ppermute x18, starting transfers between devices, send(): lax.ppermute(value, BOTH, ring(first, shift))  31.8 us
    pallas_call x2, Pallas kernels, select(): pl.pallas_call(functools.partial(select_kernel, scaled), out_shape=(jax.S...  15.4 us
    pallas_call x1, Pallas kernels, expert_pre(): pl.pallas_call(pre_kernel, out_shape=(jax.ShapeDtypeStruct((WIDE + ROWS,...  14.6 us
    pallas_call x1, Pallas kernels, up_partial(): pl.pallas_call(up_kernel, out_shape=jax.ShapeDtypeStruct((width, hidden),...  13.6 us
    reduce_scatter x1, waiting for transfers between devices, body(): up_grad = lax.psum_scatter(up_part, 'dp', scatter_dimension=0, tiled=True)  12.7 us
    pallas_call x1, Pallas kernels, down_partial(): pl.pallas_call(down_kernel, out_shape=jax.ShapeDtypeStruct((hidden, width...  12.5 us
  transfers between devices with their start and end apart: 20, of which 11 were waited for; matrix products, arithmetic and copies ran while one was open for 0% of the time, Pallas kernels for 28%

profile of v1, /device:TPU:0, one launch (start us, length us, event | category | flops | bytes accessed | tf_op | source)
XLA Modules:
  0.0 330.6 jit_solution(2283044545441298086)
XLA Ops:
  9.9 3.2 collective-permute-start.2
  16.4 10.7 %collective-permute-done.2.m3.b3 = bf16[136,4096]{1,0:T(8,128)(2,1)S(1)} collective-permute-done((bf16[136,4096]{1,0:T(8,128)(2,1)S(1)}, bf16[136,4096]{1,0:T(8,128)(2,1)S(1)}, u32[]{:S(2)}, u32[]{:S(2)}) %collective-permute-start.2) | collective-permute-done | bytes 1114144 | tf_op jit(solution)/shard_map/p1x/ppermute | solution.py:47
  27.1 12.0 %collective-permute-done.1.m2.b2 = bf16[136,4096]{1,0:T(8,128)(2,1)S(1)} collective-permute-done((bf16[136,4096]{1,0:T(8,128)(2,1)S(1)}, bf16[136,4096]{1,0:T(8,128)(2,1)S(1)}, u32[]{:S(2)}, u32[]{:S(2)}) %collective-permute-start.1) | collective-permute-done | bytes 1114144 | tf_op jit(solution)/shard_map/p1x/ppermute | solution.py:47
  39.2 3.0 collective-permute-start.8
  46.3 7.7 %select.22 = (bf16[4,72,4096]{2,1,0:T(8,128)(2,1)}, bf16[4,72,4096]{2,1,0:T(8,128)(2,1)}, bf16[4,72,4096]{2,1,0:T(8,128)(2,1)}, bf16[4,72,4096]{2,1,0:T(8,128)(2,1)}) custom-call(bf16[4,288,128]{2,1,0:T(8,128)(2,1)} %get-tuple-element.36.pick_ref, f32[4,288,128]{2,1,0:T(8,128)} %get-tuple-element.37.weight_ref, bf16[136,4096]{1,0:T(8,128)(2,1)} %copy-done.1, ...), custom_call_target="tpu_custom_call" | custom-call | flops 30000001024 | bytes 1 | tf_op jit(solution)/shard_map/select/pallas_call | solution.py:118
  57.3 3.5 %collective-permute-start.5 = (bf16[4,72,4096]{2,1,0:T(8,128)(2,1)}, bf16[4,72,4096]{2,1,0:T(8,128)(2,1)}, u32[]{:S(2)}, u32[]{:S(2)}) collective-permute-start(bf16[4,72,4096]{2,1,0:T(8,128)(2,1)} %get-tuple-element.41), channel_id=1, source_target_pairs={{0,8},{1,9},{2,10},{3,11},{4,12},{5,13},{6,14},{7,15},{8,0},{9,1},... | collective-permute-start | bytes 7077896 | tf_op jit(solution)/shard_map/p2x/ppermute | solution.py:47
  60.8 16.7 %collective-permute-done.7.b2 = bf16[128,4096]{1,0:T(8,128)(2,1)} collective-permute-done((bf16[128,4096]{1,0:T(8,128)(2,1)}, bf16[128,4096]{1,0:T(8,128)(2,1)}, u32[]{:S(2)}, u32[]{:S(2)}) %collective-permute-start.7) | collective-permute-done | bytes 1048608 | tf_op jit(solution)/shard_map/p1g/ppermute | solution.py:47
  77.8 7.7 %select_scaled.1 = (bf16[4,72,4096]{2,1,0:T(8,128)(2,1)}, bf16[4,72,4096]{2,1,0:T(8,128)(2,1)}, bf16[4,72,4096]{2,1,0:T(8,128)(2,1)}, bf16[4,72,4096]{2,1,0:T(8,128)(2,1)}) custom-call(bf16[4,288,128]{2,1,0:T(8,128)(2,1)} %get-tuple-element.36.pick_ref, f32[4,288,128]{2,1,0:T(8,128)} %get-tuple-element.37.weight_ref, bf16[128,4096]{1,0:T(8,128)(2,1)} %b0, ...), custom_call_target="tpu_custom_call" | custom-call | flops 30000001024 | bytes 1 | tf_op jit(solution)/shard_map/select_scaled/pallas_call | solution.py:118
  85.5 2.9 collective-permute-start.9
  90.6 25.5 %collective-permute-done.5 = bf16[4,72,4096]{2,1,0:T(8,128)(2,1)} collective-permute-done((bf16[4,72,4096]{2,1,0:T(8,128)(2,1)}, bf16[4,72,4096]{2,1,0:T(8,128)(2,1)}, u32[]{:S(2)}, u32[]{:S(2)}) %collective-permute-start.5) | collective-permute-done | bytes 2359328 | tf_op jit(solution)/shard_map/p2x/ppermute | solution.py:47
  116.1 25.1 %collective-permute-done.9 = bf16[4,72,4096]{2,1,0:T(8,128)(2,1)S(1)} collective-permute-done((bf16[4,72,4096]{2,1,0:T(8,128)(2,1)}, bf16[4,72,4096]{2,1,0:T(8,128)(2,1)S(1)}, u32[]{:S(2)}, u32[]{:S(2)}) %collective-permute-start.9) | collective-permute-done | bytes 2359328 | tf_op jit(solution)/shard_map/p2g/ppermute | solution.py:47
  142.6 2.8 collective-permute-start.11
  145.4 14.6 %expert_pre.1 = (f32[1152,768]{1,0:T(8,128)}, bf16[768,1152]{1,0:T(8,128)(2,1)}) custom-call(bf16[288,4096]{1,0:T(8,128)(2,1)} %bitcast.35, bf16[288,4096]{1,0:T(8,128)(2,1)} %bitcast.37, bf16[288,4096]{1,0:T(8,128)(2,1)} %bitcast.39, bf16[288,4096]{1,0:T(8,128)(2,1)} %bitcast.7.refs_3_.x3, bf16[4096,768]{1,0:T(8,128)(2,1)} %bitcast.30), custom_call_target="tpu_custom_call" | custom-call | flops 7247757312 | bytes 17498112 | tf_op jit(solution)/shard_map/expert_pre/pallas_call | solution.py:188
  160.0 20.3 %expert_back.2 = (bf16[864,768]{1,0:T(8,128)(2,1)}, bf16[288,4096]{1,0:T(8,128)(2,1)}, bf16[288,4096]{1,0:T(8,128)(2,1)}, bf16[288,4096]{1,0:T(8,128)(2,1)}) custom-call(bf16[288,4096]{1,0:T(8,128)(2,1)} %bitcast.41, bf16[288,4096]{1,0:T(8,128)(2,1)} %bitcast.43, bf16[288,4096]{1,0:T(8,128)(2,1)} %bitcast.45, f32[1152,768]{1,0:T(8,128)} %get-tuple-element.46.refs_3_.refs_1_, ...), custom_call_target="tpu_custom_call" | custom-call | flops 10871635968 | bytes 23101440 | tf_op jit(solution)/shard_map/expert_back/pallas_call | solution.py:236
  181.8 12.5 %down_partial.1 = bf16[768,4096]{1,0:T(8,128)(2,1)} custom-call(bf16[768,1152]{1,0:T(8,128)(2,1)} %get-tuple-element.54.act, bf16[288,4096]{1,0:T(8,128)(2,1)} %bitcast.42, bf16[288,4096]{1,0:T(8,128)(2,1)} %bitcast.44, bf16[288,4096]{1,0:T(8,128)(2,1)} %bitcast.46, bf16[288,4096]{1,0:T(8,128)(2,1)} %bitcast.28), custom_call_target="tpu_custom_call" | custom-call | flops 1000000 | bytes 1 | tf_op jit(solution)/shard_map/down_partial/pallas_call | solution.py:284
  194.4 3.2 collective-permute-start.12
  197.6 12.5 %expert_back.3 = (bf16[288,768]{1,0:T(8,128)(2,1)}, bf16[288,4096]{1,0:T(8,128)(2,1)}) custom-call(bf16[288,4096]{1,0:T(8,128)(2,1)} %bitcast.29, f32[1152,768]{1,0:T(8,128)} %get-tuple-element.46.refs_3_.refs_1_, bf16[768,4096]{1,0:T(8,128)(2,1)} %bitcast.34, bf16[4096,768]{1,0:T(8,128)(2,1)} %bitcast.32), custom_call_target="tpu_custom_call" | custom-call | flops 1000000 | bytes 1 | tf_op jit(solution)/shard_map/expert_back/pallas_call | solution.py:236
  210.1 39.8 %collective-permute-done.13.r2 = bf16[4,72,4096]{2,1,0:T(8,128)(2,1)S(1)} collective-permute-done((bf16[4,72,4096]{2,1,0:T(8,128)(2,1)}, bf16[4,72,4096]{2,1,0:T(8,128)(2,1)S(1)}, u32[]{:S(2)}, u32[]{:S(2)}) %collective-permute-start.13) | collective-permute-done | bytes 2359328 | tf_op jit(solution)/shard_map/r2/ppermute | solution.py:47
  249.9 13.6 %up_partial.1 = bf16[4096,768]{1,0:T(8,128)(2,1)} custom-call(bf16[288,4096]{1,0:T(8,128)(2,1)} %bitcast.36, bf16[288,4096]{1,0:T(8,128)(2,1)} %bitcast.38, bf16[288,4096]{1,0:T(8,128)(2,1)} %bitcast.40, bf16[288,4096]{1,0:T(8,128)(2,1)} %bitcast.7.refs_3_.x3, bf16[864,768]{1,0:T(8,128)(2,1)} %get-tuple-element.47.grad, ...), custom_call_target="tpu_custom_call" | custom-call | flops 1000000 | bytes 1 | tf_op jit(solution)/shard_map/up_partial/pallas_call | solution.py:264
  263.5 8.3 %combine.1 = (bf16[128,4096]{1,0:T(8,128)(2,1)}, bf16[128,4096]{1,0:T(8,128)(2,1)}, bf16[128,4096]{1,0:T(8,128)(2,1)}, bf16[128,4096]{1,0:T(8,128)(2,1)}) custom-call(bf16[4,4,128,72]{3,2,1,0:T(8,128)(2,1)} %get-tuple-element.59.put_ref, bf16[4,72,4096]{2,1,0:T(8,128)(2,1)} %bitcast.47, bf16[4,72,4096]{2,1,0:T(8,128)(2,1)} %collective-permute-done.12.r1, ...), custom_call_target="tpu_custom_call" | custom-call | flops 1000000 | bytes 1 | tf_op jit(solution)/shard_map/combine/pallas_call | solution.py:146
  276.8 21.5 %collective-permute-done.15.p1 = bf16[128,4096]{1,0:T(8,128)(2,1)S(1)} collective-permute-done((bf16[128,4096]{1,0:T(8,128)(2,1)}, bf16[128,4096]{1,0:T(8,128)(2,1)S(1)}, u32[]{:S(2)}, u32[]{:S(2)}) %collective-permute-start.15) | collective-permute-done | bytes 1048608 | tf_op jit(solution)/shard_map/r1/ppermute | solution.py:47
  298.3 3.6 %collective-permute-done.16.p2 = bf16[128,4096]{1,0:T(8,128)(2,1)S(1)} collective-permute-done((bf16[128,4096]{1,0:T(8,128)(2,1)}, bf16[128,4096]{1,0:T(8,128)(2,1)S(1)}, u32[]{:S(2)}, u32[]{:S(2)}) %collective-permute-start.16) | collective-permute-done | bytes 1048608 | tf_op jit(solution)/shard_map/r1/ppermute | solution.py:47
  303.2 4.2 %sum_parts.1 = bf16[128,4096]{1,0:T(8,128)(2,1)} custom-call(bf16[128,4096]{1,0:T(8,128)(2,1)} %get-tuple-element.60.p0, bf16[128,4096]{1,0:T(8,128)(2,1)} %copy-done.10, bf16[128,4096]{1,0:T(8,128)(2,1)} %copy-done.11, bf16[128,4096]{1,0:T(8,128)(2,1)} %copy-done.12), custom_call_target="tpu_custom_call" | custom-call | flops 299999985664 | bytes 1 | tf_op jit(solution)/shard_map/sum_parts/pallas_call | solution.py:305
  307.4 12.7 %reduce-scatter.3.cloned.1.call-done = bf16[512,768]{1,0:T(8,128)(2,1)} async-done(((bf16[4096,768]{1,0:T(8,128)(2,1)}), bf16[512,768]{1,0:T(8,128)(2,1)}) %reduce-scatter.3.cloned.1.call-update) | async-done | bytes 786448 | tf_op jit(solution)/shard_map/reduce_scatter | solution.py:369
  (61 shorter events, 28.9 us)
Async XLA Ops:
  7.2 300.2 %reduce-scatter.5.cloned.1.call-start = ((), (), s32[]{:S(2)}) async-start(), calls=%async_computation.3 | async-start | bytes 7077888 | tf_op jit(solution)/shard_map/reduce_scatter | solution.py:362
  9.9 34.3 %copy-start.1 = (bf16[136,4096]{1,0:T(8,128)(2,1)}, bf16[136,4096]{1,0:T(8,128)(2,1)S(1)}, u32[]{:S(2)}) copy-start(bf16[136,4096]{1,0:T(8,128)(2,1)S(1)} %pad_maximum_fusion.m0.b0) | copy-start | bytes 3342340
  9.9 17.2 %collective-permute-start.2 = (bf16[136,4096]{1,0:T(8,128)(2,1)S(1)}, bf16[136,4096]{1,0:T(8,128)(2,1)S(1)}, u32[]{:S(2)}, u32[]{:S(2)}) collective-permute-start(bf16[136,4096]{1,0:T(8,128)(2,1)S(1)} %pad_maximum_fusion.m0.b0), channel_id=1, source_target_pairs={{0,2},{1,3},{2,0},{3,1},{4,6},{5,7},{6,4},{7,5},{8,10},{9,11},{10,... | collective-permute-start | bytes 3342344 | tf_op jit(solution)/shard_map/p1x/ppermute | solution.py:47
  13.1 26.0 %collective-permute-start.1 = (bf16[136,4096]{1,0:T(8,128)(2,1)S(1)}, bf16[136,4096]{1,0:T(8,128)(2,1)S(1)}, u32[]{:S(2)}, u32[]{:S(2)}) collective-permute-start(bf16[136,4096]{1,0:T(8,128)(2,1)S(1)} %pad_maximum_fusion.m0.b0), channel_id=1, source_target_pairs={{0,3},{1,0},{2,1},{3,2},{4,7},{5,4},{6,5},{7,6},{8,11},{9,8},{10,9... | collective-permute-start | bytes 3342344 | tf_op jit(solution)/shard_map/p1x/ppermute | solution.py:47
  14.2 24.9 %collective-permute-start = (bf16[136,4096]{1,0:T(8,128)(2,1)S(1)}, bf16[136,4096]{1,0:T(8,128)(2,1)}, u32[]{:S(2)}, u32[]{:S(2)}) collective-permute-start(bf16[136,4096]{1,0:T(8,128)(2,1)S(1)} %pad_maximum_fusion.m0.b0), channel_id=1, source_target_pairs={{0,1},{1,2},{2,3},{3,0},{4,5},{5,6},{6,7},{7,4},{8,9},{9,10},{10,1... | collective-permute-start | bytes 3342344 | tf_op jit(solution)/shard_map/p1x/ppermute | solution.py:47
  27.1 17.1 %copy-start.7 = (bf16[136,4096]{1,0:T(8,128)(2,1)}, bf16[136,4096]{1,0:T(8,128)(2,1)S(1)}, u32[]{:S(2)}) copy-start(bf16[136,4096]{1,0:T(8,128)(2,1)S(1)} %collective-permute-done.2.m3.b3) | copy-start | bytes 3342340
  39.2 18.1 %collective-permute-start.8 = (bf16[128,4096]{1,0:T(8,128)(2,1)}, bf16[128,4096]{1,0:T(8,128)(2,1)}, u32[]{:S(2)}, u32[]{:S(2)}) collective-permute-start(bf16[128,4096]{1,0:T(8,128)(2,1)} %b0), channel_id=1, source_target_pairs={{0,2},{1,3},{2,0},{3,1},{4,6},{5,7},{6,4},{7,5},{8,10},{9,11},{10,... | collective-permute-start | bytes 3145736 | tf_op jit(solution)/shard_map/p1g/ppermute | solution.py:47
  42.1 35.4 %collective-permute-start.7 = (bf16[128,4096]{1,0:T(8,128)(2,1)}, bf16[128,4096]{1,0:T(8,128)(2,1)}, u32[]{:S(2)}, u32[]{:S(2)}) collective-permute-start(bf16[128,4096]{1,0:T(8,128)(2,1)} %b0), channel_id=1, source_target_pairs={{0,3},{1,0},{2,1},{3,2},{4,7},{5,4},{6,5},{7,6},{8,11},{9,8},{10,9... | collective-permute-start | bytes 3145736 | tf_op jit(solution)/shard_map/p1g/ppermute | solution.py:47
  43.4 34.5 %collective-permute-start.6 = (bf16[128,4096]{1,0:T(8,128)(2,1)}, bf16[128,4096]{1,0:T(8,128)(2,1)}, u32[]{:S(2)}, u32[]{:S(2)}) collective-permute-start(bf16[128,4096]{1,0:T(8,128)(2,1)} %b0), channel_id=1, source_target_pairs={{0,1},{1,2},{2,3},{3,0},{4,5},{5,6},{6,7},{7,4},{8,9},{9,10},{10,1... | collective-permute-start | bytes 3145736 | tf_op jit(solution)/shard_map/p1g/ppermute | solution.py:47
  54.0 36.5 %collective-permute-start.3 = (bf16[4,72,4096]{2,1,0:T(8,128)(2,1)}, bf16[4,72,4096]{2,1,0:T(8,128)(2,1)S(1)}, u32[]{:S(2)}, u32[]{:S(2)}) collective-permute-start(bf16[4,72,4096]{2,1,0:T(8,128)(2,1)} %get-tuple-element.39), channel_id=1, source_target_pairs={{0,4},{1,5},{2,6},{3,7},{4,8},{5,9},{6,10},{7,11},{8,12},{9,13},{1... | collective-permute-start | bytes 7077896 | tf_op jit(solution)/shard_map/p2x/ppermute | solution.py:47
  55.6 35.0 %collective-permute-start.4 = (bf16[4,72,4096]{2,1,0:T(8,128)(2,1)}, bf16[4,72,4096]{2,1,0:T(8,128)(2,1)S(1)}, u32[]{:S(2)}, u32[]{:S(2)}) collective-permute-start(bf16[4,72,4096]{2,1,0:T(8,128)(2,1)} %get-tuple-element.40), channel_id=1, source_target_pairs={{0,12},{1,13},{2,14},{3,15},{4,0},{5,1},{6,2},{7,3},{8,4},{9,5},{1... | collective-permute-start | bytes 7077896 | tf_op jit(solution)/shard_map/p2x/ppermute | solution.py:47
  57.3 58.8 %collective-permute-start.5 = (bf16[4,72,4096]{2,1,0:T(8,128)(2,1)}, bf16[4,72,4096]{2,1,0:T(8,128)(2,1)}, u32[]{:S(2)}, u32[]{:S(2)}) collective-permute-start(bf16[4,72,4096]{2,1,0:T(8,128)(2,1)} %get-tuple-element.41), channel_id=1, source_target_pairs={{0,8},{1,9},{2,10},{3,11},{4,12},{5,13},{6,14},{7,15},{8,0},{9,1},... | collective-permute-start | bytes 7077896 | tf_op jit(solution)/shard_map/p2x/ppermute | solution.py:47
  85.5 55.6 %collective-permute-start.9 = (bf16[4,72,4096]{2,1,0:T(8,128)(2,1)}, bf16[4,72,4096]{2,1,0:T(8,128)(2,1)S(1)}, u32[]{:S(2)}, u32[]{:S(2)}) collective-permute-start(bf16[4,72,4096]{2,1,0:T(8,128)(2,1)} %get-tuple-element.44), channel_id=1, source_target_pairs={{0,4},{1,5},{2,6},{3,7},{4,8},{5,9},{6,10},{7,11},{8,12},{9,13},{1... | collective-permute-start | bytes 7077896 | tf_op jit(solution)/shard_map/p2g/ppermute | solution.py:47
  88.4 52.8 %collective-permute-start.10 = (bf16[4,72,4096]{2,1,0:T(8,128)(2,1)}, bf16[4,72,4096]{2,1,0:T(8,128)(2,1)S(1)}, u32[]{:S(2)}, u32[]{:S(2)}) collective-permute-start(bf16[4,72,4096]{2,1,0:T(8,128)(2,1)} %get-tuple-element.45), channel_id=1, source_target_pairs={{0,12},{1,13},{2,14},{3,15},{4,0},{5,1},{6,2},{7,3},{8,4},{9,5},{1... | collective-permute-start | bytes 7077896 | tf_op jit(solution)/shard_map/p2g/ppermute | solution.py:47
  90.6 54.8 %copy-start.2 = (bf16[4,72,4096]{2,1,0:T(8,128)(2,1)}, bf16[4,72,4096]{2,1,0:T(8,128)(2,1)S(1)}, u32[]{:S(2)}) copy-start(bf16[4,72,4096]{2,1,0:T(8,128)(2,1)S(1)} %collective-permute-done.3) | copy-start | bytes 7077892
  90.6 50.6 %copy-start.3 = (bf16[4,72,4096]{2,1,0:T(8,128)(2,1)}, bf16[4,72,4096]{2,1,0:T(8,128)(2,1)S(1)}, u32[]{:S(2)}) copy-start(bf16[4,72,4096]{2,1,0:T(8,128)(2,1)S(1)} %collective-permute-done.4) | copy-start | bytes 7077892
  142.6 37.8 %collective-permute-start.11 = (bf16[4,72,4096]{2,1,0:T(8,128)(2,1)}, bf16[4,72,4096]{2,1,0:T(8,128)(2,1)S(1)}, u32[]{:S(2)}, u32[]{:S(2)}) collective-permute-start(bf16[4,72,4096]{2,1,0:T(8,128)(2,1)} %get-tuple-element.49), channel_id=1, source_target_pairs={{0,8},{1,9},{2,10},{3,11},{4,12},{5,13},{6,14},{7,15},{8,0},{9,1},... | collective-permute-start | bytes 7077896 | tf_op jit(solution)/shard_map/p2g2/ppermute | solution.py:47
  194.3 125.8 %reduce-scatter.3.cloned.1.call-start = ((), (), s32[]{:S(2)}) async-start(), calls=%async_computation.2 | async-start | bytes 7077888 | tf_op jit(solution)/shard_map/reduce_scatter | solution.py:369
  194.3 55.6 %collective-permute-start.13 = (bf16[4,72,4096]{2,1,0:T(8,128)(2,1)}, bf16[4,72,4096]{2,1,0:T(8,128)(2,1)S(1)}, u32[]{:S(2)}, u32[]{:S(2)}) collective-permute-start(bf16[4,72,4096]{2,1,0:T(8,128)(2,1)} %bitcast.49), channel_id=1, source_target_pairs={{0,4},{1,5},{2,6},{3,7},{4,8},{5,9},{6,10},{7,11},{8,12},{9,13},{1... | collective-permute-start | bytes 7077896 | tf_op jit(solution)/shard_map/r2/ppermute | solution.py:47
  194.4 55.5 %collective-permute-start.12 = (bf16[4,72,4096]{2,1,0:T(8,128)(2,1)}, bf16[4,72,4096]{2,1,0:T(8,128)(2,1)}, u32[]{:S(2)}, u32[]{:S(2)}) collective-permute-start(bf16[4,72,4096]{2,1,0:T(8,128)(2,1)} %bitcast.48), channel_id=1, source_target_pairs={{0,12},{1,13},{2,14},{3,15},{4,0},{5,1},{6,2},{7,3},{8,4},{9,5},{1... | collective-permute-start | bytes 7077896 | tf_op jit(solution)/shard_map/r2/ppermute | solution.py:47
  210.1 53.4 %collective-permute-start.14 = (bf16[4,72,4096]{2,1,0:T(8,128)(2,1)}, bf16[4,72,4096]{2,1,0:T(8,128)(2,1)}, u32[]{:S(2)}, u32[]{:S(2)}) collective-permute-start(bf16[4,72,4096]{2,1,0:T(8,128)(2,1)} %bitcast.50), channel_id=1, source_target_pairs={{0,8},{1,9},{2,10},{3,11},{4,12},{5,13},{6,14},{7,15},{8,0},{9,1},... | collective-permute-start | bytes 7077896 | tf_op jit(solution)/shard_map/r2/ppermute | solution.py:47
  271.8 26.5 %collective-permute-start.15 = (bf16[128,4096]{1,0:T(8,128)(2,1)}, bf16[128,4096]{1,0:T(8,128)(2,1)S(1)}, u32[]{:S(2)}, u32[]{:S(2)}) collective-permute-start(bf16[128,4096]{1,0:T(8,128)(2,1)} %get-tuple-element.61), channel_id=1, source_target_pairs={{0,3},{1,0},{2,1},{3,2},{4,7},{5,4},{6,5},{7,6},{8,11},{9,8},{10,9... | collective-permute-start | bytes 3145736 | tf_op jit(solution)/shard_map/r1/ppermute | solution.py:47
  274.4 27.5 %collective-permute-start.16 = (bf16[128,4096]{1,0:T(8,128)(2,1)}, bf16[128,4096]{1,0:T(8,128)(2,1)S(1)}, u32[]{:S(2)}, u32[]{:S(2)}) collective-permute-start(bf16[128,4096]{1,0:T(8,128)(2,1)} %get-tuple-element.62), channel_id=1, source_target_pairs={{0,1},{1,2},{2,3},{3,0},{4,5},{5,6},{6,7},{7,4},{8,9},{9,10},{10,1... | collective-permute-start | bytes 3145736 | tf_op jit(solution)/shard_map/r1/ppermute | solution.py:47
  274.4 27.5 %collective-permute-start.17 = (bf16[128,4096]{1,0:T(8,128)(2,1)}, bf16[128,4096]{1,0:T(8,128)(2,1)S(1)}, u32[]{:S(2)}, u32[]{:S(2)}) collective-permute-start(bf16[128,4096]{1,0:T(8,128)(2,1)} %get-tuple-element.63), channel_id=1, source_target_pairs={{0,2},{1,3},{2,0},{3,1},{4,6},{5,7},{6,4},{7,5},{8,10},{9,11},{10,... | collective-permute-start | bytes 3145736 | tf_op jit(solution)/shard_map/r1/ppermute | solution.py:47
  (9 other events, 46.7 us)
Sparse Core Ops, SparseCore 0:
  194.4 44.4 reduce-scatter.4
  277.0 43.0 reduce-scatter.2

commit v2 on v1

--- a/solution.py
+++ b/solution.py
@@ -269,7 +269,7 @@
         + [pl.BlockSpec(g.shape, lambda c: (0, 0)) for g in grads],
         out_specs=pl.BlockSpec((TILE, hidden), lambda c: (c, 0)),
         compiler_params=PARAMS,
-        cost_estimate=LIGHT,
+        cost_estimate=LONGEST,
         name="up_partial",
     )(*xs, *grads)
 
@@ -309,7 +309,7 @@
         in_specs=[spec] * SIDE,
         out_specs=spec,
         compiler_params=PARAMS,
-        cost_estimate=LONGEST,
+        cost_estimate=LIGHT,
         name="sum_parts",
     )(*parts)
 
@@ -351,7 +351,7 @@
         rg = [send(r, False, o).reshape(ROWS, width) for r, o in zip(out_g[:3], OFFSETS)]
     pre, act = expert_pre(rx, up_matrix)
     with jax.named_scope("p2g2"):
-        last = send(after(out_g[3], *rx, *rg), False, OFFSETS[3]).reshape(ROWS, width)
+        last = send(after(out_g[3], pre, *rx, *rg), False, OFFSETS[3]).reshape(ROWS, width)
 
     grad, rows = expert_back(rg, pre, 0, down_matrix, up_matrix)
     with jax.named_scope("r2"):
@@ -363,12 +363,14 @@
     last = after(last, down_part)
     grad_last, rows_last = expert_back([last], pre, 3, down_matrix, up_matrix)
     with jax.named_scope("r2"):
-        returned.append(send(rows_last[0].reshape(SIDE, SLOTS, width), False, -OFFSETS[3]))
-    grad_last = after(grad_last, rows_last[0], *returned[:3])
+        rows_last = after(rows_last[0], *returned).reshape(SIDE, SLOTS, width)
+        returned.append(send(rows_last, False, -OFFSETS[3]))
+    grad_last = after(grad_last, *returned[:3])
     up_part = up_partial(rx, [grad, grad_last])
+    up_done, up_part = up_part, after(up_part, down_grad, returned[3])
     up_grad = lax.psum_scatter(up_part, "dp", scatter_dimension=0, tiled=True)
 
-    parts = combine(after(put, up_part), returned)
+    parts = combine(after(put, up_done), returned)
     with jax.named_scope("r1"):
         parts = [send(p, True, -o) for p, o in zip(parts, OFFSETS)]
     token_grad = sum_parts(parts)

time: 332 us -> 289 us (0.87)
  waiting for transfers between devices: 169 us -> 125 us
    ppermute x18, waiting for transfers between devices: 157 us -> 122 us  [send(): lax.ppermute(value, BOTH, ring(first, shift))]
    reduce_scatter x1, waiting for transfers between devices: 12.7 us -> 0.71 us  [body(): up_grad = lax.psum_scatter(up_part, 'dp', scatter_dimension=0, tiled=True)]
  transfers between devices with their start and end apart: 20 -> 20, of which waited for: 11 -> 13; matrix products, arithmetic and copies ran while one was open for 0% -> 0% of each run, Pallas kernels for 28% -> 36%
where the time goes in v2:
time: 289 us; the launch traced here: 288 us
  waiting for transfers between devices  125 us (43%)
  Pallas kernels  103 us (36%)
  starting transfers between devices  34.6 us (12%)
  between operations  14.1 us (5%)
  other arithmetic  7.59 us (3%)
  local copies, waits for them, and re-layouts  4.14 us (1%)
    ppermute x18, waiting for transfers between devices, send(): lax.ppermute(value, BOTH, ring(first, shift))  122 us
    ppermute x18, starting transfers between devices, send(): lax.ppermute(value, BOTH, ring(first, shift))  34.6 us
    pallas_call x2, Pallas kernels, expert_back(): pl.pallas_call(functools.partial(back_kernel, n), out_shape=(jax.ShapeDty...  32.7 us
    pallas_call x2, Pallas kernels, select(): pl.pallas_call(functools.partial(select_kernel, scaled), out_shape=(jax.S...  15.4 us
    pallas_call x1, Pallas kernels, expert_pre(): pl.pallas_call(pre_kernel, out_shape=(jax.ShapeDtypeStruct((WIDE + ROWS,...  14.6 us
    pallas_call x1, Pallas kernels, up_partial(): pl.pallas_call(up_kernel, out_shape=jax.ShapeDtypeStruct((width, hidden),...  12.8 us
    pallas_call x1, Pallas kernels, down_partial(): pl.pallas_call(down_kernel, out_shape=jax.ShapeDtypeStruct((hidden, width...  12.5 us
    pallas_call x1, Pallas kernels, combine(): pl.pallas_call(combine_kernel, out_shape=(jax.ShapeDtypeStruct((128, widt...  8.28 us
  transfers between devices with their start and end apart: 20, of which 13 were waited for; matrix products, arithmetic and copies ran while one was open for 0% of the time, Pallas kernels for 36%

profile of v2, /device:TPU:0, one launch (start us, length us, event | category | flops | bytes accessed | tf_op | source)
XLA Modules:
  0.0 288.2 jit_solution(17441201989941516871)
XLA Ops:
  9.9 3.2 %collective-permute-start.2 = (bf16[136,4096]{1,0:T(8,128)(2,1)S(1)}, bf16[136,4096]{1,0:T(8,128)(2,1)S(1)}, u32[]{:S(2)}, u32[]{:S(2)}) collective-permute-start(bf16[136,4096]{1,0:T(8,128)(2,1)S(1)} %pad_maximum_fusion.m0.b0), channel_id=1, source_target_pairs={{0,2},{1,3},{2,0},{3,1},{4,6},{5,7},{6,4},{7,5},{8,10},{9,11},{10,... | collective-permute-start | bytes 3342344 | tf_op jit(solution)/shard_map/p1x/ppermute | solution.py:47
  16.4 10.7 %collective-permute-done.2.m3.b3 = bf16[136,4096]{1,0:T(8,128)(2,1)S(1)} collective-permute-done((bf16[136,4096]{1,0:T(8,128)(2,1)S(1)}, bf16[136,4096]{1,0:T(8,128)(2,1)S(1)}, u32[]{:S(2)}, u32[]{:S(2)}) %collective-permute-start.2) | collective-permute-done | bytes 1114144 | tf_op jit(solution)/shard_map/p1x/ppermute | solution.py:47
  27.1 12.0 %collective-permute-done.1.m2.b2 = bf16[136,4096]{1,0:T(8,128)(2,1)S(1)} collective-permute-done((bf16[136,4096]{1,0:T(8,128)(2,1)S(1)}, bf16[136,4096]{1,0:T(8,128)(2,1)S(1)}, u32[]{:S(2)}, u32[]{:S(2)}) %collective-permute-start.1) | collective-permute-done | bytes 1114144 | tf_op jit(solution)/shard_map/p1x/ppermute | solution.py:47
  39.2 3.0 %collective-permute-start.8 = (bf16[128,4096]{1,0:T(8,128)(2,1)}, bf16[128,4096]{1,0:T(8,128)(2,1)}, u32[]{:S(2)}, u32[]{:S(2)}) collective-permute-start(bf16[128,4096]{1,0:T(8,128)(2,1)} %b0), channel_id=1, source_target_pairs={{0,2},{1,3},{2,0},{3,1},{4,6},{5,7},{6,4},{7,5},{8,10},{9,11},{10,... | collective-permute-start | bytes 3145736 | tf_op jit(solution)/shard_map/p1g/ppermute | solution.py:47
  46.3 7.7 %select.22 = (bf16[4,72,4096]{2,1,0:T(8,128)(2,1)}, bf16[4,72,4096]{2,1,0:T(8,128)(2,1)}, bf16[4,72,4096]{2,1,0:T(8,128)(2,1)}, bf16[4,72,4096]{2,1,0:T(8,128)(2,1)}) custom-call(bf16[4,288,128]{2,1,0:T(8,128)(2,1)} %get-tuple-element.38.pick_ref, f32[4,288,128]{2,1,0:T(8,128)} %get-tuple-element.39.weight_ref, bf16[136,4096]{1,0:T(8,128)(2,1)} %copy-done.1, ...), custom_call_target="tpu_custom_call" | custom-call | flops 30000001024 | bytes 1 | tf_op jit(solution)/shard_map/select/pallas_call | solution.py:118
  57.3 3.5 %collective-permute-start.5 = (bf16[4,72,4096]{2,1,0:T(8,128)(2,1)}, bf16[4,72,4096]{2,1,0:T(8,128)(2,1)}, u32[]{:S(2)}, u32[]{:S(2)}) collective-permute-start(bf16[4,72,4096]{2,1,0:T(8,128)(2,1)} %get-tuple-element.43), channel_id=1, source_target_pairs={{0,8},{1,9},{2,10},{3,11},{4,12},{5,13},{6,14},{7,15},{8,0},{9,1},... | collective-permute-start | bytes 7077896 | tf_op jit(solution)/shard_map/p2x/ppermute | solution.py:47
  60.8 16.7 %collective-permute-done.7.b2 = bf16[128,4096]{1,0:T(8,128)(2,1)} collective-permute-done((bf16[128,4096]{1,0:T(8,128)(2,1)}, bf16[128,4096]{1,0:T(8,128)(2,1)}, u32[]{:S(2)}, u32[]{:S(2)}) %collective-permute-start.7) | collective-permute-done | bytes 1048608 | tf_op jit(solution)/shard_map/p1g/ppermute | solution.py:47
  77.8 7.7 %select_scaled.1 = (bf16[4,72,4096]{2,1,0:T(8,128)(2,1)}, bf16[4,72,4096]{2,1,0:T(8,128)(2,1)}, bf16[4,72,4096]{2,1,0:T(8,128)(2,1)}, bf16[4,72,4096]{2,1,0:T(8,128)(2,1)}) custom-call(bf16[4,288,128]{2,1,0:T(8,128)(2,1)} %get-tuple-element.38.pick_ref, f32[4,288,128]{2,1,0:T(8,128)} %get-tuple-element.39.weight_ref, bf16[128,4096]{1,0:T(8,128)(2,1)} %b0, ...), custom_call_target="tpu_custom_call" | custom-call | flops 30000001024 | bytes 1 | tf_op jit(solution)/shard_map/select_scaled/pallas_call | solution.py:118
  85.5 2.9 collective-permute-start.9
  90.7 25.4 %collective-permute-done.5 = bf16[4,72,4096]{2,1,0:T(8,128)(2,1)} collective-permute-done((bf16[4,72,4096]{2,1,0:T(8,128)(2,1)}, bf16[4,72,4096]{2,1,0:T(8,128)(2,1)}, u32[]{:S(2)}, u32[]{:S(2)}) %collective-permute-start.5) | collective-permute-done | bytes 2359328 | tf_op jit(solution)/shard_map/p2x/ppermute | solution.py:47
  116.1 14.6 %expert_pre.1 = (f32[1152,768]{1,0:T(8,128)}, bf16[768,1152]{1,0:T(8,128)(2,1)}) custom-call(bf16[288,4096]{1,0:T(8,128)(2,1)} %bitcast.45, bf16[288,4096]{1,0:T(8,128)(2,1)} %bitcast.5.refs_1_.x1, bf16[288,4096]{1,0:T(8,128)(2,1)} %bitcast.6.refs_2_.x2, bf16[288,4096]{1,0:T(8,128)(2,1)} %bitcast.7.refs_3_.x3, bf16[4096,768]{1,0:T(8,128)(2,1)} %bitcast.30), custom_call_target="tpu_custom_call" | custom-call | flops 7247757312 | bytes 17498112 | tf_op jit(solution)/shard_map/expert_pre/pallas_call | solution.py:188
  130.7 10.5 %collective-permute-done.9 = bf16[4,72,4096]{2,1,0:T(8,128)(2,1)S(1)} collective-permute-done((bf16[4,72,4096]{2,1,0:T(8,128)(2,1)}, bf16[4,72,4096]{2,1,0:T(8,128)(2,1)S(1)}, u32[]{:S(2)}, u32[]{:S(2)}) %collective-permute-start.9) | collective-permute-done | bytes 2359328 | tf_op jit(solution)/shard_map/p2g/ppermute | solution.py:47
  142.6 2.8 collective-permute-start.11
  145.4 20.4 %expert_back.2 = (bf16[864,768]{1,0:T(8,128)(2,1)}, bf16[288,4096]{1,0:T(8,128)(2,1)}, bf16[288,4096]{1,0:T(8,128)(2,1)}, bf16[288,4096]{1,0:T(8,128)(2,1)}) custom-call(bf16[288,4096]{1,0:T(8,128)(2,1)} %bitcast.35, bf16[288,4096]{1,0:T(8,128)(2,1)} %bitcast.37, bf16[288,4096]{1,0:T(8,128)(2,1)} %bitcast.39, f32[1152,768]{1,0:T(8,128)} %get-tuple-element.48.refs_3_.refs_1_, ...), custom_call_target="tpu_custom_call" | custom-call | flops 10871635968 | bytes 23101440 | tf_op jit(solution)/shard_map/expert_back/pallas_call | solution.py:236
  169.0 4.2 %collective-permute-done.11 = bf16[4,72,4096]{2,1,0:T(8,128)(2,1)S(1)} collective-permute-done((bf16[4,72,4096]{2,1,0:T(8,128)(2,1)}, bf16[4,72,4096]{2,1,0:T(8,128)(2,1)S(1)}, u32[]{:S(2)}, u32[]{:S(2)}) %collective-permute-start.11) | collective-permute-done | bytes 2359328 | tf_op jit(solution)/shard_map/p2g2/ppermute | solution.py:47
  174.7 12.5 %down_partial.1 = bf16[768,4096]{1,0:T(8,128)(2,1)} custom-call(bf16[768,1152]{1,0:T(8,128)(2,1)} %get-tuple-element.56.act, bf16[288,4096]{1,0:T(8,128)(2,1)} %bitcast.36, bf16[288,4096]{1,0:T(8,128)(2,1)} %bitcast.38, bf16[288,4096]{1,0:T(8,128)(2,1)} %bitcast.40, bf16[288,4096]{1,0:T(8,128)(2,1)} %bitcast.28), custom_call_target="tpu_custom_call" | custom-call | flops 1000000 | bytes 1 | tf_op jit(solution)/shard_map/down_partial/pallas_call | solution.py:284
  187.2 12.4 %expert_back.3 = (bf16[288,768]{1,0:T(8,128)(2,1)}, bf16[288,4096]{1,0:T(8,128)(2,1)}) custom-call(bf16[288,4096]{1,0:T(8,128)(2,1)} %bitcast.29, f32[1152,768]{1,0:T(8,128)} %get-tuple-element.48.refs_3_.refs_1_, bf16[768,4096]{1,0:T(8,128)(2,1)} %bitcast.34, bf16[4096,768]{1,0:T(8,128)(2,1)} %bitcast.32), custom_call_target="tpu_custom_call" | custom-call | flops 1000000 | bytes 1 | tf_op jit(solution)/shard_map/expert_back/pallas_call | solution.py:236
  199.6 2.9 collective-permute-start.14
  202.5 12.8 %up_partial.1 = bf16[4096,768]{1,0:T(8,128)(2,1)} custom-call(bf16[288,4096]{1,0:T(8,128)(2,1)} %bitcast.46, bf16[288,4096]{1,0:T(8,128)(2,1)} %bitcast.5.refs_1_.x1, bf16[288,4096]{1,0:T(8,128)(2,1)} %bitcast.6.refs_2_.x2, bf16[288,4096]{1,0:T(8,128)(2,1)} %bitcast.7.refs_3_.x3, bf16[864,768]{1,0:T(8,128)(2,1)} %get-tuple-element.49.grad, ...), custom_call_target="tpu_custom_call" | custom-call | flops 299999985664 | bytes 1 | tf_op jit(solution)/shard_map/up_partial/pallas_call | solution.py:264
  215.3 15.1 %collective-permute-done.14.r3 = bf16[4,72,4096]{2,1,0:T(8,128)(2,1)} collective-permute-done((bf16[4,72,4096]{2,1,0:T(8,128)(2,1)}, bf16[4,72,4096]{2,1,0:T(8,128)(2,1)}, u32[]{:S(2)}, u32[]{:S(2)}) %collective-permute-start.14) | collective-permute-done | bytes 2359328 | tf_op jit(solution)/shard_map/r2/ppermute | solution.py:47
  233.1 8.3 %combine.1 = (bf16[128,4096]{1,0:T(8,128)(2,1)}, bf16[128,4096]{1,0:T(8,128)(2,1)}, bf16[128,4096]{1,0:T(8,128)(2,1)}, bf16[128,4096]{1,0:T(8,128)(2,1)}) custom-call(bf16[4,4,128,72]{3,2,1,0:T(8,128)(2,1)} %get-tuple-element.60.put_ref, bf16[4,72,4096]{2,1,0:T(8,128)(2,1)} %bitcast.41, bf16[4,72,4096]{2,1,0:T(8,128)(2,1)} %collective-permute-done.12.r1, ...), custom_call_target="tpu_custom_call" | custom-call | flops 1000000 | bytes 1 | tf_op jit(solution)/shard_map/combine/pallas_call | solution.py:146
  246.3 21.6 %collective-permute-done.15.p1 = bf16[128,4096]{1,0:T(8,128)(2,1)S(1)} collective-permute-done((bf16[128,4096]{1,0:T(8,128)(2,1)}, bf16[128,4096]{1,0:T(8,128)(2,1)S(1)}, u32[]{:S(2)}, u32[]{:S(2)}) %collective-permute-start.15) | collective-permute-done | bytes 1048608 | tf_op jit(solution)/shard_map/r1/ppermute | solution.py:47
  267.9 3.6 %collective-permute-done.16.p2 = bf16[128,4096]{1,0:T(8,128)(2,1)S(1)} collective-permute-done((bf16[128,4096]{1,0:T(8,128)(2,1)}, bf16[128,4096]{1,0:T(8,128)(2,1)S(1)}, u32[]{:S(2)}, u32[]{:S(2)}) %collective-permute-start.16) | collective-permute-done | bytes 1048608 | tf_op jit(solution)/shard_map/r1/ppermute | solution.py:47
  272.8 4.1 %sum_parts.1 = bf16[128,4096]{1,0:T(8,128)(2,1)} custom-call(bf16[128,4096]{1,0:T(8,128)(2,1)} %get-tuple-element.63.p0, bf16[128,4096]{1,0:T(8,128)(2,1)} %copy-done.6, bf16[128,4096]{1,0:T(8,128)(2,1)} %copy-done.7, bf16[128,4096]{1,0:T(8,128)(2,1)} %copy-done.8), custom_call_target="tpu_custom_call" | custom-call | flops 1000000 | bytes 1 | tf_op jit(solution)/shard_map/sum_parts/pallas_call | solution.py:305
  (55 shorter events, 35.6 us)
Async XLA Ops:
  7.2 225.9 %reduce-scatter.3.cloned.1.call-start = ((), (), s32[]{:S(2)}) async-start(), calls=%async_computation.2 | async-start | bytes 7077888 | tf_op jit(solution)/shard_map/reduce_scatter | solution.py:362
  9.9 34.3 %copy-start.1 = (bf16[136,4096]{1,0:T(8,128)(2,1)}, bf16[136,4096]{1,0:T(8,128)(2,1)S(1)}, u32[]{:S(2)}) copy-start(bf16[136,4096]{1,0:T(8,128)(2,1)S(1)} %pad_maximum_fusion.m0.b0) | copy-start | bytes 3342340
  9.9 17.2 %collective-permute-start.2 = (bf16[136,4096]{1,0:T(8,128)(2,1)S(1)}, bf16[136,4096]{1,0:T(8,128)(2,1)S(1)}, u32[]{:S(2)}, u32[]{:S(2)}) collective-permute-start(bf16[136,4096]{1,0:T(8,128)(2,1)S(1)} %pad_maximum_fusion.m0.b0), channel_id=1, source_target_pairs={{0,2},{1,3},{2,0},{3,1},{4,6},{5,7},{6,4},{7,5},{8,10},{9,11},{10,... | collective-permute-start | bytes 3342344 | tf_op jit(solution)/shard_map/p1x/ppermute | solution.py:47
  13.1 26.0 %collective-permute-start.1 = (bf16[136,4096]{1,0:T(8,128)(2,1)S(1)}, bf16[136,4096]{1,0:T(8,128)(2,1)S(1)}, u32[]{:S(2)}, u32[]{:S(2)}) collective-permute-start(bf16[136,4096]{1,0:T(8,128)(2,1)S(1)} %pad_maximum_fusion.m0.b0), channel_id=1, source_target_pairs={{0,3},{1,0},{2,1},{3,2},{4,7},{5,4},{6,5},{7,6},{8,11},{9,8},{10,9... | collective-permute-start | bytes 3342344 | tf_op jit(solution)/shard_map/p1x/ppermute | solution.py:47
  14.2 24.9 %collective-permute-start = (bf16[136,4096]{1,0:T(8,128)(2,1)S(1)}, bf16[136,4096]{1,0:T(8,128)(2,1)}, u32[]{:S(2)}, u32[]{:S(2)}) collective-permute-start(bf16[136,4096]{1,0:T(8,128)(2,1)S(1)} %pad_maximum_fusion.m0.b0), channel_id=1, source_target_pairs={{0,1},{1,2},{2,3},{3,0},{4,5},{5,6},{6,7},{7,4},{8,9},{9,10},{10,1... | collective-permute-start | bytes 3342344 | tf_op jit(solution)/shard_map/p1x/ppermute | solution.py:47
  27.1 17.1 %copy-start.4 = (bf16[136,4096]{1,0:T(8,128)(2,1)}, bf16[136,4096]{1,0:T(8,128)(2,1)S(1)}, u32[]{:S(2)}) copy-start(bf16[136,4096]{1,0:T(8,128)(2,1)S(1)} %collective-permute-done.2.m3.b3) | copy-start | bytes 3342340
  39.1 5.0 %copy-start.5 = (bf16[136,4096]{1,0:T(8,128)(2,1)}, bf16[136,4096]{1,0:T(8,128)(2,1)S(1)}, u32[]{:S(2)}) copy-start(bf16[136,4096]{1,0:T(8,128)(2,1)S(1)} %collective-permute-done.1.m2.b2) | copy-start | bytes 3342340
  39.2 18.1 %collective-permute-start.8 = (bf16[128,4096]{1,0:T(8,128)(2,1)}, bf16[128,4096]{1,0:T(8,128)(2,1)}, u32[]{:S(2)}, u32[]{:S(2)}) collective-permute-start(bf16[128,4096]{1,0:T(8,128)(2,1)} %b0), channel_id=1, source_target_pairs={{0,2},{1,3},{2,0},{3,1},{4,6},{5,7},{6,4},{7,5},{8,10},{9,11},{10,... | collective-permute-start | bytes 3145736 | tf_op jit(solution)/shard_map/p1g/ppermute | solution.py:47
  42.1 35.3 %collective-permute-start.7 = (bf16[128,4096]{1,0:T(8,128)(2,1)}, bf16[128,4096]{1,0:T(8,128)(2,1)}, u32[]{:S(2)}, u32[]{:S(2)}) collective-permute-start(bf16[128,4096]{1,0:T(8,128)(2,1)} %b0), channel_id=1, source_target_pairs={{0,3},{1,0},{2,1},{3,2},{4,7},{5,4},{6,5},{7,6},{8,11},{9,8},{10,9... | collective-permute-start | bytes 3145736 | tf_op jit(solution)/shard_map/p1g/ppermute | solution.py:47
  43.4 34.4 %collective-permute-start.6 = (bf16[128,4096]{1,0:T(8,128)(2,1)}, bf16[128,4096]{1,0:T(8,128)(2,1)}, u32[]{:S(2)}, u32[]{:S(2)}) collective-permute-start(bf16[128,4096]{1,0:T(8,128)(2,1)} %b0), channel_id=1, source_target_pairs={{0,1},{1,2},{2,3},{3,0},{4,5},{5,6},{6,7},{7,4},{8,9},{9,10},{10,1... | collective-permute-start | bytes 3145736 | tf_op jit(solution)/shard_map/p1g/ppermute | solution.py:47
  54.0 36.6 %collective-permute-start.3 = (bf16[4,72,4096]{2,1,0:T(8,128)(2,1)}, bf16[4,72,4096]{2,1,0:T(8,128)(2,1)}, u32[]{:S(2)}, u32[]{:S(2)}) collective-permute-start(bf16[4,72,4096]{2,1,0:T(8,128)(2,1)} %get-tuple-element.41), channel_id=1, source_target_pairs={{0,4},{1,5},{2,6},{3,7},{4,8},{5,9},{6,10},{7,11},{8,12},{9,13},{1... | collective-permute-start | bytes 7077896 | tf_op jit(solution)/shard_map/p2x/ppermute | solution.py:47
  55.6 35.0 %collective-permute-start.4 = (bf16[4,72,4096]{2,1,0:T(8,128)(2,1)}, bf16[4,72,4096]{2,1,0:T(8,128)(2,1)}, u32[]{:S(2)}, u32[]{:S(2)}) collective-permute-start(bf16[4,72,4096]{2,1,0:T(8,128)(2,1)} %get-tuple-element.42), channel_id=1, source_target_pairs={{0,12},{1,13},{2,14},{3,15},{4,0},{5,1},{6,2},{7,3},{8,4},{9,5},{1... | collective-permute-start | bytes 7077896 | tf_op jit(solution)/shard_map/p2x/ppermute | solution.py:47
  57.3 58.8 %collective-permute-start.5 = (bf16[4,72,4096]{2,1,0:T(8,128)(2,1)}, bf16[4,72,4096]{2,1,0:T(8,128)(2,1)}, u32[]{:S(2)}, u32[]{:S(2)}) collective-permute-start(bf16[4,72,4096]{2,1,0:T(8,128)(2,1)} %get-tuple-element.43), channel_id=1, source_target_pairs={{0,8},{1,9},{2,10},{3,11},{4,12},{5,13},{6,14},{7,15},{8,0},{9,1},... | collective-permute-start | bytes 7077896 | tf_op jit(solution)/shard_map/p2x/ppermute | solution.py:47
  85.5 55.7 %collective-permute-start.9 = (bf16[4,72,4096]{2,1,0:T(8,128)(2,1)}, bf16[4,72,4096]{2,1,0:T(8,128)(2,1)S(1)}, u32[]{:S(2)}, u32[]{:S(2)}) collective-permute-start(bf16[4,72,4096]{2,1,0:T(8,128)(2,1)} %get-tuple-element.46), channel_id=1, source_target_pairs={{0,4},{1,5},{2,6},{3,7},{4,8},{5,9},{6,10},{7,11},{8,12},{9,13},{1... | collective-permute-start | bytes 7077896 | tf_op jit(solution)/shard_map/p2g/ppermute | solution.py:47
  88.4 52.8 %collective-permute-start.10 = (bf16[4,72,4096]{2,1,0:T(8,128)(2,1)}, bf16[4,72,4096]{2,1,0:T(8,128)(2,1)S(1)}, u32[]{:S(2)}, u32[]{:S(2)}) collective-permute-start(bf16[4,72,4096]{2,1,0:T(8,128)(2,1)} %get-tuple-element.47), channel_id=1, source_target_pairs={{0,12},{1,13},{2,14},{3,15},{4,0},{5,1},{6,2},{7,3},{8,4},{9,5},{1... | collective-permute-start | bytes 7077896 | tf_op jit(solution)/shard_map/p2g/ppermute | solution.py:47
  141.2 4.3 %copy-start.2 = (bf16[4,72,4096]{2,1,0:T(8,128)(2,1)}, bf16[4,72,4096]{2,1,0:T(8,128)(2,1)S(1)}, u32[]{:S(2)}) copy-start(bf16[4,72,4096]{2,1,0:T(8,128)(2,1)S(1)} %collective-permute-done.9) | copy-start | bytes 7077892
  142.6 30.7 %collective-permute-start.11 = (bf16[4,72,4096]{2,1,0:T(8,128)(2,1)}, bf16[4,72,4096]{2,1,0:T(8,128)(2,1)S(1)}, u32[]{:S(2)}, u32[]{:S(2)}) collective-permute-start(bf16[4,72,4096]{2,1,0:T(8,128)(2,1)} %get-tuple-element.51), channel_id=1, source_target_pairs={{0,8},{1,9},{2,10},{3,11},{4,12},{5,13},{6,14},{7,15},{8,0},{9,1},... | collective-permute-start | bytes 7077896 | tf_op jit(solution)/shard_map/p2g2/ppermute | solution.py:47
  165.8 33.8 %collective-permute-start.13 = (bf16[4,72,4096]{2,1,0:T(8,128)(2,1)}, bf16[4,72,4096]{2,1,0:T(8,128)(2,1)}, u32[]{:S(2)}, u32[]{:S(2)}) collective-permute-start(bf16[4,72,4096]{2,1,0:T(8,128)(2,1)} %bitcast.43), channel_id=1, source_target_pairs={{0,4},{1,5},{2,6},{3,7},{4,8},{5,9},{6,10},{7,11},{8,12},{9,13},{1... | collective-permute-start | bytes 7077896 | tf_op jit(solution)/shard_map/r2/ppermute | solution.py:47
  166.5 33.1 %collective-permute-start.12 = (bf16[4,72,4096]{2,1,0:T(8,128)(2,1)}, bf16[4,72,4096]{2,1,0:T(8,128)(2,1)}, u32[]{:S(2)}, u32[]{:S(2)}) collective-permute-start(bf16[4,72,4096]{2,1,0:T(8,128)(2,1)} %bitcast.42), channel_id=1, source_target_pairs={{0,12},{1,13},{2,14},{3,15},{4,0},{5,1},{6,2},{7,3},{8,4},{9,5},{1... | collective-permute-start | bytes 7077896 | tf_op jit(solution)/shard_map/r2/ppermute | solution.py:47
  187.2 90.5 %reduce-scatter.5.cloned.1.call-start = ((), (), s32[]{:S(2)}) async-start(), calls=%async_computation.3 | async-start | bytes 7077888 | tf_op jit(solution)/shard_map/reduce_scatter | solution.py:371
  199.6 30.7 %collective-permute-start.14 = (bf16[4,72,4096]{2,1,0:T(8,128)(2,1)}, bf16[4,72,4096]{2,1,0:T(8,128)(2,1)}, u32[]{:S(2)}, u32[]{:S(2)}) collective-permute-start(bf16[4,72,4096]{2,1,0:T(8,128)(2,1)} %bitcast.44), channel_id=1, source_target_pairs={{0,8},{1,9},{2,10},{3,11},{4,12},{5,13},{6,14},{7,15},{8,0},{9,1},... | collective-permute-start | bytes 7077896 | tf_op jit(solution)/shard_map/r2/ppermute | solution.py:47
  241.3 26.6 %collective-permute-start.15 = (bf16[128,4096]{1,0:T(8,128)(2,1)}, bf16[128,4096]{1,0:T(8,128)(2,1)S(1)}, u32[]{:S(2)}, u32[]{:S(2)}) collective-permute-start(bf16[128,4096]{1,0:T(8,128)(2,1)} %get-tuple-element.64), channel_id=1, source_target_pairs={{0,3},{1,0},{2,1},{3,2},{4,7},{5,4},{6,5},{7,6},{8,11},{9,8},{10,9... | collective-permute-start | bytes 3145736 | tf_op jit(solution)/shard_map/r1/ppermute | solution.py:47
  244.0 27.5 %collective-permute-start.16 = (bf16[128,4096]{1,0:T(8,128)(2,1)}, bf16[128,4096]{1,0:T(8,128)(2,1)S(1)}, u32[]{:S(2)}, u32[]{:S(2)}) collective-permute-start(bf16[128,4096]{1,0:T(8,128)(2,1)} %get-tuple-element.65), channel_id=1, source_target_pairs={{0,1},{1,2},{2,3},{3,0},{4,5},{5,6},{6,7},{7,4},{8,9},{9,10},{10,1... | collective-permute-start | bytes 3145736 | tf_op jit(solution)/shard_map/r1/ppermute | solution.py:47
  244.0 27.5 %collective-permute-start.17 = (bf16[128,4096]{1,0:T(8,128)(2,1)}, bf16[128,4096]{1,0:T(8,128)(2,1)S(1)}, u32[]{:S(2)}, u32[]{:S(2)}) collective-permute-start(bf16[128,4096]{1,0:T(8,128)(2,1)} %get-tuple-element.66), channel_id=1, source_target_pairs={{0,2},{1,3},{2,0},{3,1},{4,6},{5,7},{6,4},{7,5},{8,10},{9,11},{10,... | collective-permute-start | bytes 3145736 | tf_op jit(solution)/shard_map/r1/ppermute | solution.py:47
  (6 other events, 11.8 us)
Sparse Core Ops, SparseCore 0:
  187.3 45.7 reduce-scatter.2
  235.5 42.1 reduce-scatter.4

commit v3 on v2

--- a/solution.py
+++ b/solution.py
@@ -26,7 +26,6 @@
 
 
 HEAVY = pl.CostEstimate(flops=30_000_000_000, bytes_accessed=1, transcendentals=0)
-LONGEST = pl.CostEstimate(flops=300_000_000_000, bytes_accessed=1, transcendentals=0)
 LIGHT = pl.CostEstimate(flops=1_000_000, bytes_accessed=1, transcendentals=0)
 PARAMS = pltpu.CompilerParams(vmem_limit_bytes=VMEM_LIMIT)
 
@@ -140,20 +139,21 @@
         out[...] = total.astype(jnp.bfloat16)
 
 
-def combine(put, returned):
-    width = returned[0].shape[2]
-    tile = TILE
+def combine(put, returned, last, half):
+    width = last.shape[2]
+    first = half * (width // TILE)
     return pl.pallas_call(
         combine_kernel,
         out_shape=(jax.ShapeDtypeStruct((128, width), jnp.bfloat16),) * SIDE,
-        grid=(width // tile,),
+        grid=(width // TILE,),
         in_specs=[pl.BlockSpec((SIDE, SIDE, 128, SLOTS), lambda c: (0, 0, 0, 0))]
-        + [pl.BlockSpec((SIDE, SLOTS, tile), lambda c: (0, 0, c))] * SIDE,
-        out_specs=(pl.BlockSpec((128, tile), lambda c: (0, c)),) * SIDE,
+        + [pl.BlockSpec((SIDE, SLOTS, TILE), lambda c: (0, 0, c + first))] * 3
+        + [pl.BlockSpec((SIDE, SLOTS, TILE), lambda c: (0, 0, c))],
+        out_specs=(pl.BlockSpec((128, TILE), lambda c: (0, c)),) * SIDE,
         compiler_params=PARAMS,
         cost_estimate=LIGHT,
         name="combine",
-    )(put, *returned)
+    )(put, *returned, last)
 
 
 def dot(a, b, dims=(((1,), (0,)), ((), ()))):
@@ -226,17 +226,36 @@
     @pl.when(step >= half)
     def _():
         out = dot(grad[...], up[...], COLS_LAST).astype(jnp.bfloat16)
-        for i in range(n):
-            rows[i][...] = out[i * ROWS : (i + 1) * ROWS, :]
+        if n > 1:
+            for i in range(n):
+                rows[i][...] = out[i * ROWS : (i + 1) * ROWS, :]
+            return
+        left = step < half + half // 2
+
+        @pl.when(left)
+        def _():
+            rows[0][...] = out
+
+        @pl.when(jnp.logical_not(left))
+        def _():
+            rows[1][...] = out
 
 
 def expert_back(gs, pre, place, down, up):
     n, (width, hidden) = len(gs), up.shape
     tiles = width // TILE
+    middle = tiles // 2
+    row_shapes = (jax.ShapeDtypeStruct((ROWS, width), jnp.bfloat16),) * n
+    row_specs = (pl.BlockSpec((ROWS, TILE), lambda c: (0, jnp.maximum(c - tiles, 0))),) * n
+    if n == 1:
+        row_shapes = (jax.ShapeDtypeStruct((ROWS, width // 2), jnp.bfloat16),) * 2
+        row_specs = (
+            pl.BlockSpec((ROWS, TILE), lambda c: (0, jnp.clip(c - tiles, 0, middle - 1))),
+            pl.BlockSpec((ROWS, TILE), lambda c: (0, jnp.maximum(c - tiles - middle, 0))),
+        )
     out = pl.pallas_call(
         functools.partial(back_kernel, n),
-        out_shape=(jax.ShapeDtypeStruct((n * ROWS, hidden), jnp.bfloat16),)
-        + (jax.ShapeDtypeStruct((ROWS, width), jnp.bfloat16),) * n,
+        out_shape=(jax.ShapeDtypeStruct((n * ROWS, hidden), jnp.bfloat16),) + row_shapes,
         grid=(2 * tiles,),
         in_specs=[pl.BlockSpec((ROWS, TILE), lambda c: (0, jnp.minimum(c, tiles - 1)))] * n
         + [
@@ -244,8 +263,7 @@
             pl.BlockSpec((hidden, TILE), lambda c: (0, jnp.minimum(c, tiles - 1))),
             pl.BlockSpec((TILE, hidden), lambda c: (jnp.maximum(c - tiles, 0), 0)),
         ],
-        out_specs=(pl.BlockSpec((n * ROWS, hidden), lambda c: (0, 0)),)
-        + (pl.BlockSpec((ROWS, TILE), lambda c: (0, jnp.maximum(c - tiles, 0))),) * n,
+        out_specs=(pl.BlockSpec((n * ROWS, hidden), lambda c: (0, 0)),) + row_specs,
         scratch_shapes=[pltpu.VMEM((n * ROWS, hidden), jnp.float32)],
         compiler_params=PARAMS,
         cost_estimate=cost(2 * n * ROWS, width, hidden) if n > 1 else LIGHT,
@@ -254,64 +272,119 @@
     return out[0], list(out[1:])
 
 
+STRIP = 128
+
+
 def up_kernel(x0, x1, x2, x3, grad, grad_last, out):
     total = dot(stacked((x0, x1, x2, x3)), stacked((grad, grad_last)), ROWS_FIRST)
-    out[...] = total.astype(jnp.bfloat16)
+    total = total.astype(jnp.bfloat16)
+    blocks = out.shape[0]
+    rows = total.shape[0] // blocks
+    for d in range(blocks):
+        for k in range(total.shape[1] // STRIP):
+            strip = total[d * rows : (d + 1) * rows, k * STRIP : (k + 1) * STRIP]
+            out[d, 0, k * rows : (k + 1) * rows, :] = strip
 
 
 def up_partial(xs, grads):
     width, hidden = xs[0].shape[1], grads[0].shape[1]
+    strips = width // 8 * hidden // STRIP
+    blocks = TILE * 8 // width
     return pl.pallas_call(
         up_kernel,
-        out_shape=jax.ShapeDtypeStruct((width, hidden), jnp.bfloat16),
+        out_shape=jax.ShapeDtypeStruct((8, 2, strips, STRIP), jnp.bfloat16),
         grid=(width // TILE,),
         in_specs=[pl.BlockSpec((ROWS, TILE), lambda c: (0, c))] * SIDE
         + [pl.BlockSpec(g.shape, lambda c: (0, 0)) for g in grads],
-        out_specs=pl.BlockSpec((TILE, hidden), lambda c: (c, 0)),
-        compiler_params=PARAMS,
-        cost_estimate=LONGEST,
+        out_specs=pl.BlockSpec((blocks, 1, strips, STRIP), lambda c: (c, 0, 0, 0)),
+        compiler_params=PARAMS,
+        cost_estimate=LIGHT,
         name="up_partial",
     )(*xs, *grads)
 
 
-def down_kernel(act, g0, g1, g2, g3, out):
-    out[...] = dot(act[...], stacked((g0, g1, g2, g3))).astype(jnp.bfloat16)
-
-
-def down_partial(act, gs):
+def down_kernel(act, g0, g1, g2, g3, shared, out):
+    total = dot(act[...], stacked((g0, g1, g2, g3))).astype(jnp.bfloat16)
+    rows = total.shape[0] // 8
+    for d in range(8):
+        for k in range(TILE // STRIP):
+            strip = total[d * rows : (d + 1) * rows, k * STRIP : (k + 1) * STRIP]
+            out[d, 0, k * rows : (k + 1) * rows, :] = strip
+
+
+def down_partial(act, gs, shared):
     hidden, rows = act.shape
     width = gs[0].shape[1]
+    tall = hidden // 8 * TILE // STRIP
     return pl.pallas_call(
         down_kernel,
-        out_shape=jax.ShapeDtypeStruct((hidden, width), jnp.bfloat16),
+        out_shape=jax.ShapeDtypeStruct(shared.shape, jnp.bfloat16),
         grid=(width // TILE,),
         in_specs=[pl.BlockSpec((hidden, rows), lambda c: (0, 0))]
-        + [pl.BlockSpec((ROWS, TILE), lambda c: (0, c))] * SIDE,
-        out_specs=pl.BlockSpec((hidden, TILE), lambda c: (0, c)),
+        + [pl.BlockSpec((ROWS, TILE), lambda c: (0, c))] * SIDE
+        + [pl.BlockSpec(memory_space=pl.ANY)],
+        out_specs=pl.BlockSpec((8, 1, tall, STRIP), lambda c: (0, 1, c, 0)),
+        input_output_aliases={5: 0},
         compiler_params=PARAMS,
         cost_estimate=LIGHT,
         name="down_partial",
-    )(act, *gs)
-
-
-def parts_kernel(p0, p1, p2, p3, out):
-    total = sum(p[...].astype(jnp.float32) for p in (p0, p1, p2, p3))
-    out[...] = total.astype(jnp.bfloat16)
-
-
-def sum_parts(parts):
-    rows, width = parts[0].shape
-    spec = pl.BlockSpec((rows // SIDE, width), lambda c: (c, 0))
+    )(act, *gs, shared)
+
+
+def widen_kernel(share, up, down):
+    for half, out in ((0, up), (1, down)):
+        rows = out.shape[1]
+        for k in range(out.shape[2] // STRIP):
+            strip = share[half, k * rows : (k + 1) * rows, :]
+            out[0, :, k * STRIP : (k + 1) * STRIP] = strip.astype(jnp.float32)
+
+
+def widen(share, up_shape, down_shape):
+    return pl.pallas_call(
+        widen_kernel,
+        out_shape=(
+            jax.ShapeDtypeStruct(up_shape, jnp.float32),
+            jax.ShapeDtypeStruct(down_shape, jnp.float32),
+        ),
+        grid=(1,),
+        in_specs=[pl.BlockSpec(share.shape, lambda c: (0, 0, 0))],
+        out_specs=(
+            pl.BlockSpec(up_shape, lambda c: (0, 0, 0)),
+            pl.BlockSpec(down_shape, lambda c: (0, 0, 0)),
+        ),
+        compiler_params=PARAMS,
+        cost_estimate=LIGHT,
+        name="widen",
+    )(share)
+
+
+def parts_kernel(*refs):
+    left, right, out = refs[:SIDE], refs[SIDE:-1], refs[-1]
+    in_left = pl.program_id(0) < pl.num_programs(0) // 2
+
+    @pl.when(in_left)
+    def _():
+        out[...] = sum(p[...].astype(jnp.float32) for p in left).astype(jnp.bfloat16)
+
+    @pl.when(jnp.logical_not(in_left))
+    def _():
+        out[...] = sum(p[...].astype(jnp.float32) for p in right).astype(jnp.bfloat16)
+
+
+def sum_parts(left, right):
+    rows, width = left[0].shape
+    tiles = width // TILE
     return pl.pallas_call(
         parts_kernel,
-        out_shape=jax.ShapeDtypeStruct((rows, width), jnp.bfloat16),
-        grid=(SIDE,),
-        in_specs=[spec] * SIDE,
-        out_specs=spec,
+        out_shape=jax.ShapeDtypeStruct((rows, 2 * width), jnp.bfloat16),
+        grid=(2 * tiles,),
+        in_specs=[pl.BlockSpec((rows, TILE), lambda c: (0, jnp.minimum(c, tiles - 1)))] * SIDE
+        + [pl.BlockSpec((rows, TILE), lambda c: (0, jnp.maximum(c - tiles, 0)))] * SIDE,
+        out_specs=pl.BlockSpec((rows, TILE), lambda c: (0, c)),
         compiler_params=PARAMS,
         cost_estimate=LIGHT,
         name="sum_parts",
-    )(*parts)
+    )(*left, *right)
 
 
 def after(value, *earlier):
@@ -358,24 +431,31 @@
         returned = [send(r.reshape(SIDE, SLOTS, width), False, -o) for r, o in zip(rows, OFFSETS)]
 
     last = after(last, *rows)
-    down_part = down_partial(act, [*rg, last])
-    down_grad = lax.psum_scatter(down_part, "dp", scatter_dimension=0, tiled=True)
-    last = after(last, down_part)
-    grad_last, rows_last = expert_back([last], pre, 3, down_matrix, up_matrix)
-    with jax.named_scope("r2"):
-        rows_last = after(rows_last[0], *returned).reshape(SIDE, SLOTS, width)
-        returned.append(send(rows_last, False, -OFFSETS[3]))
-    grad_last = after(grad_last, *returned[:3])
-    up_part = up_partial(rx, [grad, grad_last])
-    up_done, up_part = up_part, after(up_part, down_grad, returned[3])
-    up_grad = lax.psum_scatter(up_part, "dp", scatter_dimension=0, tiled=True)
-
-    parts = combine(after(put, up_done), returned)
-    with jax.named_scope("r1"):
-        parts = [send(p, True, -o) for p, o in zip(parts, OFFSETS)]
-    token_grad = sum_parts(parts)
-    token_grad, up_grad, down_grad = lax.optimization_barrier((token_grad, up_grad, down_grad))
-    return token_grad, up_grad.astype(jnp.float32)[None], down_grad.astype(jnp.float32)[None]
+    grad_last, (left, right) = expert_back([last], pre, 3, down_matrix, up_matrix)
+    shared = up_partial(rx, [grad, grad_last])
+    shared = after(shared, act, *returned)
+    shared = down_partial(act, [*rg, last], shared)
+    share = lax.psum_scatter(
+        shared.reshape(-1, STRIP), "dp", scatter_dimension=0, tiled=True
+    ).reshape(2, -1, STRIP)
+
+    with jax.named_scope("r2l"):
+        left = send(after(left, *returned).reshape(SIDE, SLOTS, -1), False, -OFFSETS[3])
+    with jax.named_scope("r2r"):
+        right = send(after(right, left).reshape(SIDE, SLOTS, -1), False, -OFFSETS[3])
+    put = after(put, shared)
+    with jax.named_scope("r1l"):
+        parts = combine(put, returned, left, 0)
+        left_parts = [send(p, True, -o) for p, o in zip(parts, OFFSETS)]
+    with jax.named_scope("r1r"):
+        parts = combine(put, returned, right, 1)
+        right_parts = [send(p, True, -o) for p, o in zip(parts, OFFSETS)]
+    token_grad = sum_parts(left_parts, right_parts)
+    token_grad, share = lax.optimization_barrier((token_grad, share))
+    up_grad, down_grad = widen(
+        share, (1, width // 8, up_matrix.shape[1]), (1, down_matrix.shape[0] // 8, width)
+    )
+    return token_grad, up_grad, down_grad
 
 
 def solution(mesh):

time: 289 us -> 298 us (1.031)
  starting transfers between devices: 34.6 us -> 44.1 us
  Pallas kernels: 103 us -> 110 us
  waiting for transfers between devices: 125 us -> 121 us
  other arithmetic: 7.59 us -> 3.88 us
    ppermute x18 -> x22, starting transfers between devices: 34.6 us -> 44.1 us  [send(): lax.ppermute(value, BOTH, ring(first, shift))]
    pallas_call x3 -> x4, Pallas kernels: 29.4 us -> 33.7 us  [the longest x1 13.3 us: down_partial(): pl.pallas_call(down_kernel, out_shape=jax.ShapeDtypeStruct(shared.shape,...]
    broadcast_in_dim x2 -> x0, other arithmetic: 3.66 us -> none  [the longest x1 2.38 us: body(): up_grad.astype(jnp.float32)[None]]
    ppermute x18 -> x22, waiting for transfers between devices: 122 us -> 118 us  [send(): lax.ppermute(value, BOTH, ring(first, shift))]
    pallas_call x1 -> x2, Pallas kernels: 8.28 us -> 10.7 us  [combine(): pl.pallas_call(combine_kernel, out_shape=(jax.ShapeDtypeStruct((128, widt...]
  transfers between devices with their start and end apart: 20 -> 23, of which waited for: 13 -> 13; matrix products, arithmetic and copies ran while one was open for 0% -> 0% of each run, Pallas kernels for 36% -> 31%
where the time goes in v3:
time: 298 us; the launch traced here: 297 us
  waiting for transfers between devices  121 us (41%)
  Pallas kernels  110 us (37%)
  starting transfers between devices  44.1 us (15%)
  between operations  14.1 us (5%)
  local copies, waits for them, and re-layouts  4.62 us (2%)
  other arithmetic  3.88 us (1%)
    ppermute x22, waiting for transfers between devices, send(): lax.ppermute(value, BOTH, ring(first, shift))  118 us
    ppermute x22, starting transfers between devices, send(): lax.ppermute(value, BOTH, ring(first, shift))  44.1 us
    pallas_call x2, Pallas kernels, expert_back(): pl.pallas_call(functools.partial(back_kernel, n), out_shape=(jax.ShapeDty...  32.9 us
    pallas_call x2, Pallas kernels, select(): pl.pallas_call(functools.partial(select_kernel, scaled), out_shape=(jax.S...  15.5 us
    pallas_call x1, Pallas kernels, expert_pre(): pl.pallas_call(pre_kernel, out_shape=(jax.ShapeDtypeStruct((WIDE + ROWS,...  14.5 us
    pallas_call x1, Pallas kernels, down_partial(): pl.pallas_call(down_kernel, out_shape=jax.ShapeDtypeStruct(shared.shape,...  13.3 us
    pallas_call x1, Pallas kernels, up_partial(): pl.pallas_call(up_kernel, out_shape=jax.ShapeDtypeStruct((8, 2, strips, S...  12.8 us
    pallas_call x2, Pallas kernels, combine(): pl.pallas_call(combine_kernel, out_shape=(jax.ShapeDtypeStruct((128, widt...  10.7 us
  transfers between devices with their start and end apart: 23, of which 13 were waited for; matrix products, arithmetic and copies ran while one was open for 0% of the time, Pallas kernels for 31%

profile of v3, /device:TPU:0, one launch (start us, length us, event | category | flops | bytes accessed | tf_op | source)
XLA Modules:
  0.0 297.0 jit_solution(4406248220099413159)
XLA Ops:
  9.9 3.2 %collective-permute-start.2 = (bf16[136,4096]{1,0:T(8,128)(2,1)S(1)}, bf16[136,4096]{1,0:T(8,128)(2,1)S(1)}, u32[]{:S(2)}, u32[]{:S(2)}) collective-permute-start(bf16[136,4096]{1,0:T(8,128)(2,1)S(1)} %pad_maximum_fusion.m0.b0), channel_id=1, source_target_pairs={{0,2},{1,3},{2,0},{3,1},{4,6},{5,7},{6,4},{7,5},{8,10},{9,11},{10,... | collective-permute-start | bytes 3342344 | tf_op jit(solution)/shard_map/p1x/ppermute | solution.py:46
  16.3 10.8 %collective-permute-done.2.m3.b3 = bf16[136,4096]{1,0:T(8,128)(2,1)S(1)} collective-permute-done((bf16[136,4096]{1,0:T(8,128)(2,1)S(1)}, bf16[136,4096]{1,0:T(8,128)(2,1)S(1)}, u32[]{:S(2)}, u32[]{:S(2)}) %collective-permute-start.2) | collective-permute-done | bytes 1114144 | tf_op jit(solution)/shard_map/p1x/ppermute | solution.py:46
  27.1 12.0 %collective-permute-done.1.m2.b2 = bf16[136,4096]{1,0:T(8,128)(2,1)S(1)} collective-permute-done((bf16[136,4096]{1,0:T(8,128)(2,1)S(1)}, bf16[136,4096]{1,0:T(8,128)(2,1)S(1)}, u32[]{:S(2)}, u32[]{:S(2)}) %collective-permute-start.1) | collective-permute-done | bytes 1114144 | tf_op jit(solution)/shard_map/p1x/ppermute | solution.py:46
  46.3 7.7 %select.22 = (bf16[4,72,4096]{2,1,0:T(8,128)(2,1)}, bf16[4,72,4096]{2,1,0:T(8,128)(2,1)}, bf16[4,72,4096]{2,1,0:T(8,128)(2,1)}, bf16[4,72,4096]{2,1,0:T(8,128)(2,1)}) custom-call(bf16[4,288,128]{2,1,0:T(8,128)(2,1)} %get-tuple-element.43.pick_ref, f32[4,288,128]{2,1,0:T(8,128)} %get-tuple-element.44.weight_ref, bf16[136,4096]{1,0:T(8,128)(2,1)} %copy-done.2, ...), custom_call_target="tpu_custom_call" | custom-call | flops 30000001024 | bytes 1 | tf_op jit(solution)/shard_map/select/pallas_call | solution.py:117
  57.3 3.5 %collective-permute-start.5 = (bf16[4,72,4096]{2,1,0:T(8,128)(2,1)}, bf16[4,72,4096]{2,1,0:T(8,128)(2,1)}, u32[]{:S(2)}, u32[]{:S(2)}) collective-permute-start(bf16[4,72,4096]{2,1,0:T(8,128)(2,1)} %get-tuple-element.48), channel_id=1, source_target_pairs={{0,8},{1,9},{2,10},{3,11},{4,12},{5,13},{6,14},{7,15},{8,0},{9,1},... | collective-permute-start | bytes 7077896 | tf_op jit(solution)/shard_map/p2x/ppermute | solution.py:46
  60.8 16.7 %collective-permute-done.7.b2 = bf16[128,4096]{1,0:T(8,128)(2,1)} collective-permute-done((bf16[128,4096]{1,0:T(8,128)(2,1)}, bf16[128,4096]{1,0:T(8,128)(2,1)}, u32[]{:S(2)}, u32[]{:S(2)}) %collective-permute-start.7) | collective-permute-done | bytes 1048608 | tf_op jit(solution)/shard_map/p1g/ppermute | solution.py:46
  77.8 7.8 %select_scaled.1 = (bf16[4,72,4096]{2,1,0:T(8,128)(2,1)}, bf16[4,72,4096]{2,1,0:T(8,128)(2,1)}, bf16[4,72,4096]{2,1,0:T(8,128)(2,1)}, bf16[4,72,4096]{2,1,0:T(8,128)(2,1)}) custom-call(bf16[4,288,128]{2,1,0:T(8,128)(2,1)} %get-tuple-element.43.pick_ref, f32[4,288,128]{2,1,0:T(8,128)} %get-tuple-element.44.weight_ref, bf16[128,4096]{1,0:T(8,128)(2,1)} %b0, ...), custom_call_target="tpu_custom_call" | custom-call | flops 30000001024 | bytes 1 | tf_op jit(solution)/shard_map/select_scaled/pallas_call | solution.py:117
  90.6 25.5 %collective-permute-done.5 = bf16[4,72,4096]{2,1,0:T(8,128)(2,1)} collective-permute-done((bf16[4,72,4096]{2,1,0:T(8,128)(2,1)}, bf16[4,72,4096]{2,1,0:T(8,128)(2,1)}, u32[]{:S(2)}, u32[]{:S(2)}) %collective-permute-start.5) | collective-permute-done | bytes 2359328 | tf_op jit(solution)/shard_map/p2x/ppermute | solution.py:46
  116.1 14.5 %expert_pre.1 = (f32[1152,768]{1,0:T(8,128)}, bf16[768,1152]{1,0:T(8,128)(2,1)}) custom-call(bf16[288,4096]{1,0:T(8,128)(2,1)} %bitcast.35, bf16[288,4096]{1,0:T(8,128)(2,1)} %bitcast.37, bf16[288,4096]{1,0:T(8,128)(2,1)} %bitcast.39, bf16[288,4096]{1,0:T(8,128)(2,1)} %bitcast.7.refs_3_.x3, bf16[4096,768]{1,0:T(8,128)(2,1)} %bitcast.30), custom_call_target="tpu_custom_call" | custom-call | flops 7247757312 | bytes 17498112 | tf_op jit(solution)/shard_map/expert_pre/pallas_call | solution.py:188
  130.6 10.6 %collective-permute-done.9 = bf16[4,72,4096]{2,1,0:T(8,128)(2,1)} collective-permute-done((bf16[4,72,4096]{2,1,0:T(8,128)(2,1)}, bf16[4,72,4096]{2,1,0:T(8,128)(2,1)}, u32[]{:S(2)}, u32[]{:S(2)}) %collective-permute-start.9) | collective-permute-done | bytes 2359328 | tf_op jit(solution)/shard_map/p2g/ppermute | solution.py:46
  144.1 20.4 %expert_back.2 = (bf16[864,768]{1,0:T(8,128)(2,1)}, bf16[288,4096]{1,0:T(8,128)(2,1)}, bf16[288,4096]{1,0:T(8,128)(2,1)}, bf16[288,4096]{1,0:T(8,128)(2,1)}) custom-call(bf16[288,4096]{1,0:T(8,128)(2,1)} %bitcast.41, bf16[288,4096]{1,0:T(8,128)(2,1)} %bitcast.10.refs_1_.g1, bf16[288,4096]{1,0:T(8,128)(2,1)} %bitcast.11.refs_2_.g2, ...), custom_call_target="tpu_custom_call" | custom-call | flops 10871635968 | bytes 23101440 | tf_op jit(solution)/shard_map/expert_back/pallas_call | solution.py:256
  167.7 4.2 %collective-permute-done.11 = bf16[4,72,4096]{2,1,0:T(8,128)(2,1)S(1)} collective-permute-done((bf16[4,72,4096]{2,1,0:T(8,128)(2,1)}, bf16[4,72,4096]{2,1,0:T(8,128)(2,1)S(1)}, u32[]{:S(2)}, u32[]{:S(2)}) %collective-permute-start.11) | collective-permute-done | bytes 2359328 | tf_op jit(solution)/shard_map/p2g2/ppermute | solution.py:46
  173.3 12.5 %expert_back.3 = (bf16[288,768]{1,0:T(8,128)(2,1)}, bf16[288,2048]{1,0:T(8,128)(2,1)}, bf16[288,2048]{1,0:T(8,128)(2,1)}) custom-call(bf16[288,4096]{1,0:T(8,128)(2,1)} %bitcast.26, f32[1152,768]{1,0:T(8,128)} %get-tuple-element.55.refs_3_.refs_1_, bf16[768,4096]{1,0:T(8,128)(2,1)} %bitcast.34, bf16[4096,768]{1,0:T(8,128)(2,1)} %bitcast.32), custom_call_target="tpu_custom_call" | custom-call | flops 1000000 | bytes 1 | tf_op jit(solution)/shard_map/expert_back/pallas_call | solution.py:256
  185.8 12.8 %up_partial.1.shared = bf16[8,2,3072,128]{3,2,1,0:T(8,128)(2,1)} custom-call(bf16[288,4096]{1,0:T(8,128)(2,1)} %bitcast.36, bf16[288,4096]{1,0:T(8,128)(2,1)} %bitcast.38, bf16[288,4096]{1,0:T(8,128)(2,1)} %bitcast.40, bf16[288,4096]{1,0:T(8,128)(2,1)} %bitcast.7.refs_3_.x3, bf16[864,768]{1,0:T(8,128)(2,1)} %get-tuple-element.61.grad, ...), custom_call_target="tpu_custom_call" | custom-call | flops 1000000 | bytes 1 | tf_op jit(solution)/shard_map/up_partial/pallas_call | solution.py:293
  198.6 13.3 %down_partial.1 = bf16[8,2,3072,128]{3,2,1,0:T(8,128)(2,1)} custom-call(bf16[768,1152]{1,0:T(8,128)(2,1)} %get-tuple-element.49.act, bf16[288,4096]{1,0:T(8,128)(2,1)} %bitcast.42, bf16[288,4096]{1,0:T(8,128)(2,1)} %bitcast.10.refs_1_.g1, bf16[288,4096]{1,0:T(8,128)(2,1)} %bitcast.11.refs_2_.g2, ...), custom_call_target="tpu_custom_call", output_to_operand_aliasing={{}: (5, {})} | custom-call | flops 1000000 | bytes 1 | tf_op jit(solution)/shard_map/down_partial/pallas_call | solution.py:319
  215.9 14.9 %collective-permute-done.14.r3 = bf16[4,72,2048]{2,1,0:T(8,128)(2,1)S(1)} collective-permute-done((bf16[4,72,2048]{2,1,0:T(8,128)(2,1)S(1)}, bf16[4,72,2048]{2,1,0:T(8,128)(2,1)S(1)}, u32[]{:S(2)}, u32[]{:S(2)}) %collective-permute-start.14) | collective-permute-done | bytes 1179680 | tf_op jit(solution)/shard_map/r2l/ppermute | solution.py:46
  233.6 5.5 %combine.2 = (bf16[128,2048]{1,0:T(8,128)(2,1)}, bf16[128,2048]{1,0:T(8,128)(2,1)}, bf16[128,2048]{1,0:T(8,128)(2,1)}, bf16[128,2048]{1,0:T(8,128)(2,1)}) custom-call(bf16[4,4,128,72]{3,2,1,0:T(8,128)(2,1)} %get-tuple-element.64.put_ref, bf16[4,72,4096]{2,1,0:T(8,128)(2,1)} %bitcast.28, bf16[4,72,4096]{2,1,0:T(8,128)(2,1)} %collective-permute-done.12.r1, ...), custom_call_target="tpu_custom_call" | custom-call | flops 1000000 | bytes 1 | tf_op jit(solution)/shard_map/r1l/combine/pallas_call | solution.py:145
  244.1 8.7 %collective-permute-done.18.r3 = bf16[4,72,2048]{2,1,0:T(8,128)(2,1)S(1)} collective-permute-done((bf16[4,72,2048]{2,1,0:T(8,128)(2,1)S(1)}, bf16[4,72,2048]{2,1,0:T(8,128)(2,1)S(1)}, u32[]{:S(2)}, u32[]{:S(2)}) %collective-permute-start.18) | collective-permute-done | bytes 1179680 | tf_op jit(solution)/shard_map/r2r/ppermute | solution.py:46
  253.8 5.3 %combine.3 = (bf16[128,2048]{1,0:T(8,128)(2,1)}, bf16[128,2048]{1,0:T(8,128)(2,1)}, bf16[128,2048]{1,0:T(8,128)(2,1)}, bf16[128,2048]{1,0:T(8,128)(2,1)}) custom-call(bf16[4,4,128,72]{3,2,1,0:T(8,128)(2,1)} %get-tuple-element.64.put_ref, bf16[4,72,4096]{2,1,0:T(8,128)(2,1)} %bitcast.29, bf16[4,72,4096]{2,1,0:T(8,128)(2,1)} %collective-permute-done.12.r1, ...), custom_call_target="tpu_custom_call" | custom-call | flops 1000000 | bytes 1 | tf_op jit(solution)/shard_map/r1r/combine/pallas_call | solution.py:145
  259.1 3.9 %collective-permute-start.19 = (bf16[128,2048]{1,0:T(8,128)(2,1)}, bf16[128,2048]{1,0:T(8,128)(2,1)S(1)}, u32[]{:S(2)}, u32[]{:S(2)}) collective-permute-start(bf16[128,2048]{1,0:T(8,128)(2,1)} %get-tuple-element.74), channel_id=1, source_target_pairs={{0,3},{1,0},{2,1},{3,2},{4,7},{5,4},{6,5},{7,6},{8,11},{9,8},{10,9... | collective-permute-start | bytes 1572872 | tf_op jit(solution)/shard_map/r1r/ppermute | solution.py:46
  265.9 9.8 %collective-permute-done.19.refs_5_ = bf16[128,2048]{1,0:T(8,128)(2,1)S(1)} collective-permute-done((bf16[128,2048]{1,0:T(8,128)(2,1)}, bf16[128,2048]{1,0:T(8,128)(2,1)S(1)}, u32[]{:S(2)}, u32[]{:S(2)}) %collective-permute-start.19) | collective-permute-done | bytes 524320 | tf_op jit(solution)/shard_map/r1r/ppermute | solution.py:46
  275.7 3.6 %collective-permute-done.20.refs_6_ = bf16[128,2048]{1,0:T(8,128)(2,1)S(1)} collective-permute-done((bf16[128,2048]{1,0:T(8,128)(2,1)}, bf16[128,2048]{1,0:T(8,128)(2,1)S(1)}, u32[]{:S(2)}, u32[]{:S(2)}) %collective-permute-start.20) | collective-permute-done | bytes 524320 | tf_op jit(solution)/shard_map/r1r/ppermute | solution.py:46
  280.2 4.5 %sum_parts.1 = bf16[128,4096]{1,0:T(8,128)(2,1)} custom-call(bf16[128,2048]{1,0:T(8,128)(2,1)} %get-tuple-element.67.refs_0_, bf16[128,2048]{1,0:T(8,128)(2,1)} %copy-done.9, bf16[128,2048]{1,0:T(8,128)(2,1)} %copy-done.10, bf16[128,2048]{1,0:T(8,128)(2,1)} %copy-done.11, bf16[128,2048]{1,0:T(8,128)(2,1)} %get-tuple-element.73.refs_4_, ...), custom_call_target="tpu_custom_call" | custom-call | flops 1000000 | bytes 1 | tf_op jit(solution)/shard_map/sum_parts/pallas_call | solution.py:377
  287.0 3.2 %widen.1 = (f32[1,512,768]{2,1,0:T(8,128)}, f32[1,96,4096]{2,1,0:T(8,128)}) custom-call(bf16[2,3072,128]{2,1,0:T(8,128)(2,1)} %bitcast.43), custom_call_target="tpu_custom_call" | custom-call | flops 1000000 | bytes 1 | tf_op jit(solution)/shard_map/widen/pallas_call | solution.py:343
  (74 shorter events, 48.1 us)
Async XLA Ops:
  7.2 279.9 %reduce-scatter.2.cloned.1.call-start = ((), (), s32[]{:S(2)}) async-start(), calls=%async_computation.1 | async-start | bytes 14155776 | tf_op jit(solution)/shard_map/reduce_scatter | solution.py:438
  9.9 34.3 %copy-start.2 = (bf16[136,4096]{1,0:T(8,128)(2,1)}, bf16[136,4096]{1,0:T(8,128)(2,1)S(1)}, u32[]{:S(2)}) copy-start(bf16[136,4096]{1,0:T(8,128)(2,1)S(1)} %pad_maximum_fusion.m0.b0) | copy-start | bytes 3342340
  9.9 17.2 %collective-permute-start.2 = (bf16[136,4096]{1,0:T(8,128)(2,1)S(1)}, bf16[136,4096]{1,0:T(8,128)(2,1)S(1)}, u32[]{:S(2)}, u32[]{:S(2)}) collective-permute-start(bf16[136,4096]{1,0:T(8,128)(2,1)S(1)} %pad_maximum_fusion.m0.b0), channel_id=1, source_target_pairs={{0,2},{1,3},{2,0},{3,1},{4,6},{5,7},{6,4},{7,5},{8,10},{9,11},{10,... | collective-permute-start | bytes 3342344 | tf_op jit(solution)/shard_map/p1x/ppermute | solution.py:46
  13.1 26.0 %collective-permute-start.1 = (bf16[136,4096]{1,0:T(8,128)(2,1)S(1)}, bf16[136,4096]{1,0:T(8,128)(2,1)S(1)}, u32[]{:S(2)}, u32[]{:S(2)}) collective-permute-start(bf16[136,4096]{1,0:T(8,128)(2,1)S(1)} %pad_maximum_fusion.m0.b0), channel_id=1, source_target_pairs={{0,3},{1,0},{2,1},{3,2},{4,7},{5,4},{6,5},{7,6},{8,11},{9,8},{10,9... | collective-permute-start | bytes 3342344 | tf_op jit(solution)/shard_map/p1x/ppermute | solution.py:46
  14.2 24.9 %collective-permute-start = (bf16[136,4096]{1,0:T(8,128)(2,1)S(1)}, bf16[136,4096]{1,0:T(8,128)(2,1)}, u32[]{:S(2)}, u32[]{:S(2)}) collective-permute-start(bf16[136,4096]{1,0:T(8,128)(2,1)S(1)} %pad_maximum_fusion.m0.b0), channel_id=1, source_target_pairs={{0,1},{1,2},{2,3},{3,0},{4,5},{5,6},{6,7},{7,4},{8,9},{9,10},{10,1... | collective-permute-start | bytes 3342344 | tf_op jit(solution)/shard_map/p1x/ppermute | solution.py:46
  39.2 18.1 %collective-permute-start.8 = (bf16[128,4096]{1,0:T(8,128)(2,1)}, bf16[128,4096]{1,0:T(8,128)(2,1)}, u32[]{:S(2)}, u32[]{:S(2)}) collective-permute-start(bf16[128,4096]{1,0:T(8,128)(2,1)} %b0), channel_id=1, source_target_pairs={{0,2},{1,3},{2,0},{3,1},{4,6},{5,7},{6,4},{7,5},{8,10},{9,11},{10,... | collective-permute-start | bytes 3145736 | tf_op jit(solution)/shard_map/p1g/ppermute | solution.py:46
  42.1 35.3 %collective-permute-start.7 = (bf16[128,4096]{1,0:T(8,128)(2,1)}, bf16[128,4096]{1,0:T(8,128)(2,1)}, u32[]{:S(2)}, u32[]{:S(2)}) collective-permute-start(bf16[128,4096]{1,0:T(8,128)(2,1)} %b0), channel_id=1, source_target_pairs={{0,3},{1,0},{2,1},{3,2},{4,7},{5,4},{6,5},{7,6},{8,11},{9,8},{10,9... | collective-permute-start | bytes 3145736 | tf_op jit(solution)/shard_map/p1g/ppermute | solution.py:46
  43.4 34.4 %collective-permute-start.6 = (bf16[128,4096]{1,0:T(8,128)(2,1)}, bf16[128,4096]{1,0:T(8,128)(2,1)}, u32[]{:S(2)}, u32[]{:S(2)}) collective-permute-start(bf16[128,4096]{1,0:T(8,128)(2,1)} %b0), channel_id=1, source_target_pairs={{0,1},{1,2},{2,3},{3,0},{4,5},{5,6},{6,7},{7,4},{8,9},{9,10},{10,1... | collective-permute-start | bytes 3145736 | tf_op jit(solution)/shard_map/p1g/ppermute | solution.py:46
  54.0 36.5 %collective-permute-start.3 = (bf16[4,72,4096]{2,1,0:T(8,128)(2,1)}, bf16[4,72,4096]{2,1,0:T(8,128)(2,1)S(1)}, u32[]{:S(2)}, u32[]{:S(2)}) collective-permute-start(bf16[4,72,4096]{2,1,0:T(8,128)(2,1)} %get-tuple-element.46), channel_id=1, source_target_pairs={{0,4},{1,5},{2,6},{3,7},{4,8},{5,9},{6,10},{7,11},{8,12},{9,13},{1... | collective-permute-start | bytes 7077896 | tf_op jit(solution)/shard_map/p2x/ppermute | solution.py:46
  55.6 34.9 %collective-permute-start.4 = (bf16[4,72,4096]{2,1,0:T(8,128)(2,1)}, bf16[4,72,4096]{2,1,0:T(8,128)(2,1)S(1)}, u32[]{:S(2)}, u32[]{:S(2)}) collective-permute-start(bf16[4,72,4096]{2,1,0:T(8,128)(2,1)} %get-tuple-element.47), channel_id=1, source_target_pairs={{0,12},{1,13},{2,14},{3,15},{4,0},{5,1},{6,2},{7,3},{8,4},{9,5},{1... | collective-permute-start | bytes 7077896 | tf_op jit(solution)/shard_map/p2x/ppermute | solution.py:46
  57.3 58.8 %collective-permute-start.5 = (bf16[4,72,4096]{2,1,0:T(8,128)(2,1)}, bf16[4,72,4096]{2,1,0:T(8,128)(2,1)}, u32[]{:S(2)}, u32[]{:S(2)}) collective-permute-start(bf16[4,72,4096]{2,1,0:T(8,128)(2,1)} %get-tuple-element.48), channel_id=1, source_target_pairs={{0,8},{1,9},{2,10},{3,11},{4,12},{5,13},{6,14},{7,15},{8,0},{9,1},... | collective-permute-start | bytes 7077896 | tf_op jit(solution)/shard_map/p2x/ppermute | solution.py:46
  85.6 55.7 %collective-permute-start.9 = (bf16[4,72,4096]{2,1,0:T(8,128)(2,1)}, bf16[4,72,4096]{2,1,0:T(8,128)(2,1)}, u32[]{:S(2)}, u32[]{:S(2)}) collective-permute-start(bf16[4,72,4096]{2,1,0:T(8,128)(2,1)} %get-tuple-element.52), channel_id=1, source_target_pairs={{0,4},{1,5},{2,6},{3,7},{4,8},{5,9},{6,10},{7,11},{8,12},{9,13},{1... | collective-permute-start | bytes 7077896 | tf_op jit(solution)/shard_map/p2g/ppermute | solution.py:46
  88.4 52.8 %collective-permute-start.10 = (bf16[4,72,4096]{2,1,0:T(8,128)(2,1)}, bf16[4,72,4096]{2,1,0:T(8,128)(2,1)}, u32[]{:S(2)}, u32[]{:S(2)}) collective-permute-start(bf16[4,72,4096]{2,1,0:T(8,128)(2,1)} %get-tuple-element.53), channel_id=1, source_target_pairs={{0,12},{1,13},{2,14},{3,15},{4,0},{5,1},{6,2},{7,3},{8,4},{9,5},{1... | collective-permute-start | bytes 7077896 | tf_op jit(solution)/shard_map/p2g/ppermute | solution.py:46
  141.3 30.7 %collective-permute-start.11 = (bf16[4,72,4096]{2,1,0:T(8,128)(2,1)}, bf16[4,72,4096]{2,1,0:T(8,128)(2,1)S(1)}, u32[]{:S(2)}, u32[]{:S(2)}) collective-permute-start(bf16[4,72,4096]{2,1,0:T(8,128)(2,1)} %get-tuple-element.56), channel_id=1, source_target_pairs={{0,8},{1,9},{2,10},{3,11},{4,12},{5,13},{6,14},{7,15},{8,0},{9,1},... | collective-permute-start | bytes 7077896 | tf_op jit(solution)/shard_map/p2g2/ppermute | solution.py:46
  164.5 34.1 %collective-permute-start.13 = (bf16[4,72,4096]{2,1,0:T(8,128)(2,1)}, bf16[4,72,4096]{2,1,0:T(8,128)(2,1)S(1)}, u32[]{:S(2)}, u32[]{:S(2)}) collective-permute-start(bf16[4,72,4096]{2,1,0:T(8,128)(2,1)} %bitcast.45), channel_id=1, source_target_pairs={{0,4},{1,5},{2,6},{3,7},{4,8},{5,9},{6,10},{7,11},{8,12},{9,13},{1... | collective-permute-start | bytes 7077896 | tf_op jit(solution)/shard_map/r2/ppermute | solution.py:46
  165.2 33.4 %collective-permute-start.12 = (bf16[4,72,4096]{2,1,0:T(8,128)(2,1)}, bf16[4,72,4096]{2,1,0:T(8,128)(2,1)}, u32[]{:S(2)}, u32[]{:S(2)}) collective-permute-start(bf16[4,72,4096]{2,1,0:T(8,128)(2,1)} %bitcast.44), channel_id=1, source_target_pairs={{0,12},{1,13},{2,14},{3,15},{4,0},{5,1},{6,2},{7,3},{8,4},{9,5},{1... | collective-permute-start | bytes 7077896 | tf_op jit(solution)/shard_map/r2/ppermute | solution.py:46
  213.1 17.7 %collective-permute-start.14 = (bf16[4,72,2048]{2,1,0:T(8,128)(2,1)S(1)}, bf16[4,72,2048]{2,1,0:T(8,128)(2,1)S(1)}, u32[]{:S(2)}, u32[]{:S(2)}) collective-permute-start(bf16[4,72,2048]{2,1,0:T(8,128)(2,1)S(1)} %bitcast.47), channel_id=1, source_target_pairs={{0,8},{1,9},{2,10},{3,11},{4,12},{5,13},{6,14},{7,15},{8,0},{9,1},... | collective-permute-start | bytes 3538952 | tf_op jit(solution)/shard_map/r2l/ppermute | solution.py:46
  230.8 22.0 %collective-permute-start.18 = (bf16[4,72,2048]{2,1,0:T(8,128)(2,1)S(1)}, bf16[4,72,2048]{2,1,0:T(8,128)(2,1)S(1)}, u32[]{:S(2)}, u32[]{:S(2)}) collective-permute-start(bf16[4,72,2048]{2,1,0:T(8,128)(2,1)S(1)} %bitcast.46), channel_id=1, source_target_pairs={{0,8},{1,9},{2,10},{3,11},{4,12},{5,13},{6,14},{7,15},{8,0},{9,1},... | collective-permute-start | bytes 3538952 | tf_op jit(solution)/shard_map/r2r/ppermute | solution.py:46
  239.1 23.9 %collective-permute-start.15 = (bf16[128,2048]{1,0:T(8,128)(2,1)}, bf16[128,2048]{1,0:T(8,128)(2,1)S(1)}, u32[]{:S(2)}, u32[]{:S(2)}) collective-permute-start(bf16[128,2048]{1,0:T(8,128)(2,1)} %get-tuple-element.68), channel_id=1, source_target_pairs={{0,3},{1,0},{2,1},{3,2},{4,7},{5,4},{6,5},{7,6},{8,11},{9,8},{10,9... | collective-permute-start | bytes 1572872 | tf_op jit(solution)/shard_map/r1l/ppermute | solution.py:46
  241.7 24.1 %collective-permute-start.16 = (bf16[128,2048]{1,0:T(8,128)(2,1)}, bf16[128,2048]{1,0:T(8,128)(2,1)S(1)}, u32[]{:S(2)}, u32[]{:S(2)}) collective-permute-start(bf16[128,2048]{1,0:T(8,128)(2,1)} %get-tuple-element.69), channel_id=1, source_target_pairs={{0,1},{1,2},{2,3},{3,0},{4,5},{5,6},{6,7},{7,4},{8,9},{9,10},{10,1... | collective-permute-start | bytes 1572872 | tf_op jit(solution)/shard_map/r1l/ppermute | solution.py:46
  241.7 24.1 %collective-permute-start.17 = (bf16[128,2048]{1,0:T(8,128)(2,1)}, bf16[128,2048]{1,0:T(8,128)(2,1)S(1)}, u32[]{:S(2)}, u32[]{:S(2)}) collective-permute-start(bf16[128,2048]{1,0:T(8,128)(2,1)} %get-tuple-element.70), channel_id=1, source_target_pairs={{0,2},{1,3},{2,0},{3,1},{4,6},{5,7},{6,4},{7,5},{8,10},{9,11},{10,... | collective-permute-start | bytes 1572872 | tf_op jit(solution)/shard_map/r1l/ppermute | solution.py:46
  259.1 16.6 %collective-permute-start.19 = (bf16[128,2048]{1,0:T(8,128)(2,1)}, bf16[128,2048]{1,0:T(8,128)(2,1)S(1)}, u32[]{:S(2)}, u32[]{:S(2)}) collective-permute-start(bf16[128,2048]{1,0:T(8,128)(2,1)} %get-tuple-element.74), channel_id=1, source_target_pairs={{0,3},{1,0},{2,1},{3,2},{4,7},{5,4},{6,5},{7,6},{8,11},{9,8},{10,9... | collective-permute-start | bytes 1572872 | tf_op jit(solution)/shard_map/r1r/ppermute | solution.py:46
  263.0 16.2 %collective-permute-start.20 = (bf16[128,2048]{1,0:T(8,128)(2,1)}, bf16[128,2048]{1,0:T(8,128)(2,1)S(1)}, u32[]{:S(2)}, u32[]{:S(2)}) collective-permute-start(bf16[128,2048]{1,0:T(8,128)(2,1)} %get-tuple-element.75), channel_id=1, source_target_pairs={{0,1},{1,2},{2,3},{3,0},{4,5},{5,6},{6,7},{7,4},{8,9},{9,10},{10,1... | collective-permute-start | bytes 1572872 | tf_op jit(solution)/shard_map/r1r/ppermute | solution.py:46
  263.0 16.2 %collective-permute-start.21 = (bf16[128,2048]{1,0:T(8,128)(2,1)}, bf16[128,2048]{1,0:T(8,128)(2,1)S(1)}, u32[]{:S(2)}, u32[]{:S(2)}) collective-permute-start(bf16[128,2048]{1,0:T(8,128)(2,1)} %get-tuple-element.76), channel_id=1, source_target_pairs={{0,2},{1,3},{2,0},{3,1},{4,6},{5,7},{6,4},{7,5},{8,10},{9,11},{10,... | collective-permute-start | bytes 1572872 | tf_op jit(solution)/shard_map/r1r/ppermute | solution.py:46
  (16 other events, 160.3 us)
Sparse Core Ops, SparseCore 0:
  212.0 74.9 reduce-scatter.1

commit v4 on v2

--- a/solution.py
+++ b/solution.py
@@ -101,10 +101,12 @@
     )(dest, *blocks)
 
 
-def select_kernel(scaled, pick_ref, weight_ref, b0, b1, b2, b3, o0, o1, o2, o3):
-    outs = (o0, o1, o2, o3)
-    for i, block in enumerate((b0, b1, b2, b3)):
-        rows = jnp.dot(pick_ref[i], block[...], preferred_element_type=jnp.float32)
+def select_kernel(scaled, pick_ref, weight_ref, *refs):
+    blocks, outs = [r[...] for r in refs[:-SIDE]], refs[-SIDE:]
+    if len(blocks) > SIDE:
+        blocks[3:] = [jnp.concatenate(blocks[3:], axis=0)]
+    for i, block in enumerate(blocks):
+        rows = jnp.dot(pick_ref[i], block, preferred_element_type=jnp.float32)
         if scaled:
             rows = rows * weight_ref[i][:, 0:1]
         rows = rows.astype(jnp.bfloat16)
@@ -123,7 +125,7 @@
             pl.BlockSpec((SIDE, SIDE * SLOTS, 128), lambda c: (0, 0, 0)),
             pl.BlockSpec((SIDE, SIDE * SLOTS, 128), lambda c: (0, 0, 0)),
         ]
-        + [pl.BlockSpec((128, tile), lambda c: (0, c))] * SIDE,
+        + [pl.BlockSpec((min(b.shape[0], 128), tile), lambda c: (0, c)) for b in blocks],
         out_specs=(pl.BlockSpec((SIDE, SLOTS, tile), lambda c: (0, 0, c)),) * SIDE,
         compiler_params=PARAMS,
         cost_estimate=HEAVY,
@@ -294,26 +296,6 @@
     )(act, *gs)
 
 
-def parts_kernel(p0, p1, p2, p3, out):
-    total = sum(p[...].astype(jnp.float32) for p in (p0, p1, p2, p3))
-    out[...] = total.astype(jnp.bfloat16)
-
-
-def sum_parts(parts):
-    rows, width = parts[0].shape
-    spec = pl.BlockSpec((rows // SIDE, width), lambda c: (c, 0))
-    return pl.pallas_call(
-        parts_kernel,
-        out_shape=jax.ShapeDtypeStruct((rows, width), jnp.bfloat16),
-        grid=(SIDE,),
-        in_specs=[spec] * SIDE,
-        out_specs=spec,
-        compiler_params=PARAMS,
-        cost_estimate=LIGHT,
-        name="sum_parts",
-    )(*parts)
-
-
 def after(value, *earlier):
     return lax.optimization_barrier((value, *earlier))[0]
 
@@ -340,10 +322,14 @@
         token_blocks = [send(message, True, o) for o in OFFSETS]
     cotangent = after(cotangent, *token_blocks)
     with jax.named_scope("p1g"):
-        cot_blocks = [send(cotangent, True, o) for o in OFFSETS]
+        cot_blocks = [send(cotangent, True, o) for o in OFFSETS[:3]]
     pick, put, weight = route(dest, token_blocks)
 
     out_x = select(pick, weight, token_blocks, False)
+    with jax.named_scope("p1f"):
+        _, low, high = lax.optimization_barrier((out_x, cot_blocks[1], cot_blocks[2]))
+        cot_blocks.append(send(low[:64], True, 1))
+        cot_blocks.append(send(high[64:], True, -1))
     with jax.named_scope("p2x"):
         rx = [send(r, False, o).reshape(ROWS, width) for r, o in zip(out_x, OFFSETS)]
     out_g = select(pick, weight, cot_blocks, True)
@@ -373,8 +359,8 @@
     parts = combine(after(put, up_done), returned)
     with jax.named_scope("r1"):
         parts = [send(p, True, -o) for p, o in zip(parts, OFFSETS)]
-    token_grad = sum_parts(parts)
-    token_grad, up_grad, down_grad = lax.optimization_barrier((token_grad, up_grad, down_grad))
+    token_grad = sum(p.astype(jnp.float32) for p in parts).astype(jnp.bfloat16)
+    token_grad, up_grad = lax.optimization_barrier((token_grad, up_grad))
     return token_grad, up_grad.astype(jnp.float32)[None], down_grad.astype(jnp.float32)[None]
 
 

time: 289 us -> 288 us (level)
  Pallas kernels: 103 us -> 98.5 us
  other arithmetic: 7.59 us -> 10.5 us
    pallas_call x1 -> x0, Pallas kernels: 4.15 us -> none  [sum_parts(): pl.pallas_call(parts_kernel, out_shape=jax.ShapeDtypeStruct((rows, width)...]
    convert_element_type x0 -> x1, other arithmetic: none -> 2.96 us  [body(): sum((p.astype(jnp.float32) for p in parts)).astype(jnp.bfloat16)]
    ppermute x18 -> x19, starting transfers between devices: 34.6 us -> 32 us  [send(): lax.ppermute(value, BOTH, ring(first, shift))]
    ppermute x18 -> x19, waiting for transfers between devices: 122 us -> 124 us  [send(): lax.ppermute(value, BOTH, ring(first, shift))]
  transfers between devices with their start and end apart: 20 -> 21, of which waited for: 13 -> 15; matrix products, arithmetic and copies ran while one was open for 0% -> 2% of each run, Pallas kernels for 36% -> 34%
where the time goes in v4:
time: 288 us; the launch traced here: 287 us
  waiting for transfers between devices  126 us (44%)
  Pallas kernels  98.5 us (34%)
  starting transfers between devices  32 us (11%)
  between operations  14.1 us (5%)
  other arithmetic  10.5 us (4%)
  local copies, waits for them, and re-layouts  5.79 us (2%)
    ppermute x19, waiting for transfers between devices, send(): lax.ppermute(value, BOTH, ring(first, shift))  124 us
    pallas_call x2, Pallas kernels, expert_back(): pl.pallas_call(functools.partial(back_kernel, n), out_shape=(jax.ShapeDty...  32.8 us
    ppermute x19, starting transfers between devices, send(): lax.ppermute(value, BOTH, ring(first, shift))  32 us
    pallas_call x2, Pallas kernels, select(): pl.pallas_call(functools.partial(select_kernel, scaled), out_shape=(jax.S...  15.5 us
    pallas_call x1, Pallas kernels, expert_pre(): pl.pallas_call(pre_kernel, out_shape=(jax.ShapeDtypeStruct((WIDE + ROWS,...  14.6 us
    pallas_call x1, Pallas kernels, up_partial(): pl.pallas_call(up_kernel, out_shape=jax.ShapeDtypeStruct((width, hidden),...  12.8 us
    pallas_call x1, Pallas kernels, down_partial(): pl.pallas_call(down_kernel, out_shape=jax.ShapeDtypeStruct((hidden, width...  12.5 us
    pallas_call x1, Pallas kernels, combine(): pl.pallas_call(combine_kernel, out_shape=(jax.ShapeDtypeStruct((128, widt...  8.23 us
  transfers between devices with their start and end apart: 21, of which 15 were waited for; matrix products, arithmetic and copies ran while one was open for 2% of the time, Pallas kernels for 34%

profile of v4, /device:TPU:0, one launch (start us, length us, event | category | flops | bytes accessed | tf_op | source)
XLA Modules:
  0.0 287.3 jit_solution(2601377363511048268)
XLA Ops:
  9.9 3.2 %collective-permute-start.2 = (bf16[136,4096]{1,0:T(8,128)(2,1)S(1)}, bf16[136,4096]{1,0:T(8,128)(2,1)S(1)}, u32[]{:S(2)}, u32[]{:S(2)}) collective-permute-start(bf16[136,4096]{1,0:T(8,128)(2,1)S(1)} %pad_maximum_fusion.m0.refs_0_), channel_id=1, source_target_pairs={{0,2},{1,3},{2,0},{3,1},{4,6},{5,7},{6,4},{7,5},{8,10},{9,11},{10,... | collective-permute-start | bytes 3342344 | tf_op jit(solution)/shard_map/p1x/ppermute | solution.py:47
  16.3 10.8 %collective-permute-done.2.m3.refs_3_ = bf16[136,4096]{1,0:T(8,128)(2,1)S(1)} collective-permute-done((bf16[136,4096]{1,0:T(8,128)(2,1)S(1)}, bf16[136,4096]{1,0:T(8,128)(2,1)S(1)}, u32[]{:S(2)}, u32[]{:S(2)}) %collective-permute-start.2) | collective-permute-done | bytes 1114144 | tf_op jit(solution)/shard_map/p1x/ppermute | solution.py:47
  27.1 12.0 %collective-permute-done.1.m2.refs_2_ = bf16[136,4096]{1,0:T(8,128)(2,1)S(1)} collective-permute-done((bf16[136,4096]{1,0:T(8,128)(2,1)S(1)}, bf16[136,4096]{1,0:T(8,128)(2,1)S(1)}, u32[]{:S(2)}, u32[]{:S(2)}) %collective-permute-start.1) | collective-permute-done | bytes 1114144 | tf_op jit(solution)/shard_map/p1x/ppermute | solution.py:47
  44.0 7.7 %select.22 = (bf16[4,72,4096]{2,1,0:T(8,128)(2,1)}, bf16[4,72,4096]{2,1,0:T(8,128)(2,1)}, bf16[4,72,4096]{2,1,0:T(8,128)(2,1)}, bf16[4,72,4096]{2,1,0:T(8,128)(2,1)}) custom-call(bf16[4,288,128]{2,1,0:T(8,128)(2,1)} %get-tuple-element.39.pick_ref, f32[4,288,128]{2,1,0:T(8,128)} %get-tuple-element.40.weight_ref, bf16[136,4096]{1,0:T(8,128)(2,1)} %copy-done.1, ...), custom_call_target="tpu_custom_call" | custom-call | flops 30000001024 | bytes 1 | tf_op jit(solution)/shard_map/select/pallas_call | solution.py:120
  51.7 2.8 collective-permute-done.7.refs_2_
  54.4 3.7 %collective-permute-done.6.refs_1_ = bf16[128,4096]{1,0:T(8,128)(2,1)} collective-permute-done((bf16[128,4096]{1,0:T(8,128)(2,1)}, bf16[128,4096]{1,0:T(8,128)(2,1)}, u32[]{:S(2)}, u32[]{:S(2)}) %collective-permute-start.6) | collective-permute-done | bytes 1048608 | tf_op jit(solution)/shard_map/p1g/ppermute | solution.py:47
  67.6 7.5 %collective-permute-done.9.refs_4_ = bf16[64,4096]{1,0:T(8,128)(2,1)S(1)} collective-permute-done((bf16[64,4096]{1,0:T(8,128)(2,1)S(1)}, bf16[64,4096]{1,0:T(8,128)(2,1)S(1)}, u32[]{:S(2)}, u32[]{:S(2)}) %collective-permute-start.9) | collective-permute-done | bytes 524320 | tf_op jit(solution)/shard_map/p1f/ppermute | solution.py:47
  77.3 7.8 %select_scaled.1 = (bf16[4,72,4096]{2,1,0:T(8,128)(2,1)}, bf16[4,72,4096]{2,1,0:T(8,128)(2,1)}, bf16[4,72,4096]{2,1,0:T(8,128)(2,1)}, bf16[4,72,4096]{2,1,0:T(8,128)(2,1)}) custom-call(bf16[4,288,128]{2,1,0:T(8,128)(2,1)} %get-tuple-element.39.pick_ref, f32[4,288,128]{2,1,0:T(8,128)} %get-tuple-element.40.weight_ref, bf16[128,4096]{1,0:T(8,128)(2,1)} %refs_0_, ...), custom_call_target="tpu_custom_call" | custom-call | flops 30000001024 | bytes 1 | tf_op jit(solution)/shard_map/select_scaled/pallas_call | solution.py:120
  88.3 5.1 %collective-permute-done.3 = bf16[4,72,4096]{2,1,0:T(8,128)(2,1)} collective-permute-done((bf16[4,72,4096]{2,1,0:T(8,128)(2,1)}, bf16[4,72,4096]{2,1,0:T(8,128)(2,1)}, u32[]{:S(2)}, u32[]{:S(2)}) %collective-permute-start.3) | collective-permute-done | bytes 2359328 | tf_op jit(solution)/shard_map/p2x/ppermute | solution.py:47
  93.4 25.9 %collective-permute-done.5 = bf16[4,72,4096]{2,1,0:T(8,128)(2,1)} collective-permute-done((bf16[4,72,4096]{2,1,0:T(8,128)(2,1)}, bf16[4,72,4096]{2,1,0:T(8,128)(2,1)}, u32[]{:S(2)}, u32[]{:S(2)}) %collective-permute-start.5) | collective-permute-done | bytes 2359328 | tf_op jit(solution)/shard_map/p2x/ppermute | solution.py:47
  119.4 14.6 %expert_pre.1 = (f32[1152,768]{1,0:T(8,128)}, bf16[768,1152]{1,0:T(8,128)(2,1)}) custom-call(bf16[288,4096]{1,0:T(8,128)(2,1)} %bitcast.45, bf16[288,4096]{1,0:T(8,128)(2,1)} %bitcast.5.refs_1_.x1, bf16[288,4096]{1,0:T(8,128)(2,1)} %bitcast.6.refs_2_.x2, bf16[288,4096]{1,0:T(8,128)(2,1)} %bitcast.7.refs_3_.x3, bf16[4096,768]{1,0:T(8,128)(2,1)} %bitcast.30), custom_call_target="tpu_custom_call" | custom-call | flops 7247757312 | bytes 17498112 | tf_op jit(solution)/shard_map/expert_pre/pallas_call | solution.py:190
  133.9 10.0 %collective-permute-done.10 = bf16[4,72,4096]{2,1,0:T(8,128)(2,1)S(1)} collective-permute-done((bf16[4,72,4096]{2,1,0:T(8,128)(2,1)}, bf16[4,72,4096]{2,1,0:T(8,128)(2,1)S(1)}, u32[]{:S(2)}, u32[]{:S(2)}) %collective-permute-start.10) | collective-permute-done | bytes 2359328 | tf_op jit(solution)/shard_map/p2g/ppermute | solution.py:47
  147.9 20.3 %expert_back.2 = (bf16[864,768]{1,0:T(8,128)(2,1)}, bf16[288,4096]{1,0:T(8,128)(2,1)}, bf16[288,4096]{1,0:T(8,128)(2,1)}, bf16[288,4096]{1,0:T(8,128)(2,1)}) custom-call(bf16[288,4096]{1,0:T(8,128)(2,1)} %bitcast.35, bf16[288,4096]{1,0:T(8,128)(2,1)} %bitcast.37, bf16[288,4096]{1,0:T(8,128)(2,1)} %bitcast.39, f32[1152,768]{1,0:T(8,128)} %get-tuple-element.51.refs_3_.refs_1_, ...), custom_call_target="tpu_custom_call" | custom-call | flops 10871635968 | bytes 23101440 | tf_op jit(solution)/shard_map/expert_back/pallas_call | solution.py:238
  171.5 4.5 %collective-permute-done.12 = bf16[4,72,4096]{2,1,0:T(8,128)(2,1)S(1)} collective-permute-done((bf16[4,72,4096]{2,1,0:T(8,128)(2,1)}, bf16[4,72,4096]{2,1,0:T(8,128)(2,1)S(1)}, u32[]{:S(2)}, u32[]{:S(2)}) %collective-permute-start.12) | collective-permute-done | bytes 2359328 | tf_op jit(solution)/shard_map/p2g2/ppermute | solution.py:47
  177.4 12.5 %down_partial.1 = bf16[768,4096]{1,0:T(8,128)(2,1)} custom-call(bf16[768,1152]{1,0:T(8,128)(2,1)} %get-tuple-element.59.act, bf16[288,4096]{1,0:T(8,128)(2,1)} %bitcast.36, bf16[288,4096]{1,0:T(8,128)(2,1)} %bitcast.38, bf16[288,4096]{1,0:T(8,128)(2,1)} %bitcast.40, bf16[288,4096]{1,0:T(8,128)(2,1)} %bitcast.28), custom_call_target="tpu_custom_call" | custom-call | flops 1000000 | bytes 1 | tf_op jit(solution)/shard_map/down_partial/pallas_call | solution.py:286
  189.9 12.4 %expert_back.3 = (bf16[288,768]{1,0:T(8,128)(2,1)}, bf16[288,4096]{1,0:T(8,128)(2,1)}) custom-call(bf16[288,4096]{1,0:T(8,128)(2,1)} %bitcast.29, f32[1152,768]{1,0:T(8,128)} %get-tuple-element.51.refs_3_.refs_1_, bf16[768,4096]{1,0:T(8,128)(2,1)} %bitcast.34, bf16[4096,768]{1,0:T(8,128)(2,1)} %bitcast.32), custom_call_target="tpu_custom_call" | custom-call | flops 1000000 | bytes 1 | tf_op jit(solution)/shard_map/expert_back/pallas_call | solution.py:238
  202.4 2.8 collective-permute-start.15
  205.1 12.8 %up_partial.1 = bf16[4096,768]{1,0:T(8,128)(2,1)} custom-call(bf16[288,4096]{1,0:T(8,128)(2,1)} %bitcast.46, bf16[288,4096]{1,0:T(8,128)(2,1)} %bitcast.5.refs_1_.x1, bf16[288,4096]{1,0:T(8,128)(2,1)} %bitcast.6.refs_2_.x2, bf16[288,4096]{1,0:T(8,128)(2,1)} %bitcast.7.refs_3_.x3, bf16[864,768]{1,0:T(8,128)(2,1)} %get-tuple-element.52.grad, ...), custom_call_target="tpu_custom_call" | custom-call | flops 299999985664 | bytes 1 | tf_op jit(solution)/shard_map/up_partial/pallas_call | solution.py:266
  217.9 15.2 %collective-permute-done.15.r3 = bf16[4,72,4096]{2,1,0:T(8,128)(2,1)} collective-permute-done((bf16[4,72,4096]{2,1,0:T(8,128)(2,1)}, bf16[4,72,4096]{2,1,0:T(8,128)(2,1)}, u32[]{:S(2)}, u32[]{:S(2)}) %collective-permute-start.15) | collective-permute-done | bytes 2359328 | tf_op jit(solution)/shard_map/r2/ppermute | solution.py:47
  233.6 8.2 %combine.1 = (bf16[128,4096]{1,0:T(8,128)(2,1)}, bf16[128,4096]{1,0:T(8,128)(2,1)}, bf16[128,4096]{1,0:T(8,128)(2,1)}, bf16[128,4096]{1,0:T(8,128)(2,1)}) custom-call(bf16[4,4,128,72]{3,2,1,0:T(8,128)(2,1)} %get-tuple-element.63.put_ref, bf16[4,72,4096]{2,1,0:T(8,128)(2,1)} %bitcast.41, bf16[4,72,4096]{2,1,0:T(8,128)(2,1)} %collective-permute-done.13.r1, ...), custom_call_target="tpu_custom_call" | custom-call | flops 1000000 | bytes 1 | tf_op jit(solution)/shard_map/combine/pallas_call | solution.py:148
  241.8 2.7 collective-permute-start.16
  246.8 21.6 %collective-permute-done.16 = bf16[128,4096]{1,0:T(8,128)(2,1)S(1)} collective-permute-done((bf16[128,4096]{1,0:T(8,128)(2,1)}, bf16[128,4096]{1,0:T(8,128)(2,1)S(1)}, u32[]{:S(2)}, u32[]{:S(2)}) %collective-permute-start.16) | collective-permute-done | bytes 1048608 | tf_op jit(solution)/shard_map/r1/ppermute | solution.py:47
  268.4 3.6 %collective-permute-done.17 = bf16[128,4096]{1,0:T(8,128)(2,1)S(1)} collective-permute-done((bf16[128,4096]{1,0:T(8,128)(2,1)}, bf16[128,4096]{1,0:T(8,128)(2,1)S(1)}, u32[]{:S(2)}, u32[]{:S(2)}) %collective-permute-start.17) | collective-permute-done | bytes 1048608 | tf_op jit(solution)/shard_map/r1/ppermute | solution.py:47
  271.9 3.0 %add_convert_fusion = bf16[128,4096]{1,0:T(8,128)(2,1)} fusion(bf16[128,4096]{1,0:T(8,128)(2,1)S(1)} %collective-permute-done.18, bf16[128,4096]{1,0:T(8,128)(2,1)S(1)} %collective-permute-done.17, bf16[128,4096]{1,0:T(8,128)(2,1)S(1)} %collective-permute-done.16, bf16[128,4096]{1,0:T(8,128)(2,1)} %get-tuple-element.66), kind=kLoop, calls=%fused_computation | loop fusion | flops 4194304 | bytes 5242880 | tf_op jit(solution)/shard_map/convert_element_type | solution.py:362
  (57 shorter events, 42.7 us)
Async XLA Ops:
  7.2 226.4 %reduce-scatter.3.cloned.1.call-start = ((), (), s32[]{:S(2)}) async-start(), calls=%async_computation.2 | async-start | bytes 7077888 | tf_op jit(solution)/shard_map/reduce_scatter | solution.py:348
  9.9 31.9 %copy-start.1 = (bf16[136,4096]{1,0:T(8,128)(2,1)}, bf16[136,4096]{1,0:T(8,128)(2,1)S(1)}, u32[]{:S(2)}) copy-start(bf16[136,4096]{1,0:T(8,128)(2,1)S(1)} %pad_maximum_fusion.m0.refs_0_) | copy-start | bytes 3342340
  9.9 17.2 %collective-permute-start.2 = (bf16[136,4096]{1,0:T(8,128)(2,1)S(1)}, bf16[136,4096]{1,0:T(8,128)(2,1)S(1)}, u32[]{:S(2)}, u32[]{:S(2)}) collective-permute-start(bf16[136,4096]{1,0:T(8,128)(2,1)S(1)} %pad_maximum_fusion.m0.refs_0_), channel_id=1, source_target_pairs={{0,2},{1,3},{2,0},{3,1},{4,6},{5,7},{6,4},{7,5},{8,10},{9,11},{10,... | collective-permute-start | bytes 3342344 | tf_op jit(solution)/shard_map/p1x/ppermute | solution.py:47
  13.1 26.0 %collective-permute-start.1 = (bf16[136,4096]{1,0:T(8,128)(2,1)S(1)}, bf16[136,4096]{1,0:T(8,128)(2,1)S(1)}, u32[]{:S(2)}, u32[]{:S(2)}) collective-permute-start(bf16[136,4096]{1,0:T(8,128)(2,1)S(1)} %pad_maximum_fusion.m0.refs_0_), channel_id=1, source_target_pairs={{0,3},{1,0},{2,1},{3,2},{4,7},{5,4},{6,5},{7,6},{8,11},{9,8},{10,9... | collective-permute-start | bytes 3342344 | tf_op jit(solution)/shard_map/p1x/ppermute | solution.py:47
  14.2 24.9 %collective-permute-start = (bf16[136,4096]{1,0:T(8,128)(2,1)S(1)}, bf16[136,4096]{1,0:T(8,128)(2,1)}, u32[]{:S(2)}, u32[]{:S(2)}) collective-permute-start(bf16[136,4096]{1,0:T(8,128)(2,1)S(1)} %pad_maximum_fusion.m0.refs_0_), channel_id=1, source_target_pairs={{0,1},{1,2},{2,3},{3,0},{4,5},{5,6},{6,7},{7,4},{8,9},{9,10},{10,1... | collective-permute-start | bytes 3342344 | tf_op jit(solution)/shard_map/p1x/ppermute | solution.py:47
  27.1 14.7 %copy-start.4 = (bf16[136,4096]{1,0:T(8,128)(2,1)}, bf16[136,4096]{1,0:T(8,128)(2,1)S(1)}, u32[]{:S(2)}) copy-start(bf16[136,4096]{1,0:T(8,128)(2,1)S(1)} %collective-permute-done.2.m3.refs_3_) | copy-start | bytes 3342340
  39.2 15.3 %collective-permute-start.7 = (bf16[128,4096]{1,0:T(8,128)(2,1)}, bf16[128,4096]{1,0:T(8,128)(2,1)}, u32[]{:S(2)}, u32[]{:S(2)}) collective-permute-start(bf16[128,4096]{1,0:T(8,128)(2,1)} %refs_0_), channel_id=1, source_target_pairs={{0,3},{1,0},{2,1},{3,2},{4,7},{5,4},{6,5},{7,6},{8,11},{9,8},{10,9... | collective-permute-start | bytes 3145736 | tf_op jit(solution)/shard_map/p1g/ppermute | solution.py:47
  41.8 16.3 %collective-permute-start.6 = (bf16[128,4096]{1,0:T(8,128)(2,1)}, bf16[128,4096]{1,0:T(8,128)(2,1)}, u32[]{:S(2)}, u32[]{:S(2)}) collective-permute-start(bf16[128,4096]{1,0:T(8,128)(2,1)} %refs_0_), channel_id=1, source_target_pairs={{0,1},{1,2},{2,3},{3,0},{4,5},{5,6},{6,7},{7,4},{8,9},{9,10},{10,1... | collective-permute-start | bytes 3145736 | tf_op jit(solution)/shard_map/p1g/ppermute | solution.py:47
  60.3 14.8 %collective-permute-start.9 = (bf16[64,4096]{1,0:T(8,128)(2,1)S(1)}, bf16[64,4096]{1,0:T(8,128)(2,1)S(1)}, u32[]{:S(2)}, u32[]{:S(2)}) collective-permute-start(bf16[64,4096]{1,0:T(8,128)(2,1)S(1)} %slice.7), channel_id=1, source_target_pairs={{0,3},{1,0},{2,1},{3,2},{4,7},{5,4},{6,5},{7,6},{8,11},{9,8},{10,9... | collective-permute-start | bytes 1572872 | tf_op jit(solution)/shard_map/p1f/ppermute | solution.py:47
  60.4 16.1 %collective-permute-start.8 = (bf16[64,4096]{1,0:T(8,128)(2,1)S(1)}, bf16[64,4096]{1,0:T(8,128)(2,1)S(1)}, u32[]{:S(2)}, u32[]{:S(2)}) collective-permute-start(bf16[64,4096]{1,0:T(8,128)(2,1)S(1)} %slice.6), channel_id=1, source_target_pairs={{0,1},{1,2},{2,3},{3,0},{4,5},{5,6},{6,7},{7,4},{8,9},{9,10},{10,1... | collective-permute-start | bytes 1572872 | tf_op jit(solution)/shard_map/p1f/ppermute | solution.py:47
  62.4 31.1 %collective-permute-start.3 = (bf16[4,72,4096]{2,1,0:T(8,128)(2,1)}, bf16[4,72,4096]{2,1,0:T(8,128)(2,1)}, u32[]{:S(2)}, u32[]{:S(2)}) collective-permute-start(bf16[4,72,4096]{2,1,0:T(8,128)(2,1)} %get-tuple-element.42), channel_id=1, source_target_pairs={{0,4},{1,5},{2,6},{3,7},{4,8},{5,9},{6,10},{7,11},{8,12},{9,13},{1... | collective-permute-start | bytes 7077896 | tf_op jit(solution)/shard_map/p2x/ppermute | solution.py:47
  63.9 29.5 %collective-permute-start.4 = (bf16[4,72,4096]{2,1,0:T(8,128)(2,1)}, bf16[4,72,4096]{2,1,0:T(8,128)(2,1)}, u32[]{:S(2)}, u32[]{:S(2)}) collective-permute-start(bf16[4,72,4096]{2,1,0:T(8,128)(2,1)} %get-tuple-element.43), channel_id=1, source_target_pairs={{0,12},{1,13},{2,14},{3,15},{4,0},{5,1},{6,2},{7,3},{8,4},{9,5},{1... | collective-permute-start | bytes 7077896 | tf_op jit(solution)/shard_map/p2x/ppermute | solution.py:47
  65.6 53.8 %collective-permute-start.5 = (bf16[4,72,4096]{2,1,0:T(8,128)(2,1)}, bf16[4,72,4096]{2,1,0:T(8,128)(2,1)}, u32[]{:S(2)}, u32[]{:S(2)}) collective-permute-start(bf16[4,72,4096]{2,1,0:T(8,128)(2,1)} %get-tuple-element.44), channel_id=1, source_target_pairs={{0,8},{1,9},{2,10},{3,11},{4,12},{5,13},{6,14},{7,15},{8,0},{9,1},... | collective-permute-start | bytes 7077896 | tf_op jit(solution)/shard_map/p2x/ppermute | solution.py:47
  85.1 58.8 %collective-permute-start.10 = (bf16[4,72,4096]{2,1,0:T(8,128)(2,1)}, bf16[4,72,4096]{2,1,0:T(8,128)(2,1)S(1)}, u32[]{:S(2)}, u32[]{:S(2)}) collective-permute-start(bf16[4,72,4096]{2,1,0:T(8,128)(2,1)} %get-tuple-element.49), channel_id=1, source_target_pairs={{0,4},{1,5},{2,6},{3,7},{4,8},{5,9},{6,10},{7,11},{8,12},{9,13},{1... | collective-permute-start | bytes 7077896 | tf_op jit(solution)/shard_map/p2g/ppermute | solution.py:47
  86.7 57.2 %collective-permute-start.11 = (bf16[4,72,4096]{2,1,0:T(8,128)(2,1)}, bf16[4,72,4096]{2,1,0:T(8,128)(2,1)S(1)}, u32[]{:S(2)}, u32[]{:S(2)}) collective-permute-start(bf16[4,72,4096]{2,1,0:T(8,128)(2,1)} %get-tuple-element.50), channel_id=1, source_target_pairs={{0,12},{1,13},{2,14},{3,15},{4,0},{5,1},{6,2},{7,3},{8,4},{9,5},{1... | collective-permute-start | bytes 7077896 | tf_op jit(solution)/shard_map/p2g/ppermute | solution.py:47
  143.9 4.0 %copy-start.2 = (bf16[4,72,4096]{2,1,0:T(8,128)(2,1)}, bf16[4,72,4096]{2,1,0:T(8,128)(2,1)S(1)}, u32[]{:S(2)}) copy-start(bf16[4,72,4096]{2,1,0:T(8,128)(2,1)S(1)} %collective-permute-done.10) | copy-start | bytes 7077892
  145.3 30.7 %collective-permute-start.12 = (bf16[4,72,4096]{2,1,0:T(8,128)(2,1)}, bf16[4,72,4096]{2,1,0:T(8,128)(2,1)S(1)}, u32[]{:S(2)}, u32[]{:S(2)}) collective-permute-start(bf16[4,72,4096]{2,1,0:T(8,128)(2,1)} %get-tuple-element.54), channel_id=1, source_target_pairs={{0,8},{1,9},{2,10},{3,11},{4,12},{5,13},{6,14},{7,15},{8,0},{9,1},... | collective-permute-start | bytes 7077896 | tf_op jit(solution)/shard_map/p2g2/ppermute | solution.py:47
  168.3 34.1 %collective-permute-start.14 = (bf16[4,72,4096]{2,1,0:T(8,128)(2,1)}, bf16[4,72,4096]{2,1,0:T(8,128)(2,1)}, u32[]{:S(2)}, u32[]{:S(2)}) collective-permute-start(bf16[4,72,4096]{2,1,0:T(8,128)(2,1)} %bitcast.43), channel_id=1, source_target_pairs={{0,4},{1,5},{2,6},{3,7},{4,8},{5,9},{6,10},{7,11},{8,12},{9,13},{1... | collective-permute-start | bytes 7077896 | tf_op jit(solution)/shard_map/r2/ppermute | solution.py:47
  169.0 33.3 %collective-permute-start.13 = (bf16[4,72,4096]{2,1,0:T(8,128)(2,1)}, bf16[4,72,4096]{2,1,0:T(8,128)(2,1)}, u32[]{:S(2)}, u32[]{:S(2)}) collective-permute-start(bf16[4,72,4096]{2,1,0:T(8,128)(2,1)} %bitcast.42), channel_id=1, source_target_pairs={{0,12},{1,13},{2,14},{3,15},{4,0},{5,1},{6,2},{7,3},{8,4},{9,5},{1... | collective-permute-start | bytes 7077896 | tf_op jit(solution)/shard_map/r2/ppermute | solution.py:47
  189.9 88.1 %reduce-scatter.5.cloned.1.call-start = ((), (), s32[]{:S(2)}) async-start(), calls=%async_computation.3 | async-start | bytes 7077888 | tf_op jit(solution)/shard_map/reduce_scatter | solution.py:357
  202.4 30.7 %collective-permute-start.15 = (bf16[4,72,4096]{2,1,0:T(8,128)(2,1)}, bf16[4,72,4096]{2,1,0:T(8,128)(2,1)}, u32[]{:S(2)}, u32[]{:S(2)}) collective-permute-start(bf16[4,72,4096]{2,1,0:T(8,128)(2,1)} %bitcast.44), channel_id=1, source_target_pairs={{0,8},{1,9},{2,10},{3,11},{4,12},{5,13},{6,14},{7,15},{8,0},{9,1},... | collective-permute-start | bytes 7077896 | tf_op jit(solution)/shard_map/r2/ppermute | solution.py:47
  241.8 26.6 %collective-permute-start.16 = (bf16[128,4096]{1,0:T(8,128)(2,1)}, bf16[128,4096]{1,0:T(8,128)(2,1)S(1)}, u32[]{:S(2)}, u32[]{:S(2)}) collective-permute-start(bf16[128,4096]{1,0:T(8,128)(2,1)} %get-tuple-element.67), channel_id=1, source_target_pairs={{0,3},{1,0},{2,1},{3,2},{4,7},{5,4},{6,5},{7,6},{8,11},{9,8},{10,9... | collective-permute-start | bytes 3145736 | tf_op jit(solution)/shard_map/r1/ppermute | solution.py:47
  244.4 27.5 %collective-permute-start.17 = (bf16[128,4096]{1,0:T(8,128)(2,1)}, bf16[128,4096]{1,0:T(8,128)(2,1)S(1)}, u32[]{:S(2)}, u32[]{:S(2)}) collective-permute-start(bf16[128,4096]{1,0:T(8,128)(2,1)} %get-tuple-element.68), channel_id=1, source_target_pairs={{0,1},{1,2},{2,3},{3,0},{4,5},{5,6},{6,7},{7,4},{8,9},{9,10},{10,1... | collective-permute-start | bytes 3145736 | tf_op jit(solution)/shard_map/r1/ppermute | solution.py:47
  244.5 27.5 %collective-permute-start.18 = (bf16[128,4096]{1,0:T(8,128)(2,1)}, bf16[128,4096]{1,0:T(8,128)(2,1)S(1)}, u32[]{:S(2)}, u32[]{:S(2)}) collective-permute-start(bf16[128,4096]{1,0:T(8,128)(2,1)} %get-tuple-element.69), channel_id=1, source_target_pairs={{0,2},{1,3},{2,0},{3,1},{4,6},{5,7},{6,4},{7,5},{8,10},{9,11},{10,... | collective-permute-start | bytes 3145736 | tf_op jit(solution)/shard_map/r1/ppermute | solution.py:47
  (6 other events, 10.6 us)
Sparse Core Ops, SparseCore 0:
  190.0 43.4 reduce-scatter.2
  235.9 42.0 reduce-scatter.4

commit v5 on v4

--- a/solution.py
+++ b/solution.py
@@ -90,7 +90,8 @@
         ),
         grid=(1,),
         in_specs=[pl.BlockSpec(memory_space=pltpu.SMEM)]
-        + [pl.BlockSpec((8, 512), lambda c: (16, 0))] * SIDE,
+        + [pl.BlockSpec((8, 512), lambda c: (16, 0))] * 3
+        + [pl.BlockSpec((8, 512), lambda c: (8, 0))],
         out_specs=(
             pl.BlockSpec((SIDE, ROWS, 128), lambda c: (0, 0, 0)),
             pl.BlockSpec((SIDE, SIDE, 128, SLOTS), lambda c: (0, 0, 0, 0)),
@@ -125,7 +126,7 @@
             pl.BlockSpec((SIDE, SIDE * SLOTS, 128), lambda c: (0, 0, 0)),
             pl.BlockSpec((SIDE, SIDE * SLOTS, 128), lambda c: (0, 0, 0)),
         ]
-        + [pl.BlockSpec((min(b.shape[0], 128), tile), lambda c: (0, c)) for b in blocks],
+        + [pl.BlockSpec((b.shape[0] // 64 * 64, tile), lambda c: (0, c)) for b in blocks],
         out_specs=(pl.BlockSpec((SIDE, SLOTS, tile), lambda c: (0, 0, c)),) * SIDE,
         compiler_params=PARAMS,
         cost_estimate=HEAVY,
@@ -310,26 +311,25 @@
     y, x = place >> 2, place & 3
     shifts = jnp.array(OFFSETS, jnp.int32)
     dest = jnp.where(core == 1, y * SIDE + ((x + shifts) & 3), ((y + shifts) & 3) * SIDE + x)
-    high = lax.reduce_precision(route_weight, 8, 7)
-    middle = lax.reduce_precision(route_weight - high, 8, 7)
-    low = route_weight - high - middle
+    first = lax.reduce_precision(route_weight, 8, 7)
+    second = lax.reduce_precision(route_weight - first, 8, 7)
+    third = route_weight - first - second
     meta = jnp.concatenate(
-        [m.astype(jnp.bfloat16).T for m in (expert_ids, high, middle, low)], axis=1
+        [m.astype(jnp.bfloat16).T for m in (expert_ids, first, second, third)], axis=1
     )
     message = jnp.concatenate([tokens, jnp.pad(meta, ((0, 0), (0, width - 512)))], axis=0)
 
     with jax.named_scope("p1x"):
-        token_blocks = [send(message, True, o) for o in OFFSETS]
-    cotangent = after(cotangent, *token_blocks)
+        token_blocks = [send(message, True, o) for o in OFFSETS[:3]]
+    with jax.named_scope("p1f"):
+        low, high = token_blocks[1][:64], token_blocks[2][64:]
+        token_blocks += [send(low, True, 1), send(high, True, -1)]
+    cotangent = after(cotangent, *token_blocks[:3])
     with jax.named_scope("p1g"):
-        cot_blocks = [send(cotangent, True, o) for o in OFFSETS[:3]]
-    pick, put, weight = route(dest, token_blocks)
+        cot_blocks = [send(cotangent, True, o) for o in OFFSETS]
+    pick, put, weight = route(dest, [*token_blocks[:3], token_blocks[4]])
 
     out_x = select(pick, weight, token_blocks, False)
-    with jax.named_scope("p1f"):
-        _, low, high = lax.optimization_barrier((out_x, cot_blocks[1], cot_blocks[2]))
-        cot_blocks.append(send(low[:64], True, 1))
-        cot_blocks.append(send(high[64:], True, -1))
     with jax.named_scope("p2x"):
         rx = [send(r, False, o).reshape(ROWS, width) for r, o in zip(out_x, OFFSETS)]
     out_g = select(pick, weight, cot_blocks, True)

time: 288 us -> 287 us (level)
  starting transfers between devices: 32 us -> 40.3 us
  waiting for transfers between devices: 126 us -> 119 us
    ppermute x19, starting transfers between devices: 32 us -> 40.2 us  [send(): lax.ppermute(value, BOTH, ring(first, shift))]
    ppermute x19, waiting for transfers between devices: 124 us -> 117 us  [send(): lax.ppermute(value, BOTH, ring(first, shift))]
  transfers between devices with their start and end apart: 21 -> 21, of which waited for: 15 -> 13; matrix products, arithmetic and copies ran while one was open for 2% -> 2% of each run, Pallas kernels for 34% -> 34%
where the time goes in v5:
time: 287 us; the launch traced here: 286 us
  waiting for transfers between devices  119 us (41%)
  Pallas kernels  98.6 us (34%)
  starting transfers between devices  40.3 us (14%)
  between operations  14.1 us (5%)
  other arithmetic  9.89 us (3%)
  local copies, waits for them, and re-layouts  4.67 us (2%)
    ppermute x19, waiting for transfers between devices, send(): lax.ppermute(value, BOTH, ring(first, shift))  117 us
    ppermute x19, starting transfers between devices, send(): lax.ppermute(value, BOTH, ring(first, shift))  40.2 us
    pallas_call x2, Pallas kernels, expert_back(): pl.pallas_call(functools.partial(back_kernel, n), out_shape=(jax.ShapeDty...  32.8 us
    pallas_call x2, Pallas kernels, select(): pl.pallas_call(functools.partial(select_kernel, scaled), out_shape=(jax.S...  15.5 us
    pallas_call x1, Pallas kernels, expert_pre(): pl.pallas_call(pre_kernel, out_shape=(jax.ShapeDtypeStruct((WIDE + ROWS,...  14.6 us
    pallas_call x1, Pallas kernels, up_partial(): pl.pallas_call(up_kernel, out_shape=jax.ShapeDtypeStruct((width, hidden),...  12.8 us
    pallas_call x1, Pallas kernels, down_partial(): pl.pallas_call(down_kernel, out_shape=jax.ShapeDtypeStruct((hidden, width...  12.4 us
    pallas_call x1, Pallas kernels, combine(): pl.pallas_call(combine_kernel, out_shape=(jax.ShapeDtypeStruct((128, widt...  8.23 us
  transfers between devices with their start and end apart: 21, of which 13 were waited for; matrix products, arithmetic and copies ran while one was open for 2% of the time, Pallas kernels for 34%

profile of v5, /device:TPU:0, one launch (start us, length us, event | category | flops | bytes accessed | tf_op | source)
XLA Modules:
  0.0 286.4 jit_solution(3379591819742340260)
XLA Ops:
  9.9 2.9 %collective-permute-start.1 = (bf16[136,4096]{1,0:T(8,128)(2,1)S(1)}, bf16[136,4096]{1,0:T(8,128)(2,1)S(1)}, u32[]{:S(2)}, u32[]{:S(2)}) collective-permute-start(bf16[136,4096]{1,0:T(8,128)(2,1)S(1)} %pad_maximum_fusion.m0.refs_0_), channel_id=1, source_target_pairs={{0,3},{1,0},{2,1},{3,2},{4,7},{5,4},{6,5},{7,6},{8,11},{9,8},{10,9... | collective-permute-start | bytes 3342344 | tf_op jit(solution)/shard_map/p1x/ppermute | solution.py:47
  12.8 13.0 %collective-permute-done.1.m2.refs_2_ = bf16[136,4096]{1,0:T(8,128)(2,1)S(1)} collective-permute-done((bf16[136,4096]{1,0:T(8,128)(2,1)S(1)}, bf16[136,4096]{1,0:T(8,128)(2,1)S(1)}, u32[]{:S(2)}, u32[]{:S(2)}) %collective-permute-start.1) | collective-permute-done | bytes 1114144 | tf_op jit(solution)/shard_map/p1x/ppermute | solution.py:47
  26.8 3.7 %collective-permute-start.2 = (bf16[72,4096]{1,0:T(8,128)(2,1)}, bf16[72,4096]{1,0:T(8,128)(2,1)}, u32[]{:S(2)}, u32[]{:S(2)}) collective-permute-start(bf16[72,4096]{1,0:T(8,128)(2,1)} %slice.8), channel_id=1, source_target_pairs={{0,3},{1,0},{2,1},{3,2},{4,7},{5,4},{6,5},{7,6},{8,11},{9,8},{10,9... | collective-permute-start | bytes 1769480 | tf_op jit(solution)/shard_map/p1f/ppermute | solution.py:47
  36.0 13.4 %collective-permute-done.2.m3.refs_4_ = bf16[72,4096]{1,0:T(8,128)(2,1)} collective-permute-done((bf16[72,4096]{1,0:T(8,128)(2,1)}, bf16[72,4096]{1,0:T(8,128)(2,1)}, u32[]{:S(2)}, u32[]{:S(2)}) %collective-permute-start.2) | collective-permute-done | bytes 589856 | tf_op jit(solution)/shard_map/p1f/ppermute | solution.py:47
  53.3 7.8 %select.22 = (bf16[4,72,4096]{2,1,0:T(8,128)(2,1)}, bf16[4,72,4096]{2,1,0:T(8,128)(2,1)}, bf16[4,72,4096]{2,1,0:T(8,128)(2,1)}, bf16[4,72,4096]{2,1,0:T(8,128)(2,1)}) custom-call(bf16[4,288,128]{2,1,0:T(8,128)(2,1)} %get-tuple-element.37.pick_ref, f32[4,288,128]{2,1,0:T(8,128)} %get-tuple-element.38.weight_ref, bf16[136,4096]{1,0:T(8,128)(2,1)} %copy-done.1, ...), custom_call_target="tpu_custom_call" | custom-call | flops 30000001024 | bytes 1 | tf_op jit(solution)/shard_map/select/pallas_call | solution.py:121
  61.1 3.2 %collective-permute-start.4 = (bf16[4,72,4096]{2,1,0:T(8,128)(2,1)}, bf16[4,72,4096]{2,1,0:T(8,128)(2,1)}, u32[]{:S(2)}, u32[]{:S(2)}) collective-permute-start(bf16[4,72,4096]{2,1,0:T(8,128)(2,1)} %get-tuple-element.40), channel_id=1, source_target_pairs={{0,4},{1,5},{2,6},{3,7},{4,8},{5,9},{6,10},{7,11},{8,12},{9,13},{1... | collective-permute-start | bytes 7077896 | tf_op jit(solution)/shard_map/p2x/ppermute | solution.py:47
  64.3 3.6 %collective-permute-start.6 = (bf16[4,72,4096]{2,1,0:T(8,128)(2,1)}, bf16[4,72,4096]{2,1,0:T(8,128)(2,1)}, u32[]{:S(2)}, u32[]{:S(2)}) collective-permute-start(bf16[4,72,4096]{2,1,0:T(8,128)(2,1)} %get-tuple-element.42), channel_id=1, source_target_pairs={{0,8},{1,9},{2,10},{3,11},{4,12},{5,13},{6,14},{7,15},{8,0},{9,1},... | collective-permute-start | bytes 7077896 | tf_op jit(solution)/shard_map/p2x/ppermute | solution.py:47
  67.9 7.7 %select_scaled.1 = (bf16[4,72,4096]{2,1,0:T(8,128)(2,1)}, bf16[4,72,4096]{2,1,0:T(8,128)(2,1)}, bf16[4,72,4096]{2,1,0:T(8,128)(2,1)}, bf16[4,72,4096]{2,1,0:T(8,128)(2,1)}) custom-call(bf16[4,288,128]{2,1,0:T(8,128)(2,1)} %get-tuple-element.37.pick_ref, f32[4,288,128]{2,1,0:T(8,128)} %get-tuple-element.38.weight_ref, bf16[128,4096]{1,0:T(8,128)(2,1)} %refs_0_, ...), custom_call_target="tpu_custom_call" | custom-call | flops 30000001024 | bytes 1 | tf_op jit(solution)/shard_map/select_scaled/pallas_call | solution.py:121
  75.6 11.0 %collective-permute-start.10 = (bf16[4,72,4096]{2,1,0:T(8,128)(2,1)}, bf16[4,72,4096]{2,1,0:T(8,128)(2,1)S(1)}, u32[]{:S(2)}, u32[]{:S(2)}) collective-permute-start(bf16[4,72,4096]{2,1,0:T(8,128)(2,1)} %get-tuple-element.45), channel_id=1, source_target_pairs={{0,4},{1,5},{2,6},{3,7},{4,8},{5,9},{6,10},{7,11},{8,12},{9,13},{1... | collective-permute-start | bytes 7077896 | tf_op jit(solution)/shard_map/p2g/ppermute | solution.py:47
  86.6 4.8 %collective-permute-done.4 = bf16[4,72,4096]{2,1,0:T(8,128)(2,1)} collective-permute-done((bf16[4,72,4096]{2,1,0:T(8,128)(2,1)}, bf16[4,72,4096]{2,1,0:T(8,128)(2,1)}, u32[]{:S(2)}, u32[]{:S(2)}) %collective-permute-start.4) | collective-permute-done | bytes 2359328 | tf_op jit(solution)/shard_map/p2x/ppermute | solution.py:47
  93.4 25.0 %collective-permute-done.6 = bf16[4,72,4096]{2,1,0:T(8,128)(2,1)} collective-permute-done((bf16[4,72,4096]{2,1,0:T(8,128)(2,1)}, bf16[4,72,4096]{2,1,0:T(8,128)(2,1)}, u32[]{:S(2)}, u32[]{:S(2)}) %collective-permute-start.6) | collective-permute-done | bytes 2359328 | tf_op jit(solution)/shard_map/p2x/ppermute | solution.py:47
  118.4 14.6 %expert_pre.1 = (f32[1152,768]{1,0:T(8,128)}, bf16[768,1152]{1,0:T(8,128)(2,1)}) custom-call(bf16[288,4096]{1,0:T(8,128)(2,1)} %bitcast.45, bf16[288,4096]{1,0:T(8,128)(2,1)} %bitcast.5.refs_1_.x1, bf16[288,4096]{1,0:T(8,128)(2,1)} %bitcast.6.refs_2_.x2, bf16[288,4096]{1,0:T(8,128)(2,1)} %bitcast.7.refs_3_.x3, bf16[4096,768]{1,0:T(8,128)(2,1)} %bitcast.30), custom_call_target="tpu_custom_call" | custom-call | flops 7247757312 | bytes 17498112 | tf_op jit(solution)/shard_map/expert_pre/pallas_call | solution.py:191
  133.1 8.9 %collective-permute-done.10 = bf16[4,72,4096]{2,1,0:T(8,128)(2,1)S(1)} collective-permute-done((bf16[4,72,4096]{2,1,0:T(8,128)(2,1)}, bf16[4,72,4096]{2,1,0:T(8,128)(2,1)S(1)}, u32[]{:S(2)}, u32[]{:S(2)}) %collective-permute-start.10) | collective-permute-done | bytes 2359328 | tf_op jit(solution)/shard_map/p2g/ppermute | solution.py:47
  147.2 20.4 %expert_back.2 = (bf16[864,768]{1,0:T(8,128)(2,1)}, bf16[288,4096]{1,0:T(8,128)(2,1)}, bf16[288,4096]{1,0:T(8,128)(2,1)}, bf16[288,4096]{1,0:T(8,128)(2,1)}) custom-call(bf16[288,4096]{1,0:T(8,128)(2,1)} %bitcast.35, bf16[288,4096]{1,0:T(8,128)(2,1)} %bitcast.37, bf16[288,4096]{1,0:T(8,128)(2,1)} %bitcast.39, f32[1152,768]{1,0:T(8,128)} %get-tuple-element.47.refs_3_.refs_1_, ...), custom_call_target="tpu_custom_call" | custom-call | flops 10871635968 | bytes 23101440 | tf_op jit(solution)/shard_map/expert_back/pallas_call | solution.py:239
  167.8 2.9 %collective-permute-start.13 = (bf16[4,72,4096]{2,1,0:T(8,128)(2,1)}, bf16[4,72,4096]{2,1,0:T(8,128)(2,1)}, u32[]{:S(2)}, u32[]{:S(2)}) collective-permute-start(bf16[4,72,4096]{2,1,0:T(8,128)(2,1)} %bitcast.42), channel_id=1, source_target_pairs={{0,12},{1,13},{2,14},{3,15},{4,0},{5,1},{6,2},{7,3},{8,4},{9,5},{1... | collective-permute-start | bytes 7077896 | tf_op jit(solution)/shard_map/r2/ppermute | solution.py:47
  170.8 5.2 %collective-permute-done.12 = bf16[4,72,4096]{2,1,0:T(8,128)(2,1)S(1)} collective-permute-done((bf16[4,72,4096]{2,1,0:T(8,128)(2,1)}, bf16[4,72,4096]{2,1,0:T(8,128)(2,1)S(1)}, u32[]{:S(2)}, u32[]{:S(2)}) %collective-permute-start.12) | collective-permute-done | bytes 2359328 | tf_op jit(solution)/shard_map/p2g2/ppermute | solution.py:47
  177.5 12.4 %down_partial.1 = bf16[768,4096]{1,0:T(8,128)(2,1)} custom-call(bf16[768,1152]{1,0:T(8,128)(2,1)} %get-tuple-element.55.act, bf16[288,4096]{1,0:T(8,128)(2,1)} %bitcast.36, bf16[288,4096]{1,0:T(8,128)(2,1)} %bitcast.38, bf16[288,4096]{1,0:T(8,128)(2,1)} %bitcast.40, bf16[288,4096]{1,0:T(8,128)(2,1)} %bitcast.28), custom_call_target="tpu_custom_call" | custom-call | flops 1000000 | bytes 1 | tf_op jit(solution)/shard_map/down_partial/pallas_call | solution.py:287
  190.0 12.4 %expert_back.3 = (bf16[288,768]{1,0:T(8,128)(2,1)}, bf16[288,4096]{1,0:T(8,128)(2,1)}) custom-call(bf16[288,4096]{1,0:T(8,128)(2,1)} %bitcast.29, f32[1152,768]{1,0:T(8,128)} %get-tuple-element.47.refs_3_.refs_1_, bf16[768,4096]{1,0:T(8,128)(2,1)} %bitcast.34, bf16[4096,768]{1,0:T(8,128)(2,1)} %bitcast.32), custom_call_target="tpu_custom_call" | custom-call | flops 1000000 | bytes 1 | tf_op jit(solution)/shard_map/expert_back/pallas_call | solution.py:239
  204.4 12.8 %up_partial.1 = bf16[4096,768]{1,0:T(8,128)(2,1)} custom-call(bf16[288,4096]{1,0:T(8,128)(2,1)} %bitcast.46, bf16[288,4096]{1,0:T(8,128)(2,1)} %bitcast.5.refs_1_.x1, bf16[288,4096]{1,0:T(8,128)(2,1)} %bitcast.6.refs_2_.x2, bf16[288,4096]{1,0:T(8,128)(2,1)} %bitcast.7.refs_3_.x3, bf16[864,768]{1,0:T(8,128)(2,1)} %get-tuple-element.48.grad, ...), custom_call_target="tpu_custom_call" | custom-call | flops 299999985664 | bytes 1 | tf_op jit(solution)/shard_map/up_partial/pallas_call | solution.py:267
  217.2 16.0 %collective-permute-done.15.r3 = bf16[4,72,4096]{2,1,0:T(8,128)(2,1)} collective-permute-done((bf16[4,72,4096]{2,1,0:T(8,128)(2,1)}, bf16[4,72,4096]{2,1,0:T(8,128)(2,1)}, u32[]{:S(2)}, u32[]{:S(2)}) %collective-permute-start.15) | collective-permute-done | bytes 2359328 | tf_op jit(solution)/shard_map/r2/ppermute | solution.py:47
  233.2 8.2 %combine.1 = (bf16[128,4096]{1,0:T(8,128)(2,1)}, bf16[128,4096]{1,0:T(8,128)(2,1)}, bf16[128,4096]{1,0:T(8,128)(2,1)}, bf16[128,4096]{1,0:T(8,128)(2,1)}) custom-call(bf16[4,4,128,72]{3,2,1,0:T(8,128)(2,1)} %get-tuple-element.59.put_ref, bf16[4,72,4096]{2,1,0:T(8,128)(2,1)} %bitcast.41, bf16[4,72,4096]{2,1,0:T(8,128)(2,1)} %collective-permute-done.13.r1, ...), custom_call_target="tpu_custom_call" | custom-call | flops 1000000 | bytes 1 | tf_op jit(solution)/shard_map/combine/pallas_call | solution.py:149
  246.1 21.6 %collective-permute-done.16 = bf16[128,4096]{1,0:T(8,128)(2,1)S(1)} collective-permute-done((bf16[128,4096]{1,0:T(8,128)(2,1)}, bf16[128,4096]{1,0:T(8,128)(2,1)S(1)}, u32[]{:S(2)}, u32[]{:S(2)}) %collective-permute-start.16) | collective-permute-done | bytes 1048608 | tf_op jit(solution)/shard_map/r1/ppermute | solution.py:47
  267.7 3.6 %collective-permute-done.17 = bf16[128,4096]{1,0:T(8,128)(2,1)S(1)} collective-permute-done((bf16[128,4096]{1,0:T(8,128)(2,1)}, bf16[128,4096]{1,0:T(8,128)(2,1)S(1)}, u32[]{:S(2)}, u32[]{:S(2)}) %collective-permute-start.17) | collective-permute-done | bytes 1048608 | tf_op jit(solution)/shard_map/r1/ppermute | solution.py:47
  271.3 3.0 %add_convert_fusion = bf16[128,4096]{1,0:T(8,128)(2,1)} fusion(bf16[128,4096]{1,0:T(8,128)(2,1)S(1)} %collective-permute-done.18, bf16[128,4096]{1,0:T(8,128)(2,1)S(1)} %collective-permute-done.17, bf16[128,4096]{1,0:T(8,128)(2,1)S(1)} %collective-permute-done.16, bf16[128,4096]{1,0:T(8,128)(2,1)} %get-tuple-element.62), kind=kLoop, calls=%fused_computation | loop fusion | flops 4194304 | bytes 5242880 | tf_op jit(solution)/shard_map/convert_element_type | solution.py:362
  (55 shorter events, 34.2 us)
Async XLA Ops:
  7.2 24.2 %copy-start.7 = (s32[4]{0:T(128)S(1)}, s32[4]{0:T(128)}, u32[]{:S(2)}) copy-start(s32[4]{0:T(128)} %constant.24.clone) | copy-start | bytes 52
  7.2 226.0 %reduce-scatter.3.cloned.1.call-start = ((), (), s32[]{:S(2)}) async-start(), calls=%async_computation.2 | async-start | bytes 7077888 | tf_op jit(solution)/shard_map/reduce_scatter | solution.py:348
  9.9 39.5 %copy-start.1 = (bf16[136,4096]{1,0:T(8,128)(2,1)}, bf16[136,4096]{1,0:T(8,128)(2,1)S(1)}, u32[]{:S(2)}) copy-start(bf16[136,4096]{1,0:T(8,128)(2,1)S(1)} %pad_maximum_fusion.m0.refs_0_) | copy-start | bytes 3342340
  9.9 15.9 %collective-permute-start.1 = (bf16[136,4096]{1,0:T(8,128)(2,1)S(1)}, bf16[136,4096]{1,0:T(8,128)(2,1)S(1)}, u32[]{:S(2)}, u32[]{:S(2)}) collective-permute-start(bf16[136,4096]{1,0:T(8,128)(2,1)S(1)} %pad_maximum_fusion.m0.refs_0_), channel_id=1, source_target_pairs={{0,3},{1,0},{2,1},{3,2},{4,7},{5,4},{6,5},{7,6},{8,11},{9,8},{10,9... | collective-permute-start | bytes 3342344 | tf_op jit(solution)/shard_map/p1x/ppermute | solution.py:47
  12.8 17.6 %collective-permute-start = (bf16[136,4096]{1,0:T(8,128)(2,1)S(1)}, bf16[136,4096]{1,0:T(8,128)(2,1)S(1)}, u32[]{:S(2)}, u32[]{:S(2)}) collective-permute-start(bf16[136,4096]{1,0:T(8,128)(2,1)S(1)} %pad_maximum_fusion.m0.refs_0_), channel_id=1, source_target_pairs={{0,1},{1,2},{2,3},{3,0},{4,5},{5,6},{6,7},{7,4},{8,9},{9,10},{10,1... | collective-permute-start | bytes 3342344 | tf_op jit(solution)/shard_map/p1x/ppermute | solution.py:47
  25.9 23.6 %copy-start.2 = (bf16[136,4096]{1,0:T(8,128)(2,1)}, bf16[136,4096]{1,0:T(8,128)(2,1)S(1)}, u32[]{:S(2)}) copy-start(bf16[136,4096]{1,0:T(8,128)(2,1)S(1)} %collective-permute-done.1.m2.refs_2_) | copy-start | bytes 3342340
  26.8 22.7 %collective-permute-start.2 = (bf16[72,4096]{1,0:T(8,128)(2,1)}, bf16[72,4096]{1,0:T(8,128)(2,1)}, u32[]{:S(2)}, u32[]{:S(2)}) collective-permute-start(bf16[72,4096]{1,0:T(8,128)(2,1)} %slice.8), channel_id=1, source_target_pairs={{0,3},{1,0},{2,1},{3,2},{4,7},{5,4},{6,5},{7,6},{8,11},{9,8},{10,9... | collective-permute-start | bytes 1769480 | tf_op jit(solution)/shard_map/p1f/ppermute | solution.py:47
  31.4 21.9 %collective-permute-start.3 = (bf16[64,4096]{1,0:T(8,128)(2,1)}, bf16[64,4096]{1,0:T(8,128)(2,1)}, u32[]{:S(2)}, u32[]{:S(2)}) collective-permute-start(bf16[64,4096]{1,0:T(8,128)(2,1)} %slice.9), channel_id=1, source_target_pairs={{0,1},{1,2},{2,3},{3,0},{4,5},{5,6},{6,7},{7,4},{8,9},{9,10},{10,1... | collective-permute-start | bytes 1572872 | tf_op jit(solution)/shard_map/p1f/ppermute | solution.py:47
  31.9 32.4 %collective-permute-start.9 = (bf16[128,4096]{1,0:T(8,128)(2,1)}, bf16[128,4096]{1,0:T(8,128)(2,1)}, u32[]{:S(2)}, u32[]{:S(2)}) collective-permute-start(bf16[128,4096]{1,0:T(8,128)(2,1)} %refs_0_), channel_id=1, source_target_pairs={{0,2},{1,3},{2,0},{3,1},{4,6},{5,7},{6,4},{7,5},{8,10},{9,11},{10,... | collective-permute-start | bytes 3145736 | tf_op jit(solution)/shard_map/p1g/ppermute | solution.py:47
  33.4 34.5 %collective-permute-start.8 = (bf16[128,4096]{1,0:T(8,128)(2,1)}, bf16[128,4096]{1,0:T(8,128)(2,1)}, u32[]{:S(2)}, u32[]{:S(2)}) collective-permute-start(bf16[128,4096]{1,0:T(8,128)(2,1)} %refs_0_), channel_id=1, source_target_pairs={{0,3},{1,0},{2,1},{3,2},{4,7},{5,4},{6,5},{7,6},{8,11},{9,8},{10,9... | collective-permute-start | bytes 3145736 | tf_op jit(solution)/shard_map/p1g/ppermute | solution.py:47
  35.2 32.8 %collective-permute-start.7 = (bf16[128,4096]{1,0:T(8,128)(2,1)}, bf16[128,4096]{1,0:T(8,128)(2,1)}, u32[]{:S(2)}, u32[]{:S(2)}) collective-permute-start(bf16[128,4096]{1,0:T(8,128)(2,1)} %refs_0_), channel_id=1, source_target_pairs={{0,1},{1,2},{2,3},{3,0},{4,5},{5,6},{6,7},{7,4},{8,9},{9,10},{10,1... | collective-permute-start | bytes 3145736 | tf_op jit(solution)/shard_map/p1g/ppermute | solution.py:47
  61.1 30.4 %collective-permute-start.4 = (bf16[4,72,4096]{2,1,0:T(8,128)(2,1)}, bf16[4,72,4096]{2,1,0:T(8,128)(2,1)}, u32[]{:S(2)}, u32[]{:S(2)}) collective-permute-start(bf16[4,72,4096]{2,1,0:T(8,128)(2,1)} %get-tuple-element.40), channel_id=1, source_target_pairs={{0,4},{1,5},{2,6},{3,7},{4,8},{5,9},{6,10},{7,11},{8,12},{9,13},{1... | collective-permute-start | bytes 7077896 | tf_op jit(solution)/shard_map/p2x/ppermute | solution.py:47
  64.3 29.2 %collective-permute-start.5 = (bf16[4,72,4096]{2,1,0:T(8,128)(2,1)}, bf16[4,72,4096]{2,1,0:T(8,128)(2,1)}, u32[]{:S(2)}, u32[]{:S(2)}) collective-permute-start(bf16[4,72,4096]{2,1,0:T(8,128)(2,1)} %get-tuple-element.41), channel_id=1, source_target_pairs={{0,12},{1,13},{2,14},{3,15},{4,0},{5,1},{6,2},{7,3},{8,4},{9,5},{1... | collective-permute-start | bytes 7077896 | tf_op jit(solution)/shard_map/p2x/ppermute | solution.py:47
  64.3 54.1 %collective-permute-start.6 = (bf16[4,72,4096]{2,1,0:T(8,128)(2,1)}, bf16[4,72,4096]{2,1,0:T(8,128)(2,1)}, u32[]{:S(2)}, u32[]{:S(2)}) collective-permute-start(bf16[4,72,4096]{2,1,0:T(8,128)(2,1)} %get-tuple-element.42), channel_id=1, source_target_pairs={{0,8},{1,9},{2,10},{3,11},{4,12},{5,13},{6,14},{7,15},{8,0},{9,1},... | collective-permute-start | bytes 7077896 | tf_op jit(solution)/shard_map/p2x/ppermute | solution.py:47
  75.6 66.3 %collective-permute-start.10 = (bf16[4,72,4096]{2,1,0:T(8,128)(2,1)}, bf16[4,72,4096]{2,1,0:T(8,128)(2,1)S(1)}, u32[]{:S(2)}, u32[]{:S(2)}) collective-permute-start(bf16[4,72,4096]{2,1,0:T(8,128)(2,1)} %get-tuple-element.45), channel_id=1, source_target_pairs={{0,4},{1,5},{2,6},{3,7},{4,8},{5,9},{6,10},{7,11},{8,12},{9,13},{1... | collective-permute-start | bytes 7077896 | tf_op jit(solution)/shard_map/p2g/ppermute | solution.py:47
  86.6 57.3 %collective-permute-start.11 = (bf16[4,72,4096]{2,1,0:T(8,128)(2,1)}, bf16[4,72,4096]{2,1,0:T(8,128)(2,1)S(1)}, u32[]{:S(2)}, u32[]{:S(2)}) collective-permute-start(bf16[4,72,4096]{2,1,0:T(8,128)(2,1)} %get-tuple-element.46), channel_id=1, source_target_pairs={{0,12},{1,13},{2,14},{3,15},{4,0},{5,1},{6,2},{7,3},{8,4},{9,5},{1... | collective-permute-start | bytes 7077896 | tf_op jit(solution)/shard_map/p2g/ppermute | solution.py:47
  145.3 30.7 %collective-permute-start.12 = (bf16[4,72,4096]{2,1,0:T(8,128)(2,1)}, bf16[4,72,4096]{2,1,0:T(8,128)(2,1)S(1)}, u32[]{:S(2)}, u32[]{:S(2)}) collective-permute-start(bf16[4,72,4096]{2,1,0:T(8,128)(2,1)} %get-tuple-element.50), channel_id=1, source_target_pairs={{0,8},{1,9},{2,10},{3,11},{4,12},{5,13},{6,14},{7,15},{8,0},{9,1},... | collective-permute-start | bytes 7077896 | tf_op jit(solution)/shard_map/p2g2/ppermute | solution.py:47
  167.5 34.9 %collective-permute-start.14 = (bf16[4,72,4096]{2,1,0:T(8,128)(2,1)}, bf16[4,72,4096]{2,1,0:T(8,128)(2,1)}, u32[]{:S(2)}, u32[]{:S(2)}) collective-permute-start(bf16[4,72,4096]{2,1,0:T(8,128)(2,1)} %bitcast.43), channel_id=1, source_target_pairs={{0,4},{1,5},{2,6},{3,7},{4,8},{5,9},{6,10},{7,11},{8,12},{9,13},{1... | collective-permute-start | bytes 7077896 | tf_op jit(solution)/shard_map/r2/ppermute | solution.py:47
  167.8 34.6 %collective-permute-start.13 = (bf16[4,72,4096]{2,1,0:T(8,128)(2,1)}, bf16[4,72,4096]{2,1,0:T(8,128)(2,1)}, u32[]{:S(2)}, u32[]{:S(2)}) collective-permute-start(bf16[4,72,4096]{2,1,0:T(8,128)(2,1)} %bitcast.42), channel_id=1, source_target_pairs={{0,12},{1,13},{2,14},{3,15},{4,0},{5,1},{6,2},{7,3},{8,4},{9,5},{1... | collective-permute-start | bytes 7077896 | tf_op jit(solution)/shard_map/r2/ppermute | solution.py:47
  189.9 87.3 %reduce-scatter.5.cloned.1.call-start = ((), (), s32[]{:S(2)}) async-start(), calls=%async_computation.3 | async-start | bytes 7077888 | tf_op jit(solution)/shard_map/reduce_scatter | solution.py:357
  202.4 30.7 %collective-permute-start.15 = (bf16[4,72,4096]{2,1,0:T(8,128)(2,1)}, bf16[4,72,4096]{2,1,0:T(8,128)(2,1)}, u32[]{:S(2)}, u32[]{:S(2)}) collective-permute-start(bf16[4,72,4096]{2,1,0:T(8,128)(2,1)} %bitcast.44), channel_id=1, source_target_pairs={{0,8},{1,9},{2,10},{3,11},{4,12},{5,13},{6,14},{7,15},{8,0},{9,1},... | collective-permute-start | bytes 7077896 | tf_op jit(solution)/shard_map/r2/ppermute | solution.py:47
  241.4 26.3 %collective-permute-start.16 = (bf16[128,4096]{1,0:T(8,128)(2,1)}, bf16[128,4096]{1,0:T(8,128)(2,1)S(1)}, u32[]{:S(2)}, u32[]{:S(2)}) collective-permute-start(bf16[128,4096]{1,0:T(8,128)(2,1)} %get-tuple-element.63), channel_id=1, source_target_pairs={{0,3},{1,0},{2,1},{3,2},{4,7},{5,4},{6,5},{7,6},{8,11},{9,8},{10,9... | collective-permute-start | bytes 3145736 | tf_op jit(solution)/shard_map/r1/ppermute | solution.py:47
  243.8 27.5 %collective-permute-start.17 = (bf16[128,4096]{1,0:T(8,128)(2,1)}, bf16[128,4096]{1,0:T(8,128)(2,1)S(1)}, u32[]{:S(2)}, u32[]{:S(2)}) collective-permute-start(bf16[128,4096]{1,0:T(8,128)(2,1)} %get-tuple-element.64), channel_id=1, source_target_pairs={{0,1},{1,2},{2,3},{3,0},{4,5},{5,6},{6,7},{7,4},{8,9},{9,10},{10,1... | collective-permute-start | bytes 3145736 | tf_op jit(solution)/shard_map/r1/ppermute | solution.py:47
  243.8 27.5 %collective-permute-start.18 = (bf16[128,4096]{1,0:T(8,128)(2,1)}, bf16[128,4096]{1,0:T(8,128)(2,1)S(1)}, u32[]{:S(2)}, u32[]{:S(2)}) collective-permute-start(bf16[128,4096]{1,0:T(8,128)(2,1)} %get-tuple-element.65), channel_id=1, source_target_pairs={{0,2},{1,3},{2,0},{3,1},{4,6},{5,7},{6,4},{7,5},{8,10},{9,11},{10,... | collective-permute-start | bytes 3145736 | tf_op jit(solution)/shard_map/r1/ppermute | solution.py:47
  (5 other events, 30.0 us)
Sparse Core Ops, SparseCore 0:
  190.0 42.4 reduce-scatter.2
  234.9 42.2 reduce-scatter.4

commit v6 on v5

--- a/solution.py
+++ b/solution.py
@@ -324,7 +324,7 @@
     with jax.named_scope("p1f"):
         low, high = token_blocks[1][:64], token_blocks[2][64:]
         token_blocks += [send(low, True, 1), send(high, True, -1)]
-    cotangent = after(cotangent, *token_blocks[:3])
+    cotangent = after(cotangent, *token_blocks)
     with jax.named_scope("p1g"):
         cot_blocks = [send(cotangent, True, o) for o in OFFSETS]
     pick, put, weight = route(dest, [*token_blocks[:3], token_blocks[4]])

time: 287 us -> 288 us (level)
  starting transfers between devices: 40.3 us -> 27 us
  waiting for transfers between devices: 119 us -> 132 us
    ppermute x19, starting transfers between devices: 40.2 us -> 26.9 us  [send(): lax.ppermute(value, BOTH, ring(first, shift))]
    ppermute x19, waiting for transfers between devices: 117 us -> 129 us  [send(): lax.ppermute(value, BOTH, ring(first, shift))]
  transfers between devices with their start and end apart: 21 -> 21, of which waited for: 13 -> 14; matrix products, arithmetic and copies ran while one was open for 2% -> 2% of each run, Pallas kernels for 34% -> 34%
where the time goes in v6:
time: 288 us; the launch traced here: 287 us
  waiting for transfers between devices  132 us (46%)
  Pallas kernels  98.8 us (34%)
  starting transfers between devices  27 us (9%)
  between operations  14.1 us (5%)
  other arithmetic  9.8 us (3%)
  local copies, waits for them, and re-layouts  5.14 us (2%)
    ppermute x19, waiting for transfers between devices, send(): lax.ppermute(value, BOTH, ring(first, shift))  129 us
    pallas_call x2, Pallas kernels, expert_back(): pl.pallas_call(functools.partial(back_kernel, n), out_shape=(jax.ShapeDty...  33.2 us
    ppermute x19, starting transfers between devices, send(): lax.ppermute(value, BOTH, ring(first, shift))  26.9 us
    pallas_call x2, Pallas kernels, select(): pl.pallas_call(functools.partial(select_kernel, scaled), out_shape=(jax.S...  15.5 us
    pallas_call x1, Pallas kernels, expert_pre(): pl.pallas_call(pre_kernel, out_shape=(jax.ShapeDtypeStruct((WIDE + ROWS,...  14.6 us
    pallas_call x1, Pallas kernels, up_partial(): pl.pallas_call(up_kernel, out_shape=jax.ShapeDtypeStruct((width, hidden),...  12.7 us
    pallas_call x1, Pallas kernels, down_partial(): pl.pallas_call(down_kernel, out_shape=jax.ShapeDtypeStruct((hidden, width...  12.4 us
    pallas_call x1, Pallas kernels, combine(): pl.pallas_call(combine_kernel, out_shape=(jax.ShapeDtypeStruct((128, widt...  8.23 us
  transfers between devices with their start and end apart: 21, of which 14 were waited for; matrix products, arithmetic and copies ran while one was open for 2% of the time, Pallas kernels for 34%

profile of v6, /device:TPU:0, one launch (start us, length us, event | category | flops | bytes accessed | tf_op | source)
XLA Modules:
  0.0 287.1 jit_solution(7628440718109635954)
XLA Ops:
  9.9 2.9 %collective-permute-start.1 = (bf16[136,4096]{1,0:T(8,128)(2,1)S(1)}, bf16[136,4096]{1,0:T(8,128)(2,1)S(1)}, u32[]{:S(2)}, u32[]{:S(2)}) collective-permute-start(bf16[136,4096]{1,0:T(8,128)(2,1)S(1)} %pad_maximum_fusion.m0.refs_0_), channel_id=1, source_target_pairs={{0,3},{1,0},{2,1},{3,2},{4,7},{5,4},{6,5},{7,6},{8,11},{9,8},{10,9... | collective-permute-start | bytes 3342344 | tf_op jit(solution)/shard_map/p1x/ppermute | solution.py:47
  12.8 13.0 %collective-permute-done.1.m2.refs_2_ = bf16[136,4096]{1,0:T(8,128)(2,1)S(1)} collective-permute-done((bf16[136,4096]{1,0:T(8,128)(2,1)S(1)}, bf16[136,4096]{1,0:T(8,128)(2,1)S(1)}, u32[]{:S(2)}, u32[]{:S(2)}) %collective-permute-start.1) | collective-permute-done | bytes 1114144 | tf_op jit(solution)/shard_map/p1x/ppermute | solution.py:47
  26.8 3.7 %collective-permute-start.2 = (bf16[72,4096]{1,0:T(8,128)(2,1)}, bf16[72,4096]{1,0:T(8,128)(2,1)}, u32[]{:S(2)}, u32[]{:S(2)}) collective-permute-start(bf16[72,4096]{1,0:T(8,128)(2,1)} %slice.8), channel_id=1, source_target_pairs={{0,3},{1,0},{2,1},{3,2},{4,7},{5,4},{6,5},{7,6},{8,11},{9,8},{10,9... | collective-permute-start | bytes 1769480 | tf_op jit(solution)/shard_map/p1f/ppermute | solution.py:47
  31.9 10.2 %collective-permute-done.3.refs_3_ = bf16[64,4096]{1,0:T(8,128)(2,1)} collective-permute-done((bf16[64,4096]{1,0:T(8,128)(2,1)}, bf16[64,4096]{1,0:T(8,128)(2,1)}, u32[]{:S(2)}, u32[]{:S(2)}) %collective-permute-start.3) | collective-permute-done | bytes 524320 | tf_op jit(solution)/shard_map/p1f/ppermute | solution.py:47
  46.3 7.8 %select.22 = (bf16[4,72,4096]{2,1,0:T(8,128)(2,1)}, bf16[4,72,4096]{2,1,0:T(8,128)(2,1)}, bf16[4,72,4096]{2,1,0:T(8,128)(2,1)}, bf16[4,72,4096]{2,1,0:T(8,128)(2,1)}) custom-call(bf16[4,288,128]{2,1,0:T(8,128)(2,1)} %get-tuple-element.37.pick_ref, f32[4,288,128]{2,1,0:T(8,128)} %get-tuple-element.38.weight_ref, bf16[136,4096]{1,0:T(8,128)(2,1)} %copy-done.1, ...), custom_call_target="tpu_custom_call" | custom-call | flops 30000001024 | bytes 1 | tf_op jit(solution)/shard_map/select/pallas_call | solution.py:121
  57.3 3.6 %collective-permute-done.9.refs_3_ = bf16[128,4096]{1,0:T(8,128)(2,1)} collective-permute-done((bf16[128,4096]{1,0:T(8,128)(2,1)}, bf16[128,4096]{1,0:T(8,128)(2,1)}, u32[]{:S(2)}, u32[]{:S(2)}) %collective-permute-start.9) | collective-permute-done | bytes 1048608 | tf_op jit(solution)/shard_map/p1g/ppermute | solution.py:47
  60.9 3.2 %collective-permute-start.6 = (bf16[4,72,4096]{2,1,0:T(8,128)(2,1)}, bf16[4,72,4096]{2,1,0:T(8,128)(2,1)}, u32[]{:S(2)}, u32[]{:S(2)}) collective-permute-start(bf16[4,72,4096]{2,1,0:T(8,128)(2,1)} %get-tuple-element.42), channel_id=1, source_target_pairs={{0,8},{1,9},{2,10},{3,11},{4,12},{5,13},{6,14},{7,15},{8,0},{9,1},... | collective-permute-start | bytes 7077896 | tf_op jit(solution)/shard_map/p2x/ppermute | solution.py:47
  64.1 14.8 %collective-permute-done.8.refs_2_ = bf16[128,4096]{1,0:T(8,128)(2,1)} collective-permute-done((bf16[128,4096]{1,0:T(8,128)(2,1)}, bf16[128,4096]{1,0:T(8,128)(2,1)}, u32[]{:S(2)}, u32[]{:S(2)}) %collective-permute-start.8) | collective-permute-done | bytes 1048608 | tf_op jit(solution)/shard_map/p1g/ppermute | solution.py:47
  81.1 7.7 %select_scaled.1 = (bf16[4,72,4096]{2,1,0:T(8,128)(2,1)}, bf16[4,72,4096]{2,1,0:T(8,128)(2,1)}, bf16[4,72,4096]{2,1,0:T(8,128)(2,1)}, bf16[4,72,4096]{2,1,0:T(8,128)(2,1)}) custom-call(bf16[4,288,128]{2,1,0:T(8,128)(2,1)} %get-tuple-element.37.pick_ref, f32[4,288,128]{2,1,0:T(8,128)} %get-tuple-element.38.weight_ref, bf16[128,4096]{1,0:T(8,128)(2,1)} %refs_0_, ...), custom_call_target="tpu_custom_call" | custom-call | flops 30000001024 | bytes 1 | tf_op jit(solution)/shard_map/select_scaled/pallas_call | solution.py:121
  92.3 25.4 %collective-permute-done.6 = bf16[4,72,4096]{2,1,0:T(8,128)(2,1)} collective-permute-done((bf16[4,72,4096]{2,1,0:T(8,128)(2,1)}, bf16[4,72,4096]{2,1,0:T(8,128)(2,1)}, u32[]{:S(2)}, u32[]{:S(2)}) %collective-permute-start.6) | collective-permute-done | bytes 2359328 | tf_op jit(solution)/shard_map/p2x/ppermute | solution.py:47
  117.8 14.6 %expert_pre.1 = (f32[1152,768]{1,0:T(8,128)}, bf16[768,1152]{1,0:T(8,128)(2,1)}) custom-call(bf16[288,4096]{1,0:T(8,128)(2,1)} %bitcast.45, bf16[288,4096]{1,0:T(8,128)(2,1)} %bitcast.5.refs_1_.x1, bf16[288,4096]{1,0:T(8,128)(2,1)} %bitcast.6.refs_2_.x2, bf16[288,4096]{1,0:T(8,128)(2,1)} %bitcast.7.refs_3_.x3, bf16[4096,768]{1,0:T(8,128)(2,1)} %bitcast.30), custom_call_target="tpu_custom_call" | custom-call | flops 7247757312 | bytes 17498112 | tf_op jit(solution)/shard_map/expert_pre/pallas_call | solution.py:191
  132.4 10.4 %collective-permute-done.10 = bf16[4,72,4096]{2,1,0:T(8,128)(2,1)S(1)} collective-permute-done((bf16[4,72,4096]{2,1,0:T(8,128)(2,1)}, bf16[4,72,4096]{2,1,0:T(8,128)(2,1)S(1)}, u32[]{:S(2)}, u32[]{:S(2)}) %collective-permute-start.10) | collective-permute-done | bytes 2359328 | tf_op jit(solution)/shard_map/p2g/ppermute | solution.py:47
  145.0 20.4 %expert_back.2 = (bf16[864,768]{1,0:T(8,128)(2,1)}, bf16[288,4096]{1,0:T(8,128)(2,1)}, bf16[288,4096]{1,0:T(8,128)(2,1)}, bf16[288,4096]{1,0:T(8,128)(2,1)}) custom-call(bf16[288,4096]{1,0:T(8,128)(2,1)} %bitcast.35, bf16[288,4096]{1,0:T(8,128)(2,1)} %bitcast.37, bf16[288,4096]{1,0:T(8,128)(2,1)} %bitcast.39, f32[1152,768]{1,0:T(8,128)} %get-tuple-element.47.refs_3_.refs_1_, ...), custom_call_target="tpu_custom_call" | custom-call | flops 10871635968 | bytes 23101440 | tf_op jit(solution)/shard_map/expert_back/pallas_call | solution.py:239
  166.1 2.5 collective-permute-start.13
  168.6 6.3 %collective-permute-done.12 = bf16[4,72,4096]{2,1,0:T(8,128)(2,1)S(1)} collective-permute-done((bf16[4,72,4096]{2,1,0:T(8,128)(2,1)}, bf16[4,72,4096]{2,1,0:T(8,128)(2,1)S(1)}, u32[]{:S(2)}, u32[]{:S(2)}) %collective-permute-start.12) | collective-permute-done | bytes 2359328 | tf_op jit(solution)/shard_map/p2g2/ppermute | solution.py:47
  176.4 12.4 %down_partial.1 = bf16[768,4096]{1,0:T(8,128)(2,1)} custom-call(bf16[768,1152]{1,0:T(8,128)(2,1)} %get-tuple-element.55.act, bf16[288,4096]{1,0:T(8,128)(2,1)} %bitcast.36, bf16[288,4096]{1,0:T(8,128)(2,1)} %bitcast.38, bf16[288,4096]{1,0:T(8,128)(2,1)} %bitcast.40, bf16[288,4096]{1,0:T(8,128)(2,1)} %bitcast.28), custom_call_target="tpu_custom_call" | custom-call | flops 1000000 | bytes 1 | tf_op jit(solution)/shard_map/down_partial/pallas_call | solution.py:287
  188.9 12.8 %expert_back.3 = (bf16[288,768]{1,0:T(8,128)(2,1)}, bf16[288,4096]{1,0:T(8,128)(2,1)}) custom-call(bf16[288,4096]{1,0:T(8,128)(2,1)} %bitcast.29, f32[1152,768]{1,0:T(8,128)} %get-tuple-element.47.refs_3_.refs_1_, bf16[768,4096]{1,0:T(8,128)(2,1)} %bitcast.34, bf16[4096,768]{1,0:T(8,128)(2,1)} %bitcast.32), custom_call_target="tpu_custom_call" | custom-call | flops 1000000 | bytes 1 | tf_op jit(solution)/shard_map/expert_back/pallas_call | solution.py:239
  201.8 12.7 %up_partial.1 = bf16[4096,768]{1,0:T(8,128)(2,1)} custom-call(bf16[288,4096]{1,0:T(8,128)(2,1)} %bitcast.46, bf16[288,4096]{1,0:T(8,128)(2,1)} %bitcast.5.refs_1_.x1, bf16[288,4096]{1,0:T(8,128)(2,1)} %bitcast.6.refs_2_.x2, bf16[288,4096]{1,0:T(8,128)(2,1)} %bitcast.7.refs_3_.x3, bf16[864,768]{1,0:T(8,128)(2,1)} %get-tuple-element.48.grad, ...), custom_call_target="tpu_custom_call" | custom-call | flops 299999985664 | bytes 1 | tf_op jit(solution)/shard_map/up_partial/pallas_call | solution.py:267
  214.5 18.0 %collective-permute-done.15.r3 = bf16[4,72,4096]{2,1,0:T(8,128)(2,1)} collective-permute-done((bf16[4,72,4096]{2,1,0:T(8,128)(2,1)}, bf16[4,72,4096]{2,1,0:T(8,128)(2,1)}, u32[]{:S(2)}, u32[]{:S(2)}) %collective-permute-start.15) | collective-permute-done | bytes 2359328 | tf_op jit(solution)/shard_map/r2/ppermute | solution.py:47
  233.5 8.2 %combine.1 = (bf16[128,4096]{1,0:T(8,128)(2,1)}, bf16[128,4096]{1,0:T(8,128)(2,1)}, bf16[128,4096]{1,0:T(8,128)(2,1)}, bf16[128,4096]{1,0:T(8,128)(2,1)}) custom-call(bf16[4,4,128,72]{3,2,1,0:T(8,128)(2,1)} %get-tuple-element.59.put_ref, bf16[4,72,4096]{2,1,0:T(8,128)(2,1)} %bitcast.41, bf16[4,72,4096]{2,1,0:T(8,128)(2,1)} %collective-permute-done.13.r1, ...), custom_call_target="tpu_custom_call" | custom-call | flops 1000000 | bytes 1 | tf_op jit(solution)/shard_map/combine/pallas_call | solution.py:149
  241.7 2.7 collective-permute-start.16
  246.7 21.6 %collective-permute-done.16 = bf16[128,4096]{1,0:T(8,128)(2,1)S(1)} collective-permute-done((bf16[128,4096]{1,0:T(8,128)(2,1)}, bf16[128,4096]{1,0:T(8,128)(2,1)S(1)}, u32[]{:S(2)}, u32[]{:S(2)}) %collective-permute-start.16) | collective-permute-done | bytes 1048608 | tf_op jit(solution)/shard_map/r1/ppermute | solution.py:47
  268.3 3.6 %collective-permute-done.17 = bf16[128,4096]{1,0:T(8,128)(2,1)S(1)} collective-permute-done((bf16[128,4096]{1,0:T(8,128)(2,1)}, bf16[128,4096]{1,0:T(8,128)(2,1)S(1)}, u32[]{:S(2)}, u32[]{:S(2)}) %collective-permute-start.17) | collective-permute-done | bytes 1048608 | tf_op jit(solution)/shard_map/r1/ppermute | solution.py:47
  271.9 3.0 %add_convert_fusion = bf16[128,4096]{1,0:T(8,128)(2,1)} fusion(bf16[128,4096]{1,0:T(8,128)(2,1)S(1)} %collective-permute-done.18, bf16[128,4096]{1,0:T(8,128)(2,1)S(1)} %collective-permute-done.17, bf16[128,4096]{1,0:T(8,128)(2,1)S(1)} %collective-permute-done.16, bf16[128,4096]{1,0:T(8,128)(2,1)} %get-tuple-element.62), kind=kLoop, calls=%fused_computation | loop fusion | flops 4194304 | bytes 5242880 | tf_op jit(solution)/shard_map/convert_element_type | solution.py:362
  (55 shorter events, 31.4 us)
Async XLA Ops:
  7.2 24.2 %copy-start.7 = (s32[4]{0:T(128)S(1)}, s32[4]{0:T(128)}, u32[]{:S(2)}) copy-start(s32[4]{0:T(128)} %constant.24.clone) | copy-start | bytes 52
  7.2 226.3 %reduce-scatter.3.cloned.1.call-start = ((), (), s32[]{:S(2)}) async-start(), calls=%async_computation.2 | async-start | bytes 7077888 | tf_op jit(solution)/shard_map/reduce_scatter | solution.py:348
  9.9 34.2 %copy-start.1 = (bf16[136,4096]{1,0:T(8,128)(2,1)}, bf16[136,4096]{1,0:T(8,128)(2,1)S(1)}, u32[]{:S(2)}) copy-start(bf16[136,4096]{1,0:T(8,128)(2,1)S(1)} %pad_maximum_fusion.m0.refs_0_) | copy-start | bytes 3342340
  9.9 15.9 %collective-permute-start.1 = (bf16[136,4096]{1,0:T(8,128)(2,1)S(1)}, bf16[136,4096]{1,0:T(8,128)(2,1)S(1)}, u32[]{:S(2)}, u32[]{:S(2)}) collective-permute-start(bf16[136,4096]{1,0:T(8,128)(2,1)S(1)} %pad_maximum_fusion.m0.refs_0_), channel_id=1, source_target_pairs={{0,3},{1,0},{2,1},{3,2},{4,7},{5,4},{6,5},{7,6},{8,11},{9,8},{10,9... | collective-permute-start | bytes 3342344 | tf_op jit(solution)/shard_map/p1x/ppermute | solution.py:47
  12.8 17.6 %collective-permute-start = (bf16[136,4096]{1,0:T(8,128)(2,1)S(1)}, bf16[136,4096]{1,0:T(8,128)(2,1)S(1)}, u32[]{:S(2)}, u32[]{:S(2)}) collective-permute-start(bf16[136,4096]{1,0:T(8,128)(2,1)S(1)} %pad_maximum_fusion.m0.refs_0_), channel_id=1, source_target_pairs={{0,1},{1,2},{2,3},{3,0},{4,5},{5,6},{6,7},{7,4},{8,9},{9,10},{10,1... | collective-permute-start | bytes 3342344 | tf_op jit(solution)/shard_map/p1x/ppermute | solution.py:47
  25.9 18.3 %copy-start.2 = (bf16[136,4096]{1,0:T(8,128)(2,1)}, bf16[136,4096]{1,0:T(8,128)(2,1)S(1)}, u32[]{:S(2)}) copy-start(bf16[136,4096]{1,0:T(8,128)(2,1)S(1)} %collective-permute-done.1.m2.refs_2_) | copy-start | bytes 3342340
  26.8 15.3 %collective-permute-start.2 = (bf16[72,4096]{1,0:T(8,128)(2,1)}, bf16[72,4096]{1,0:T(8,128)(2,1)}, u32[]{:S(2)}, u32[]{:S(2)}) collective-permute-start(bf16[72,4096]{1,0:T(8,128)(2,1)} %slice.8), channel_id=1, source_target_pairs={{0,3},{1,0},{2,1},{3,2},{4,7},{5,4},{6,5},{7,6},{8,11},{9,8},{10,9... | collective-permute-start | bytes 1769480 | tf_op jit(solution)/shard_map/p1f/ppermute | solution.py:47
  31.4 10.7 %collective-permute-start.3 = (bf16[64,4096]{1,0:T(8,128)(2,1)}, bf16[64,4096]{1,0:T(8,128)(2,1)}, u32[]{:S(2)}, u32[]{:S(2)}) collective-permute-start(bf16[64,4096]{1,0:T(8,128)(2,1)} %slice.9), channel_id=1, source_target_pairs={{0,1},{1,2},{2,3},{3,0},{4,5},{5,6},{6,7},{7,4},{8,9},{9,10},{10,1... | collective-permute-start | bytes 1572872 | tf_op jit(solution)/shard_map/p1f/ppermute | solution.py:47
  42.1 18.9 %collective-permute-start.9 = (bf16[128,4096]{1,0:T(8,128)(2,1)}, bf16[128,4096]{1,0:T(8,128)(2,1)}, u32[]{:S(2)}, u32[]{:S(2)}) collective-permute-start(bf16[128,4096]{1,0:T(8,128)(2,1)} %refs_0_), channel_id=1, source_target_pairs={{0,2},{1,3},{2,0},{3,1},{4,6},{5,7},{6,4},{7,5},{8,10},{9,11},{10,... | collective-permute-start | bytes 3145736 | tf_op jit(solution)/shard_map/p1g/ppermute | solution.py:47
  42.1 36.9 %collective-permute-start.8 = (bf16[128,4096]{1,0:T(8,128)(2,1)}, bf16[128,4096]{1,0:T(8,128)(2,1)}, u32[]{:S(2)}, u32[]{:S(2)}) collective-permute-start(bf16[128,4096]{1,0:T(8,128)(2,1)} %refs_0_), channel_id=1, source_target_pairs={{0,3},{1,0},{2,1},{3,2},{4,7},{5,4},{6,5},{7,6},{8,11},{9,8},{10,9... | collective-permute-start | bytes 3145736 | tf_op jit(solution)/shard_map/p1g/ppermute | solution.py:47
  43.5 37.5 %collective-permute-start.7 = (bf16[128,4096]{1,0:T(8,128)(2,1)}, bf16[128,4096]{1,0:T(8,128)(2,1)}, u32[]{:S(2)}, u32[]{:S(2)}) collective-permute-start(bf16[128,4096]{1,0:T(8,128)(2,1)} %refs_0_), channel_id=1, source_target_pairs={{0,1},{1,2},{2,3},{3,0},{4,5},{5,6},{6,7},{7,4},{8,9},{9,10},{10,1... | collective-permute-start | bytes 3145736 | tf_op jit(solution)/shard_map/p1g/ppermute | solution.py:47
  54.1 38.3 %collective-permute-start.4 = (bf16[4,72,4096]{2,1,0:T(8,128)(2,1)}, bf16[4,72,4096]{2,1,0:T(8,128)(2,1)}, u32[]{:S(2)}, u32[]{:S(2)}) collective-permute-start(bf16[4,72,4096]{2,1,0:T(8,128)(2,1)} %get-tuple-element.40), channel_id=1, source_target_pairs={{0,4},{1,5},{2,6},{3,7},{4,8},{5,9},{6,10},{7,11},{8,12},{9,13},{1... | collective-permute-start | bytes 7077896 | tf_op jit(solution)/shard_map/p2x/ppermute | solution.py:47
  55.6 36.7 %collective-permute-start.5 = (bf16[4,72,4096]{2,1,0:T(8,128)(2,1)}, bf16[4,72,4096]{2,1,0:T(8,128)(2,1)}, u32[]{:S(2)}, u32[]{:S(2)}) collective-permute-start(bf16[4,72,4096]{2,1,0:T(8,128)(2,1)} %get-tuple-element.41), channel_id=1, source_target_pairs={{0,12},{1,13},{2,14},{3,15},{4,0},{5,1},{6,2},{7,3},{8,4},{9,5},{1... | collective-permute-start | bytes 7077896 | tf_op jit(solution)/shard_map/p2x/ppermute | solution.py:47
  60.9 56.8 %collective-permute-start.6 = (bf16[4,72,4096]{2,1,0:T(8,128)(2,1)}, bf16[4,72,4096]{2,1,0:T(8,128)(2,1)}, u32[]{:S(2)}, u32[]{:S(2)}) collective-permute-start(bf16[4,72,4096]{2,1,0:T(8,128)(2,1)} %get-tuple-element.42), channel_id=1, source_target_pairs={{0,8},{1,9},{2,10},{3,11},{4,12},{5,13},{6,14},{7,15},{8,0},{9,1},... | collective-permute-start | bytes 7077896 | tf_op jit(solution)/shard_map/p2x/ppermute | solution.py:47
  88.8 54.1 %collective-permute-start.10 = (bf16[4,72,4096]{2,1,0:T(8,128)(2,1)}, bf16[4,72,4096]{2,1,0:T(8,128)(2,1)S(1)}, u32[]{:S(2)}, u32[]{:S(2)}) collective-permute-start(bf16[4,72,4096]{2,1,0:T(8,128)(2,1)} %get-tuple-element.45), channel_id=1, source_target_pairs={{0,4},{1,5},{2,6},{3,7},{4,8},{5,9},{6,10},{7,11},{8,12},{9,13},{1... | collective-permute-start | bytes 7077896 | tf_op jit(solution)/shard_map/p2g/ppermute | solution.py:47
  90.3 52.5 %collective-permute-start.11 = (bf16[4,72,4096]{2,1,0:T(8,128)(2,1)}, bf16[4,72,4096]{2,1,0:T(8,128)(2,1)S(1)}, u32[]{:S(2)}, u32[]{:S(2)}) collective-permute-start(bf16[4,72,4096]{2,1,0:T(8,128)(2,1)} %get-tuple-element.46), channel_id=1, source_target_pairs={{0,12},{1,13},{2,14},{3,15},{4,0},{5,1},{6,2},{7,3},{8,4},{9,5},{1... | collective-permute-start | bytes 7077896 | tf_op jit(solution)/shard_map/p2g/ppermute | solution.py:47
  144.3 30.7 %collective-permute-start.12 = (bf16[4,72,4096]{2,1,0:T(8,128)(2,1)}, bf16[4,72,4096]{2,1,0:T(8,128)(2,1)S(1)}, u32[]{:S(2)}, u32[]{:S(2)}) collective-permute-start(bf16[4,72,4096]{2,1,0:T(8,128)(2,1)} %get-tuple-element.50), channel_id=1, source_target_pairs={{0,8},{1,9},{2,10},{3,11},{4,12},{5,13},{6,14},{7,15},{8,0},{9,1},... | collective-permute-start | bytes 7077896 | tf_op jit(solution)/shard_map/p2g2/ppermute | solution.py:47
  165.4 36.3 %collective-permute-start.14 = (bf16[4,72,4096]{2,1,0:T(8,128)(2,1)}, bf16[4,72,4096]{2,1,0:T(8,128)(2,1)}, u32[]{:S(2)}, u32[]{:S(2)}) collective-permute-start(bf16[4,72,4096]{2,1,0:T(8,128)(2,1)} %bitcast.43), channel_id=1, source_target_pairs={{0,4},{1,5},{2,6},{3,7},{4,8},{5,9},{6,10},{7,11},{8,12},{9,13},{1... | collective-permute-start | bytes 7077896 | tf_op jit(solution)/shard_map/r2/ppermute | solution.py:47
  166.1 35.5 %collective-permute-start.13 = (bf16[4,72,4096]{2,1,0:T(8,128)(2,1)}, bf16[4,72,4096]{2,1,0:T(8,128)(2,1)}, u32[]{:S(2)}, u32[]{:S(2)}) collective-permute-start(bf16[4,72,4096]{2,1,0:T(8,128)(2,1)} %bitcast.42), channel_id=1, source_target_pairs={{0,12},{1,13},{2,14},{3,15},{4,0},{5,1},{6,2},{7,3},{8,4},{9,5},{1... | collective-permute-start | bytes 7077896 | tf_op jit(solution)/shard_map/r2/ppermute | solution.py:47
  188.8 89.0 %reduce-scatter.5.cloned.1.call-start = ((), (), s32[]{:S(2)}) async-start(), calls=%async_computation.3 | async-start | bytes 7077888 | tf_op jit(solution)/shard_map/reduce_scatter | solution.py:357
  201.7 30.7 %collective-permute-start.15 = (bf16[4,72,4096]{2,1,0:T(8,128)(2,1)}, bf16[4,72,4096]{2,1,0:T(8,128)(2,1)}, u32[]{:S(2)}, u32[]{:S(2)}) collective-permute-start(bf16[4,72,4096]{2,1,0:T(8,128)(2,1)} %bitcast.44), channel_id=1, source_target_pairs={{0,8},{1,9},{2,10},{3,11},{4,12},{5,13},{6,14},{7,15},{8,0},{9,1},... | collective-permute-start | bytes 7077896 | tf_op jit(solution)/shard_map/r2/ppermute | solution.py:47
  241.7 26.6 %collective-permute-start.16 = (bf16[128,4096]{1,0:T(8,128)(2,1)}, bf16[128,4096]{1,0:T(8,128)(2,1)S(1)}, u32[]{:S(2)}, u32[]{:S(2)}) collective-permute-start(bf16[128,4096]{1,0:T(8,128)(2,1)} %get-tuple-element.63), channel_id=1, source_target_pairs={{0,3},{1,0},{2,1},{3,2},{4,7},{5,4},{6,5},{7,6},{8,11},{9,8},{10,9... | collective-permute-start | bytes 3145736 | tf_op jit(solution)/shard_map/r1/ppermute | solution.py:47
  244.4 27.5 %collective-permute-start.17 = (bf16[128,4096]{1,0:T(8,128)(2,1)}, bf16[128,4096]{1,0:T(8,128)(2,1)S(1)}, u32[]{:S(2)}, u32[]{:S(2)}) collective-permute-start(bf16[128,4096]{1,0:T(8,128)(2,1)} %get-tuple-element.64), channel_id=1, source_target_pairs={{0,1},{1,2},{2,3},{3,0},{4,5},{5,6},{6,7},{7,4},{8,9},{9,10},{10,1... | collective-permute-start | bytes 3145736 | tf_op jit(solution)/shard_map/r1/ppermute | solution.py:47
  244.4 27.5 %collective-permute-start.18 = (bf16[128,4096]{1,0:T(8,128)(2,1)}, bf16[128,4096]{1,0:T(8,128)(2,1)S(1)}, u32[]{:S(2)}, u32[]{:S(2)}) collective-permute-start(bf16[128,4096]{1,0:T(8,128)(2,1)} %get-tuple-element.65), channel_id=1, source_target_pairs={{0,2},{1,3},{2,0},{3,1},{4,6},{5,7},{6,4},{7,5},{8,10},{9,11},{10,... | collective-permute-start | bytes 3145736 | tf_op jit(solution)/shard_map/r1/ppermute | solution.py:47
  (5 other events, 21.6 us)
Sparse Core Ops, SparseCore 0:
  188.9 44.4 reduce-scatter.2
  235.9 41.9 reduce-scatter.4

commit v7 on v4

--- a/solution.py
+++ b/solution.py
@@ -101,12 +101,10 @@
     )(dest, *blocks)
 
 
-def select_kernel(scaled, pick_ref, weight_ref, *refs):
-    blocks, outs = [r[...] for r in refs[:-SIDE]], refs[-SIDE:]
-    if len(blocks) > SIDE:
-        blocks[3:] = [jnp.concatenate(blocks[3:], axis=0)]
-    for i, block in enumerate(blocks):
-        rows = jnp.dot(pick_ref[i], block, preferred_element_type=jnp.float32)
+def select_kernel(scaled, pick_ref, weight_ref, b0, b1, b2, b3, o0, o1, o2, o3):
+    outs = (o0, o1, o2, o3)
+    for i, block in enumerate((b0, b1, b2, b3)):
+        rows = jnp.dot(pick_ref[i], block[...], preferred_element_type=jnp.float32)
         if scaled:
             rows = rows * weight_ref[i][:, 0:1]
         rows = rows.astype(jnp.bfloat16)
@@ -125,7 +123,7 @@
             pl.BlockSpec((SIDE, SIDE * SLOTS, 128), lambda c: (0, 0, 0)),
             pl.BlockSpec((SIDE, SIDE * SLOTS, 128), lambda c: (0, 0, 0)),
         ]
-        + [pl.BlockSpec((min(b.shape[0], 128), tile), lambda c: (0, c)) for b in blocks],
+        + [pl.BlockSpec((128, tile), lambda c: (0, c))] * SIDE,
         out_specs=(pl.BlockSpec((SIDE, SLOTS, tile), lambda c: (0, 0, c)),) * SIDE,
         compiler_params=PARAMS,
         cost_estimate=HEAVY,
@@ -322,14 +320,10 @@
         token_blocks = [send(message, True, o) for o in OFFSETS]
     cotangent = after(cotangent, *token_blocks)
     with jax.named_scope("p1g"):
-        cot_blocks = [send(cotangent, True, o) for o in OFFSETS[:3]]
+        cot_blocks = [send(cotangent, True, o) for o in OFFSETS]
     pick, put, weight = route(dest, token_blocks)
 
     out_x = select(pick, weight, token_blocks, False)
-    with jax.named_scope("p1f"):
-        _, low, high = lax.optimization_barrier((out_x, cot_blocks[1], cot_blocks[2]))
-        cot_blocks.append(send(low[:64], True, 1))
-        cot_blocks.append(send(high[64:], True, -1))
     with jax.named_scope("p2x"):
         rx = [send(r, False, o).reshape(ROWS, width) for r, o in zip(out_x, OFFSETS)]
     out_g = select(pick, weight, cot_blocks, True)
@@ -337,7 +331,7 @@
         rg = [send(r, False, o).reshape(ROWS, width) for r, o in zip(out_g[:3], OFFSETS)]
     pre, act = expert_pre(rx, up_matrix)
     with jax.named_scope("p2g2"):
-        last = send(after(out_g[3], pre, *rx, *rg), False, OFFSETS[3]).reshape(ROWS, width)
+        last = send(after(out_g[3], pre, *rx), False, OFFSETS[3]).reshape(ROWS, width)
 
     grad, rows = expert_back(rg, pre, 0, down_matrix, up_matrix)
     with jax.named_scope("r2"):

time: 288 us -> 282 us (0.979)
  waiting for transfers between devices: 126 us -> 122 us
  local copies, waits for them, and re-layouts: 5.79 us -> 2.77 us
    ppermute x19 -> x18, waiting for transfers between devices: 124 us -> 116 us  [send(): lax.ppermute(value, BOTH, ring(first, shift))]
    ppermute x19 -> x18, starting transfers between devices: 32 us -> 33.9 us  [send(): lax.ppermute(value, BOTH, ring(first, shift))]
  transfers between devices with their start and end apart: 21 -> 20, of which waited for: 15 -> 17; matrix products, arithmetic and copies ran while one was open for 2% -> 2% of each run, Pallas kernels for 34% -> 35%
where the time goes in v7:
time: 282 us; the launch traced here: 281 us
  waiting for transfers between devices  122 us (43%)
  Pallas kernels  98.2 us (35%)
  starting transfers between devices  34 us (12%)
  between operations  14.1 us (5%)
  other arithmetic  10.5 us (4%)
    ppermute x18, waiting for transfers between devices, send(): lax.ppermute(value, BOTH, ring(first, shift))  116 us
    ppermute x18, starting transfers between devices, send(): lax.ppermute(value, BOTH, ring(first, shift))  33.9 us
    pallas_call x2, Pallas kernels, expert_back(): pl.pallas_call(functools.partial(back_kernel, n), out_shape=(jax.ShapeDty...  32.7 us
    pallas_call x2, Pallas kernels, select(): pl.pallas_call(functools.partial(select_kernel, scaled), out_shape=(jax.S...  15.4 us
    pallas_call x1, Pallas kernels, expert_pre(): pl.pallas_call(pre_kernel, out_shape=(jax.ShapeDtypeStruct((WIDE + ROWS,...  14.5 us
    pallas_call x1, Pallas kernels, up_partial(): pl.pallas_call(up_kernel, out_shape=jax.ShapeDtypeStruct((width, hidden),...  12.7 us
    pallas_call x1, Pallas kernels, down_partial(): pl.pallas_call(down_kernel, out_shape=jax.ShapeDtypeStruct((hidden, width...  12.5 us
    pallas_call x1, Pallas kernels, combine(): pl.pallas_call(combine_kernel, out_shape=(jax.ShapeDtypeStruct((128, widt...  8.24 us
  transfers between devices with their start and end apart: 20, of which 17 were waited for; matrix products, arithmetic and copies ran while one was open for 2% of the time, Pallas kernels for 35%

profile of v7, /device:TPU:0, one launch (start us, length us, event | category | flops | bytes accessed | tf_op | source)
XLA Modules:
  0.0 281.3 jit_solution(7956467912021368245)
XLA Ops:
  9.9 3.2 %collective-permute-start.2 = (bf16[136,4096]{1,0:T(8,128)(2,1)S(1)}, bf16[136,4096]{1,0:T(8,128)(2,1)S(1)}, u32[]{:S(2)}, u32[]{:S(2)}) collective-permute-start(bf16[136,4096]{1,0:T(8,128)(2,1)S(1)} %pad_maximum_fusion.m0.b0), channel_id=1, source_target_pairs={{0,2},{1,3},{2,0},{3,1},{4,6},{5,7},{6,4},{7,5},{8,10},{9,11},{10,... | collective-permute-start | bytes 3342344 | tf_op jit(solution)/shard_map/p1x/ppermute | solution.py:47
  16.3 10.8 %collective-permute-done.2.m3.b3 = bf16[136,4096]{1,0:T(8,128)(2,1)S(1)} collective-permute-done((bf16[136,4096]{1,0:T(8,128)(2,1)S(1)}, bf16[136,4096]{1,0:T(8,128)(2,1)S(1)}, u32[]{:S(2)}, u32[]{:S(2)}) %collective-permute-start.2) | collective-permute-done | bytes 1114144 | tf_op jit(solution)/shard_map/p1x/ppermute | solution.py:47
  27.1 12.0 %collective-permute-done.1.m2.b2 = bf16[136,4096]{1,0:T(8,128)(2,1)S(1)} collective-permute-done((bf16[136,4096]{1,0:T(8,128)(2,1)S(1)}, bf16[136,4096]{1,0:T(8,128)(2,1)S(1)}, u32[]{:S(2)}, u32[]{:S(2)}) %collective-permute-start.1) | collective-permute-done | bytes 1114144 | tf_op jit(solution)/shard_map/p1x/ppermute | solution.py:47
  39.2 3.0 %collective-permute-start.8 = (bf16[128,4096]{1,0:T(8,128)(2,1)}, bf16[128,4096]{1,0:T(8,128)(2,1)}, u32[]{:S(2)}, u32[]{:S(2)}) collective-permute-start(bf16[128,4096]{1,0:T(8,128)(2,1)} %b0), channel_id=1, source_target_pairs={{0,2},{1,3},{2,0},{3,1},{4,6},{5,7},{6,4},{7,5},{8,10},{9,11},{10,... | collective-permute-start | bytes 3145736 | tf_op jit(solution)/shard_map/p1g/ppermute | solution.py:47
  46.3 7.7 %select.22 = (bf16[4,72,4096]{2,1,0:T(8,128)(2,1)}, bf16[4,72,4096]{2,1,0:T(8,128)(2,1)}, bf16[4,72,4096]{2,1,0:T(8,128)(2,1)}, bf16[4,72,4096]{2,1,0:T(8,128)(2,1)}) custom-call(bf16[4,288,128]{2,1,0:T(8,128)(2,1)} %get-tuple-element.37.pick_ref, f32[4,288,128]{2,1,0:T(8,128)} %get-tuple-element.38.weight_ref, bf16[136,4096]{1,0:T(8,128)(2,1)} %copy-done.1, ...), custom_call_target="tpu_custom_call" | custom-call | flops 30000001024 | bytes 1 | tf_op jit(solution)/shard_map/select/pallas_call | solution.py:118
  57.3 3.5 %collective-permute-start.5 = (bf16[4,72,4096]{2,1,0:T(8,128)(2,1)}, bf16[4,72,4096]{2,1,0:T(8,128)(2,1)}, u32[]{:S(2)}, u32[]{:S(2)}) collective-permute-start(bf16[4,72,4096]{2,1,0:T(8,128)(2,1)} %get-tuple-element.42), channel_id=1, source_target_pairs={{0,8},{1,9},{2,10},{3,11},{4,12},{5,13},{6,14},{7,15},{8,0},{9,1},... | collective-permute-start | bytes 7077896 | tf_op jit(solution)/shard_map/p2x/ppermute | solution.py:47
  60.8 16.7 %collective-permute-done.7.b2 = bf16[128,4096]{1,0:T(8,128)(2,1)} collective-permute-done((bf16[128,4096]{1,0:T(8,128)(2,1)}, bf16[128,4096]{1,0:T(8,128)(2,1)}, u32[]{:S(2)}, u32[]{:S(2)}) %collective-permute-start.7) | collective-permute-done | bytes 1048608 | tf_op jit(solution)/shard_map/p1g/ppermute | solution.py:47
  77.8 7.7 %select_scaled.1 = (bf16[4,72,4096]{2,1,0:T(8,128)(2,1)}, bf16[4,72,4096]{2,1,0:T(8,128)(2,1)}, bf16[4,72,4096]{2,1,0:T(8,128)(2,1)}, bf16[4,72,4096]{2,1,0:T(8,128)(2,1)}) custom-call(bf16[4,288,128]{2,1,0:T(8,128)(2,1)} %get-tuple-element.37.pick_ref, f32[4,288,128]{2,1,0:T(8,128)} %get-tuple-element.38.weight_ref, bf16[128,4096]{1,0:T(8,128)(2,1)} %b0, ...), custom_call_target="tpu_custom_call" | custom-call | flops 30000001024 | bytes 1 | tf_op jit(solution)/shard_map/select_scaled/pallas_call | solution.py:118
  85.5 2.9 %collective-permute-start.9 = (bf16[4,72,4096]{2,1,0:T(8,128)(2,1)}, bf16[4,72,4096]{2,1,0:T(8,128)(2,1)S(1)}, u32[]{:S(2)}, u32[]{:S(2)}) collective-permute-start(bf16[4,72,4096]{2,1,0:T(8,128)(2,1)} %get-tuple-element.45), channel_id=1, source_target_pairs={{0,4},{1,5},{2,6},{3,7},{4,8},{5,9},{6,10},{7,11},{8,12},{9,13},{1... | collective-permute-start | bytes 7077896 | tf_op jit(solution)/shard_map/p2g/ppermute | solution.py:47
  90.7 25.4 %collective-permute-done.5 = bf16[4,72,4096]{2,1,0:T(8,128)(2,1)} collective-permute-done((bf16[4,72,4096]{2,1,0:T(8,128)(2,1)}, bf16[4,72,4096]{2,1,0:T(8,128)(2,1)}, u32[]{:S(2)}, u32[]{:S(2)}) %collective-permute-start.5) | collective-permute-done | bytes 2359328 | tf_op jit(solution)/shard_map/p2x/ppermute | solution.py:47
  116.1 14.5 %expert_pre.1 = (f32[1152,768]{1,0:T(8,128)}, bf16[768,1152]{1,0:T(8,128)(2,1)}) custom-call(bf16[288,4096]{1,0:T(8,128)(2,1)} %bitcast.45, bf16[288,4096]{1,0:T(8,128)(2,1)} %bitcast.40, bf16[288,4096]{1,0:T(8,128)(2,1)} %bitcast.6.refs_2_.x2, bf16[288,4096]{1,0:T(8,128)(2,1)} %bitcast.7.refs_3_.x3, bf16[4096,768]{1,0:T(8,128)(2,1)} %bitcast.30), custom_call_target="tpu_custom_call" | custom-call | flops 7247757312 | bytes 17498112 | tf_op jit(solution)/shard_map/expert_pre/pallas_call | solution.py:188
  130.6 2.8 collective-permute-start.11
  133.4 7.8 %collective-permute-done.9 = bf16[4,72,4096]{2,1,0:T(8,128)(2,1)S(1)} collective-permute-done((bf16[4,72,4096]{2,1,0:T(8,128)(2,1)}, bf16[4,72,4096]{2,1,0:T(8,128)(2,1)S(1)}, u32[]{:S(2)}, u32[]{:S(2)}) %collective-permute-start.9) | collective-permute-done | bytes 2359328 | tf_op jit(solution)/shard_map/p2g/ppermute | solution.py:47
  142.6 20.4 %expert_back.2 = (bf16[864,768]{1,0:T(8,128)(2,1)}, bf16[288,4096]{1,0:T(8,128)(2,1)}, bf16[288,4096]{1,0:T(8,128)(2,1)}, bf16[288,4096]{1,0:T(8,128)(2,1)}) custom-call(bf16[288,4096]{1,0:T(8,128)(2,1)} %bitcast.35, bf16[288,4096]{1,0:T(8,128)(2,1)} %bitcast.37, bf16[288,4096]{1,0:T(8,128)(2,1)} %bitcast.10.refs_2_.g2, ...), custom_call_target="tpu_custom_call" | custom-call | flops 10871635968 | bytes 23101440 | tf_op jit(solution)/shard_map/expert_back/pallas_call | solution.py:236
  167.9 12.5 %down_partial.1 = bf16[768,4096]{1,0:T(8,128)(2,1)} custom-call(bf16[768,1152]{1,0:T(8,128)(2,1)} %get-tuple-element.55.act, bf16[288,4096]{1,0:T(8,128)(2,1)} %bitcast.36, bf16[288,4096]{1,0:T(8,128)(2,1)} %bitcast.38, bf16[288,4096]{1,0:T(8,128)(2,1)} %bitcast.10.refs_2_.g2, bf16[288,4096]{1,0:T(8,128)(2,1)} %bitcast.28), custom_call_target="tpu_custom_call" | custom-call | flops 1000000 | bytes 1 | tf_op jit(solution)/shard_map/down_partial/pallas_call | solution.py:284
  180.4 12.4 %expert_back.3 = (bf16[288,768]{1,0:T(8,128)(2,1)}, bf16[288,4096]{1,0:T(8,128)(2,1)}) custom-call(bf16[288,4096]{1,0:T(8,128)(2,1)} %bitcast.29, f32[1152,768]{1,0:T(8,128)} %get-tuple-element.47.refs_3_.refs_1_, bf16[768,4096]{1,0:T(8,128)(2,1)} %bitcast.34, bf16[4096,768]{1,0:T(8,128)(2,1)} %bitcast.32), custom_call_target="tpu_custom_call" | custom-call | flops 1000000 | bytes 1 | tf_op jit(solution)/shard_map/expert_back/pallas_call | solution.py:236
  195.7 12.7 %up_partial.1 = bf16[4096,768]{1,0:T(8,128)(2,1)} custom-call(bf16[288,4096]{1,0:T(8,128)(2,1)} %bitcast.46, bf16[288,4096]{1,0:T(8,128)(2,1)} %bitcast.41, bf16[288,4096]{1,0:T(8,128)(2,1)} %bitcast.6.refs_2_.x2, bf16[288,4096]{1,0:T(8,128)(2,1)} %bitcast.7.refs_3_.x3, bf16[864,768]{1,0:T(8,128)(2,1)} %get-tuple-element.48.grad, ...), custom_call_target="tpu_custom_call" | custom-call | flops 299999985664 | bytes 1 | tf_op jit(solution)/shard_map/up_partial/pallas_call | solution.py:264
  208.4 15.7 %collective-permute-done.14.r3 = bf16[4,72,4096]{2,1,0:T(8,128)(2,1)} collective-permute-done((bf16[4,72,4096]{2,1,0:T(8,128)(2,1)}, bf16[4,72,4096]{2,1,0:T(8,128)(2,1)}, u32[]{:S(2)}, u32[]{:S(2)}) %collective-permute-start.14) | collective-permute-done | bytes 2359328 | tf_op jit(solution)/shard_map/r2/ppermute | solution.py:47
  224.1 3.3 %reduce-scatter.3.cloned.1.call-done = bf16[96,4096]{1,0:T(8,128)(2,1)} async-done(((bf16[768,4096]{1,0:T(8,128)(2,1)}), bf16[96,4096]{1,0:T(8,128)(2,1)}) %reduce-scatter.3.cloned.1.call-update) | async-done | bytes 786448 | tf_op jit(solution)/shard_map/reduce_scatter | solution.py:342
  227.4 8.2 %combine.1 = (bf16[128,4096]{1,0:T(8,128)(2,1)}, bf16[128,4096]{1,0:T(8,128)(2,1)}, bf16[128,4096]{1,0:T(8,128)(2,1)}, bf16[128,4096]{1,0:T(8,128)(2,1)}) custom-call(bf16[4,4,128,72]{3,2,1,0:T(8,128)(2,1)} %get-tuple-element.59.put_ref, bf16[4,72,4096]{2,1,0:T(8,128)(2,1)} %bitcast.39, bf16[4,72,4096]{2,1,0:T(8,128)(2,1)} %collective-permute-done.12.r1, ...), custom_call_target="tpu_custom_call" | custom-call | flops 1000000 | bytes 1 | tf_op jit(solution)/shard_map/combine/pallas_call | solution.py:146
  235.7 2.7 collective-permute-start.15
  240.7 21.6 %collective-permute-done.15 = bf16[128,4096]{1,0:T(8,128)(2,1)S(1)} collective-permute-done((bf16[128,4096]{1,0:T(8,128)(2,1)}, bf16[128,4096]{1,0:T(8,128)(2,1)S(1)}, u32[]{:S(2)}, u32[]{:S(2)}) %collective-permute-start.15) | collective-permute-done | bytes 1048608 | tf_op jit(solution)/shard_map/r1/ppermute | solution.py:47
  262.2 3.6 %collective-permute-done.16 = bf16[128,4096]{1,0:T(8,128)(2,1)S(1)} collective-permute-done((bf16[128,4096]{1,0:T(8,128)(2,1)}, bf16[128,4096]{1,0:T(8,128)(2,1)S(1)}, u32[]{:S(2)}, u32[]{:S(2)}) %collective-permute-start.16) | collective-permute-done | bytes 1048608 | tf_op jit(solution)/shard_map/r1/ppermute | solution.py:47
  265.8 2.9 %add_convert_fusion = bf16[128,4096]{1,0:T(8,128)(2,1)} fusion(bf16[128,4096]{1,0:T(8,128)(2,1)S(1)} %collective-permute-done.17, bf16[128,4096]{1,0:T(8,128)(2,1)S(1)} %collective-permute-done.16, bf16[128,4096]{1,0:T(8,128)(2,1)S(1)} %collective-permute-done.15, bf16[128,4096]{1,0:T(8,128)(2,1)} %get-tuple-element.62), kind=kLoop, calls=%fused_computation | loop fusion | flops 4194304 | bytes 5242880 | tf_op jit(solution)/shard_map/convert_element_type | solution.py:356
  (49 shorter events, 33.3 us)
Async XLA Ops:
  7.2 220.2 %reduce-scatter.3.cloned.1.call-start = ((), (), s32[]{:S(2)}) async-start(), calls=%async_computation.2 | async-start | bytes 7077888 | tf_op jit(solution)/shard_map/reduce_scatter | solution.py:342
  9.9 34.3 %copy-start.1 = (bf16[136,4096]{1,0:T(8,128)(2,1)}, bf16[136,4096]{1,0:T(8,128)(2,1)S(1)}, u32[]{:S(2)}) copy-start(bf16[136,4096]{1,0:T(8,128)(2,1)S(1)} %pad_maximum_fusion.m0.b0) | copy-start | bytes 3342340
  9.9 17.2 %collective-permute-start.2 = (bf16[136,4096]{1,0:T(8,128)(2,1)S(1)}, bf16[136,4096]{1,0:T(8,128)(2,1)S(1)}, u32[]{:S(2)}, u32[]{:S(2)}) collective-permute-start(bf16[136,4096]{1,0:T(8,128)(2,1)S(1)} %pad_maximum_fusion.m0.b0), channel_id=1, source_target_pairs={{0,2},{1,3},{2,0},{3,1},{4,6},{5,7},{6,4},{7,5},{8,10},{9,11},{10,... | collective-permute-start | bytes 3342344 | tf_op jit(solution)/shard_map/p1x/ppermute | solution.py:47
  13.1 26.0 %collective-permute-start.1 = (bf16[136,4096]{1,0:T(8,128)(2,1)S(1)}, bf16[136,4096]{1,0:T(8,128)(2,1)S(1)}, u32[]{:S(2)}, u32[]{:S(2)}) collective-permute-start(bf16[136,4096]{1,0:T(8,128)(2,1)S(1)} %pad_maximum_fusion.m0.b0), channel_id=1, source_target_pairs={{0,3},{1,0},{2,1},{3,2},{4,7},{5,4},{6,5},{7,6},{8,11},{9,8},{10,9... | collective-permute-start | bytes 3342344 | tf_op jit(solution)/shard_map/p1x/ppermute | solution.py:47
  14.2 24.9 %collective-permute-start = (bf16[136,4096]{1,0:T(8,128)(2,1)S(1)}, bf16[136,4096]{1,0:T(8,128)(2,1)}, u32[]{:S(2)}, u32[]{:S(2)}) collective-permute-start(bf16[136,4096]{1,0:T(8,128)(2,1)S(1)} %pad_maximum_fusion.m0.b0), channel_id=1, source_target_pairs={{0,1},{1,2},{2,3},{3,0},{4,5},{5,6},{6,7},{7,4},{8,9},{9,10},{10,1... | collective-permute-start | bytes 3342344 | tf_op jit(solution)/shard_map/p1x/ppermute | solution.py:47
  27.1 17.1 %copy-start.3 = (bf16[136,4096]{1,0:T(8,128)(2,1)}, bf16[136,4096]{1,0:T(8,128)(2,1)S(1)}, u32[]{:S(2)}) copy-start(bf16[136,4096]{1,0:T(8,128)(2,1)S(1)} %collective-permute-done.2.m3.b3) | copy-start | bytes 3342340
  39.1 5.0 %copy-start.4 = (bf16[136,4096]{1,0:T(8,128)(2,1)}, bf16[136,4096]{1,0:T(8,128)(2,1)S(1)}, u32[]{:S(2)}) copy-start(bf16[136,4096]{1,0:T(8,128)(2,1)S(1)} %collective-permute-done.1.m2.b2) | copy-start | bytes 3342340
  39.2 18.1 %collective-permute-start.8 = (bf16[128,4096]{1,0:T(8,128)(2,1)}, bf16[128,4096]{1,0:T(8,128)(2,1)}, u32[]{:S(2)}, u32[]{:S(2)}) collective-permute-start(bf16[128,4096]{1,0:T(8,128)(2,1)} %b0), channel_id=1, source_target_pairs={{0,2},{1,3},{2,0},{3,1},{4,6},{5,7},{6,4},{7,5},{8,10},{9,11},{10,... | collective-permute-start | bytes 3145736 | tf_op jit(solution)/shard_map/p1g/ppermute | solution.py:47
  42.1 35.3 %collective-permute-start.7 = (bf16[128,4096]{1,0:T(8,128)(2,1)}, bf16[128,4096]{1,0:T(8,128)(2,1)}, u32[]{:S(2)}, u32[]{:S(2)}) collective-permute-start(bf16[128,4096]{1,0:T(8,128)(2,1)} %b0), channel_id=1, source_target_pairs={{0,3},{1,0},{2,1},{3,2},{4,7},{5,4},{6,5},{7,6},{8,11},{9,8},{10,9... | collective-permute-start | bytes 3145736 | tf_op jit(solution)/shard_map/p1g/ppermute | solution.py:47
  43.4 34.4 %collective-permute-start.6 = (bf16[128,4096]{1,0:T(8,128)(2,1)}, bf16[128,4096]{1,0:T(8,128)(2,1)}, u32[]{:S(2)}, u32[]{:S(2)}) collective-permute-start(bf16[128,4096]{1,0:T(8,128)(2,1)} %b0), channel_id=1, source_target_pairs={{0,1},{1,2},{2,3},{3,0},{4,5},{5,6},{6,7},{7,4},{8,9},{9,10},{10,1... | collective-permute-start | bytes 3145736 | tf_op jit(solution)/shard_map/p1g/ppermute | solution.py:47
  54.0 36.5 %collective-permute-start.3 = (bf16[4,72,4096]{2,1,0:T(8,128)(2,1)}, bf16[4,72,4096]{2,1,0:T(8,128)(2,1)S(1)}, u32[]{:S(2)}, u32[]{:S(2)}) collective-permute-start(bf16[4,72,4096]{2,1,0:T(8,128)(2,1)} %get-tuple-element.40), channel_id=1, source_target_pairs={{0,4},{1,5},{2,6},{3,7},{4,8},{5,9},{6,10},{7,11},{8,12},{9,13},{1... | collective-permute-start | bytes 7077896 | tf_op jit(solution)/shard_map/p2x/ppermute | solution.py:47
  55.6 35.0 %collective-permute-start.4 = (bf16[4,72,4096]{2,1,0:T(8,128)(2,1)}, bf16[4,72,4096]{2,1,0:T(8,128)(2,1)}, u32[]{:S(2)}, u32[]{:S(2)}) collective-permute-start(bf16[4,72,4096]{2,1,0:T(8,128)(2,1)} %get-tuple-element.41), channel_id=1, source_target_pairs={{0,12},{1,13},{2,14},{3,15},{4,0},{5,1},{6,2},{7,3},{8,4},{9,5},{1... | collective-permute-start | bytes 7077896 | tf_op jit(solution)/shard_map/p2x/ppermute | solution.py:47
  57.3 58.8 %collective-permute-start.5 = (bf16[4,72,4096]{2,1,0:T(8,128)(2,1)}, bf16[4,72,4096]{2,1,0:T(8,128)(2,1)}, u32[]{:S(2)}, u32[]{:S(2)}) collective-permute-start(bf16[4,72,4096]{2,1,0:T(8,128)(2,1)} %get-tuple-element.42), channel_id=1, source_target_pairs={{0,8},{1,9},{2,10},{3,11},{4,12},{5,13},{6,14},{7,15},{8,0},{9,1},... | collective-permute-start | bytes 7077896 | tf_op jit(solution)/shard_map/p2x/ppermute | solution.py:47
  85.5 55.7 %collective-permute-start.9 = (bf16[4,72,4096]{2,1,0:T(8,128)(2,1)}, bf16[4,72,4096]{2,1,0:T(8,128)(2,1)S(1)}, u32[]{:S(2)}, u32[]{:S(2)}) collective-permute-start(bf16[4,72,4096]{2,1,0:T(8,128)(2,1)} %get-tuple-element.45), channel_id=1, source_target_pairs={{0,4},{1,5},{2,6},{3,7},{4,8},{5,9},{6,10},{7,11},{8,12},{9,13},{1... | collective-permute-start | bytes 7077896 | tf_op jit(solution)/shard_map/p2g/ppermute | solution.py:47
  88.4 52.9 %collective-permute-start.10 = (bf16[4,72,4096]{2,1,0:T(8,128)(2,1)}, bf16[4,72,4096]{2,1,0:T(8,128)(2,1)}, u32[]{:S(2)}, u32[]{:S(2)}) collective-permute-start(bf16[4,72,4096]{2,1,0:T(8,128)(2,1)} %get-tuple-element.46), channel_id=1, source_target_pairs={{0,12},{1,13},{2,14},{3,15},{4,0},{5,1},{6,2},{7,3},{8,4},{9,5},{1... | collective-permute-start | bytes 7077896 | tf_op jit(solution)/shard_map/p2g/ppermute | solution.py:47
  90.6 25.5 %copy-start.6 = (bf16[4,72,4096]{2,1,0:T(8,128)(2,1)}, bf16[4,72,4096]{2,1,0:T(8,128)(2,1)S(1)}, u32[]{:S(2)}) copy-start(bf16[4,72,4096]{2,1,0:T(8,128)(2,1)S(1)} %collective-permute-done.3) | copy-start | bytes 7077892
  130.6 35.9 %collective-permute-start.11 = (bf16[4,72,4096]{2,1,0:T(8,128)(2,1)}, bf16[4,72,4096]{2,1,0:T(8,128)(2,1)S(1)}, u32[]{:S(2)}, u32[]{:S(2)}) collective-permute-start(bf16[4,72,4096]{2,1,0:T(8,128)(2,1)} %get-tuple-element.50), channel_id=1, source_target_pairs={{0,8},{1,9},{2,10},{3,11},{4,12},{5,13},{6,14},{7,15},{8,0},{9,1},... | collective-permute-start | bytes 7077896 | tf_op jit(solution)/shard_map/p2g2/ppermute | solution.py:47
  162.9 30.4 %collective-permute-start.13 = (bf16[4,72,4096]{2,1,0:T(8,128)(2,1)}, bf16[4,72,4096]{2,1,0:T(8,128)(2,1)}, u32[]{:S(2)}, u32[]{:S(2)}) collective-permute-start(bf16[4,72,4096]{2,1,0:T(8,128)(2,1)} %bitcast.43), channel_id=1, source_target_pairs={{0,4},{1,5},{2,6},{3,7},{4,8},{5,9},{6,10},{7,11},{8,12},{9,13},{1... | collective-permute-start | bytes 7077896 | tf_op jit(solution)/shard_map/r2/ppermute | solution.py:47
  164.3 29.2 %collective-permute-start.12 = (bf16[4,72,4096]{2,1,0:T(8,128)(2,1)}, bf16[4,72,4096]{2,1,0:T(8,128)(2,1)}, u32[]{:S(2)}, u32[]{:S(2)}) collective-permute-start(bf16[4,72,4096]{2,1,0:T(8,128)(2,1)} %bitcast.42), channel_id=1, source_target_pairs={{0,12},{1,13},{2,14},{3,15},{4,0},{5,1},{6,2},{7,3},{8,4},{9,5},{1... | collective-permute-start | bytes 7077896 | tf_op jit(solution)/shard_map/r2/ppermute | solution.py:47
  180.4 91.6 %reduce-scatter.5.cloned.1.call-start = ((), (), s32[]{:S(2)}) async-start(), calls=%async_computation.3 | async-start | bytes 7077888 | tf_op jit(solution)/shard_map/reduce_scatter | solution.py:351
  193.5 30.7 %collective-permute-start.14 = (bf16[4,72,4096]{2,1,0:T(8,128)(2,1)}, bf16[4,72,4096]{2,1,0:T(8,128)(2,1)}, u32[]{:S(2)}, u32[]{:S(2)}) collective-permute-start(bf16[4,72,4096]{2,1,0:T(8,128)(2,1)} %bitcast.44), channel_id=1, source_target_pairs={{0,8},{1,9},{2,10},{3,11},{4,12},{5,13},{6,14},{7,15},{8,0},{9,1},... | collective-permute-start | bytes 7077896 | tf_op jit(solution)/shard_map/r2/ppermute | solution.py:47
  235.7 26.6 %collective-permute-start.15 = (bf16[128,4096]{1,0:T(8,128)(2,1)}, bf16[128,4096]{1,0:T(8,128)(2,1)S(1)}, u32[]{:S(2)}, u32[]{:S(2)}) collective-permute-start(bf16[128,4096]{1,0:T(8,128)(2,1)} %get-tuple-element.63), channel_id=1, source_target_pairs={{0,3},{1,0},{2,1},{3,2},{4,7},{5,4},{6,5},{7,6},{8,11},{9,8},{10,9... | collective-permute-start | bytes 3145736 | tf_op jit(solution)/shard_map/r1/ppermute | solution.py:47
  238.3 27.5 %collective-permute-start.16 = (bf16[128,4096]{1,0:T(8,128)(2,1)}, bf16[128,4096]{1,0:T(8,128)(2,1)S(1)}, u32[]{:S(2)}, u32[]{:S(2)}) collective-permute-start(bf16[128,4096]{1,0:T(8,128)(2,1)} %get-tuple-element.64), channel_id=1, source_target_pairs={{0,1},{1,2},{2,3},{3,0},{4,5},{5,6},{6,7},{7,4},{8,9},{9,10},{10,1... | collective-permute-start | bytes 3145736 | tf_op jit(solution)/shard_map/r1/ppermute | solution.py:47
  238.3 27.5 %collective-permute-start.17 = (bf16[128,4096]{1,0:T(8,128)(2,1)}, bf16[128,4096]{1,0:T(8,128)(2,1)S(1)}, u32[]{:S(2)}, u32[]{:S(2)}) collective-permute-start(bf16[128,4096]{1,0:T(8,128)(2,1)} %get-tuple-element.65), channel_id=1, source_target_pairs={{0,2},{1,3},{2,0},{3,1},{4,6},{5,7},{6,4},{7,5},{8,10},{9,11},{10,... | collective-permute-start | bytes 3145736 | tf_op jit(solution)/shard_map/r1/ppermute | solution.py:47
  (3 other events, 5.8 us)
Sparse Core Ops, SparseCore 0:
  180.5 46.8 reduce-scatter.2
  229.8 42.1 reduce-scatter.4

commit v8 on v7

--- a/solution.py
+++ b/solution.py
@@ -254,8 +254,8 @@
     return out[0], list(out[1:])
 
 
-def up_kernel(x0, x1, x2, x3, grad, grad_last, out):
-    total = dot(stacked((x0, x1, x2, x3)), stacked((grad, grad_last)), ROWS_FIRST)
+def up_kernel(x0, x1, x2, x3, p0, p1, p2, out):
+    total = dot(stacked((x0, x1, x2, x3)), stacked((p0, p1, p2)), ROWS_FIRST)
     out[...] = total.astype(jnp.bfloat16)
 
 
@@ -329,11 +329,15 @@
     out_g = select(pick, weight, cot_blocks, True)
     with jax.named_scope("p2g"):
         rg = [send(r, False, o).reshape(ROWS, width) for r, o in zip(out_g[:3], OFFSETS)]
+    rx = [rx[1], rx[2], rx[0], rx[3]]
     pre, act = expert_pre(rx, up_matrix)
     with jax.named_scope("p2g2"):
         last = send(after(out_g[3], pre, *rx), False, OFFSETS[3]).reshape(ROWS, width)
 
-    grad, rows = expert_back(rg, pre, 0, down_matrix, up_matrix)
+    grad_own, (rows_own,) = expert_back([rg[0]], pre, 2, down_matrix, up_matrix)
+    rg = [after(rg[1], rows_own), rg[2], rg[0]]
+    grad, rows = expert_back(rg[:2], pre, 0, down_matrix, up_matrix)
+    rows = [rows_own, *rows]
     with jax.named_scope("r2"):
         returned = [send(r.reshape(SIDE, SLOTS, width), False, -o) for r, o in zip(rows, OFFSETS)]
 
@@ -346,7 +350,7 @@
         rows_last = after(rows_last[0], *returned).reshape(SIDE, SLOTS, width)
         returned.append(send(rows_last, False, -OFFSETS[3]))
     grad_last = after(grad_last, *returned[:3])
-    up_part = up_partial(rx, [grad, grad_last])
+    up_part = up_partial(rx, [grad, grad_own, grad_last])
     up_done, up_part = up_part, after(up_part, down_grad, returned[3])
     up_grad = lax.psum_scatter(up_part, "dp", scatter_dimension=0, tiled=True)
 

time: 282 us -> 282 us (level)
  waiting for transfers between devices: 122 us -> 114 us
  Pallas kernels: 98.2 us -> 106 us
    ppermute x18, waiting for transfers between devices: 116 us -> 108 us  [send(): lax.ppermute(value, BOTH, ring(first, shift))]
    pallas_call x2 -> x3, Pallas kernels: 32.7 us -> 40.7 us  [expert_back(): pl.pallas_call(functools.partial(back_kernel, n), out_shape=(jax.ShapeDty...]
  transfers between devices with their start and end apart: 20 -> 20, of which waited for: 17 -> 14; matrix products, arithmetic and copies ran while one was open for 2% -> 2% of each run, Pallas kernels for 35% -> 38%
where the time goes in v8:
time: 282 us; the launch traced here: 281 us
  waiting for transfers between devices  114 us (40%)
  Pallas kernels  106 us (38%)
  starting transfers between devices  34.1 us (12%)
  between operations  14.1 us (5%)
  other arithmetic  10.5 us (4%)
  local copies, waits for them, and re-layouts  2.87 us (1%)
    ppermute x18, waiting for transfers between devices, send(): lax.ppermute(value, BOTH, ring(first, shift))  108 us
    pallas_call x3, Pallas kernels, expert_back(): pl.pallas_call(functools.partial(back_kernel, n), out_shape=(jax.ShapeDty...  40.7 us
    ppermute x18, starting transfers between devices, send(): lax.ppermute(value, BOTH, ring(first, shift))  34 us
    pallas_call x2, Pallas kernels, select(): pl.pallas_call(functools.partial(select_kernel, scaled), out_shape=(jax.S...  15.3 us
    pallas_call x1, Pallas kernels, expert_pre(): pl.pallas_call(pre_kernel, out_shape=(jax.ShapeDtypeStruct((WIDE + ROWS,...  14.5 us
    pallas_call x1, Pallas kernels, up_partial(): pl.pallas_call(up_kernel, out_shape=jax.ShapeDtypeStruct((width, hidden),...  12.7 us
    pallas_call x1, Pallas kernels, down_partial(): pl.pallas_call(down_kernel, out_shape=jax.ShapeDtypeStruct((hidden, width...  12.4 us
    pallas_call x1, Pallas kernels, combine(): pl.pallas_call(combine_kernel, out_shape=(jax.ShapeDtypeStruct((128, widt...  8.22 us
  transfers between devices with their start and end apart: 20, of which 14 were waited for; matrix products, arithmetic and copies ran while one was open for 2% of the time, Pallas kernels for 38%

profile of v8, /device:TPU:0, one launch (start us, length us, event | category | flops | bytes accessed | tf_op | source)
XLA Modules:
  0.0 281.3 jit_solution(14149972849000887241)
XLA Ops:
  9.9 3.2 %collective-permute-start.2 = (bf16[136,4096]{1,0:T(8,128)(2,1)S(1)}, bf16[136,4096]{1,0:T(8,128)(2,1)S(1)}, u32[]{:S(2)}, u32[]{:S(2)}) collective-permute-start(bf16[136,4096]{1,0:T(8,128)(2,1)S(1)} %pad_maximum_fusion.m0.b0), channel_id=1, source_target_pairs={{0,2},{1,3},{2,0},{3,1},{4,6},{5,7},{6,4},{7,5},{8,10},{9,11},{10,... | collective-permute-start | bytes 3342344 | tf_op jit(solution)/shard_map/p1x/ppermute | solution.py:47
  16.4 10.7 %collective-permute-done.2.m3.b3 = bf16[136,4096]{1,0:T(8,128)(2,1)S(1)} collective-permute-done((bf16[136,4096]{1,0:T(8,128)(2,1)S(1)}, bf16[136,4096]{1,0:T(8,128)(2,1)S(1)}, u32[]{:S(2)}, u32[]{:S(2)}) %collective-permute-start.2) | collective-permute-done | bytes 1114144 | tf_op jit(solution)/shard_map/p1x/ppermute | solution.py:47
  27.1 12.0 %collective-permute-done.1.m2.b2 = bf16[136,4096]{1,0:T(8,128)(2,1)S(1)} collective-permute-done((bf16[136,4096]{1,0:T(8,128)(2,1)S(1)}, bf16[136,4096]{1,0:T(8,128)(2,1)S(1)}, u32[]{:S(2)}, u32[]{:S(2)}) %collective-permute-start.1) | collective-permute-done | bytes 1114144 | tf_op jit(solution)/shard_map/p1x/ppermute | solution.py:47
  39.2 3.0 %collective-permute-start.8 = (bf16[128,4096]{1,0:T(8,128)(2,1)}, bf16[128,4096]{1,0:T(8,128)(2,1)}, u32[]{:S(2)}, u32[]{:S(2)}) collective-permute-start(bf16[128,4096]{1,0:T(8,128)(2,1)} %b0), channel_id=1, source_target_pairs={{0,2},{1,3},{2,0},{3,1},{4,6},{5,7},{6,4},{7,5},{8,10},{9,11},{10,... | collective-permute-start | bytes 3145736 | tf_op jit(solution)/shard_map/p1g/ppermute | solution.py:47
  46.3 7.6 %select.22 = (bf16[4,72,4096]{2,1,0:T(8,128)(2,1)}, bf16[4,72,4096]{2,1,0:T(8,128)(2,1)}, bf16[4,72,4096]{2,1,0:T(8,128)(2,1)}, bf16[4,72,4096]{2,1,0:T(8,128)(2,1)}) custom-call(bf16[4,288,128]{2,1,0:T(8,128)(2,1)} %get-tuple-element.39.pick_ref, f32[4,288,128]{2,1,0:T(8,128)} %get-tuple-element.40.weight_ref, bf16[136,4096]{1,0:T(8,128)(2,1)} %copy-done.1, ...), custom_call_target="tpu_custom_call" | custom-call | flops 30000001024 | bytes 1 | tf_op jit(solution)/shard_map/select/pallas_call | solution.py:118
  57.2 3.7 %collective-permute-start.5 = (bf16[4,72,4096]{2,1,0:T(8,128)(2,1)}, bf16[4,72,4096]{2,1,0:T(8,128)(2,1)}, u32[]{:S(2)}, u32[]{:S(2)}) collective-permute-start(bf16[4,72,4096]{2,1,0:T(8,128)(2,1)} %get-tuple-element.44), channel_id=1, source_target_pairs={{0,8},{1,9},{2,10},{3,11},{4,12},{5,13},{6,14},{7,15},{8,0},{9,1},... | collective-permute-start | bytes 7077896 | tf_op jit(solution)/shard_map/p2x/ppermute | solution.py:47
  60.9 16.7 %collective-permute-done.7.b2 = bf16[128,4096]{1,0:T(8,128)(2,1)} collective-permute-done((bf16[128,4096]{1,0:T(8,128)(2,1)}, bf16[128,4096]{1,0:T(8,128)(2,1)}, u32[]{:S(2)}, u32[]{:S(2)}) %collective-permute-start.7) | collective-permute-done | bytes 1048608 | tf_op jit(solution)/shard_map/p1g/ppermute | solution.py:47
  77.9 7.7 %select_scaled.1 = (bf16[4,72,4096]{2,1,0:T(8,128)(2,1)}, bf16[4,72,4096]{2,1,0:T(8,128)(2,1)}, bf16[4,72,4096]{2,1,0:T(8,128)(2,1)}, bf16[4,72,4096]{2,1,0:T(8,128)(2,1)}) custom-call(bf16[4,288,128]{2,1,0:T(8,128)(2,1)} %get-tuple-element.39.pick_ref, f32[4,288,128]{2,1,0:T(8,128)} %get-tuple-element.40.weight_ref, bf16[128,4096]{1,0:T(8,128)(2,1)} %b0, ...), custom_call_target="tpu_custom_call" | custom-call | flops 30000001024 | bytes 1 | tf_op jit(solution)/shard_map/select_scaled/pallas_call | solution.py:118
  85.6 2.9 %collective-permute-start.9 = (bf16[4,72,4096]{2,1,0:T(8,128)(2,1)}, bf16[4,72,4096]{2,1,0:T(8,128)(2,1)S(1)}, u32[]{:S(2)}, u32[]{:S(2)}) collective-permute-start(bf16[4,72,4096]{2,1,0:T(8,128)(2,1)} %get-tuple-element.46), channel_id=1, source_target_pairs={{0,4},{1,5},{2,6},{3,7},{4,8},{5,9},{6,10},{7,11},{8,12},{9,13},{1... | collective-permute-start | bytes 7077896 | tf_op jit(solution)/shard_map/p2g/ppermute | solution.py:47
  90.7 25.4 %collective-permute-done.5 = bf16[4,72,4096]{2,1,0:T(8,128)(2,1)} collective-permute-done((bf16[4,72,4096]{2,1,0:T(8,128)(2,1)}, bf16[4,72,4096]{2,1,0:T(8,128)(2,1)}, u32[]{:S(2)}, u32[]{:S(2)}) %collective-permute-start.5) | collective-permute-done | bytes 2359328 | tf_op jit(solution)/shard_map/p2x/ppermute | solution.py:47
  116.1 14.5 %expert_pre.1 = (f32[1152,768]{1,0:T(8,128)}, bf16[768,1152]{1,0:T(8,128)(2,1)}) custom-call(bf16[288,4096]{1,0:T(8,128)(2,1)} %bitcast.42, bf16[288,4096]{1,0:T(8,128)(2,1)} %bitcast.5.refs_1_.x1, bf16[288,4096]{1,0:T(8,128)(2,1)} %bitcast.47, bf16[288,4096]{1,0:T(8,128)(2,1)} %bitcast.7.refs_3_.x3, bf16[4096,768]{1,0:T(8,128)(2,1)} %bitcast.28), custom_call_target="tpu_custom_call" | custom-call | flops 7247757312 | bytes 17498112 | tf_op jit(solution)/shard_map/expert_pre/pallas_call | solution.py:188
  130.6 2.8 collective-permute-start.11
  133.4 12.3 %expert_back.3 = (bf16[288,768]{1,0:T(8,128)(2,1)}, bf16[288,4096]{1,0:T(8,128)(2,1)}) custom-call(bf16[288,4096]{1,0:T(8,128)(2,1)} %bitcast.35, f32[1152,768]{1,0:T(8,128)} %get-tuple-element.48.refs_1_.refs_2_, bf16[768,4096]{1,0:T(8,128)(2,1)} %bitcast.32, bf16[4096,768]{1,0:T(8,128)(2,1)} %bitcast.29), custom_call_target="tpu_custom_call" | custom-call | flops 1000000 | bytes 1 | tf_op jit(solution)/shard_map/expert_back/pallas_call | solution.py:236
  147.1 16.0 %expert_back.4 = (bf16[576,768]{1,0:T(8,128)(2,1)}, bf16[288,4096]{1,0:T(8,128)(2,1)}, bf16[288,4096]{1,0:T(8,128)(2,1)}) custom-call(bf16[288,4096]{1,0:T(8,128)(2,1)} %bitcast.39, bf16[288,4096]{1,0:T(8,128)(2,1)} %bitcast.12.refs_1_.g1, f32[1152,768]{1,0:T(8,128)} %get-tuple-element.48.refs_1_.refs_2_, bf16[768,4096]{1,0:T(8,128)(2,1)} %bitcast.33, ...), custom_call_target="tpu_custom_call" | custom-call | flops 7247757312 | bytes 17498112 | tf_op jit(solution)/shard_map/expert_back/pallas_call | solution.py:236
  167.9 12.4 %down_partial.1 = bf16[768,4096]{1,0:T(8,128)(2,1)} custom-call(bf16[768,1152]{1,0:T(8,128)(2,1)} %get-tuple-element.59.act, bf16[288,4096]{1,0:T(8,128)(2,1)} %bitcast.40, bf16[288,4096]{1,0:T(8,128)(2,1)} %bitcast.12.refs_1_.g1, bf16[288,4096]{1,0:T(8,128)(2,1)} %bitcast.36, bf16[288,4096]{1,0:T(8,128)(2,1)} %bitcast.37), custom_call_target="tpu_custom_call" | custom-call | flops 1000000 | bytes 1 | tf_op jit(solution)/shard_map/down_partial/pallas_call | solution.py:284
  180.4 12.3 %expert_back.5 = (bf16[288,768]{1,0:T(8,128)(2,1)}, bf16[288,4096]{1,0:T(8,128)(2,1)}) custom-call(bf16[288,4096]{1,0:T(8,128)(2,1)} %bitcast.38, f32[1152,768]{1,0:T(8,128)} %get-tuple-element.48.refs_1_.refs_2_, bf16[768,4096]{1,0:T(8,128)(2,1)} %bitcast.34, bf16[4096,768]{1,0:T(8,128)(2,1)} %bitcast.31), custom_call_target="tpu_custom_call" | custom-call | flops 1000000 | bytes 1 | tf_op jit(solution)/shard_map/expert_back/pallas_call | solution.py:236
  195.7 12.7 %up_partial.1 = bf16[4096,768]{1,0:T(8,128)(2,1)} custom-call(bf16[288,4096]{1,0:T(8,128)(2,1)} %bitcast.43, bf16[288,4096]{1,0:T(8,128)(2,1)} %bitcast.5.refs_1_.x1, bf16[288,4096]{1,0:T(8,128)(2,1)} %bitcast.48, bf16[288,4096]{1,0:T(8,128)(2,1)} %bitcast.7.refs_3_.x3, bf16[576,768]{1,0:T(8,128)(2,1)} %get-tuple-element.52.p0, ...), custom_call_target="tpu_custom_call" | custom-call | flops 299999985664 | bytes 1 | tf_op jit(solution)/shard_map/up_partial/pallas_call | solution.py:264
  208.4 15.8 %collective-permute-done.14.r3 = bf16[4,72,4096]{2,1,0:T(8,128)(2,1)} collective-permute-done((bf16[4,72,4096]{2,1,0:T(8,128)(2,1)}, bf16[4,72,4096]{2,1,0:T(8,128)(2,1)}, u32[]{:S(2)}, u32[]{:S(2)}) %collective-permute-start.14) | collective-permute-done | bytes 2359328 | tf_op jit(solution)/shard_map/r2/ppermute | solution.py:47
  224.2 3.2 %reduce-scatter.3.cloned.1.call-done = bf16[96,4096]{1,0:T(8,128)(2,1)} async-done(((bf16[768,4096]{1,0:T(8,128)(2,1)}), bf16[96,4096]{1,0:T(8,128)(2,1)}) %reduce-scatter.3.cloned.1.call-update) | async-done | bytes 786448 | tf_op jit(solution)/shard_map/reduce_scatter | solution.py:346
  227.5 8.2 %combine.1 = (bf16[128,4096]{1,0:T(8,128)(2,1)}, bf16[128,4096]{1,0:T(8,128)(2,1)}, bf16[128,4096]{1,0:T(8,128)(2,1)}, bf16[128,4096]{1,0:T(8,128)(2,1)}) custom-call(bf16[4,4,128,72]{3,2,1,0:T(8,128)(2,1)} %get-tuple-element.63.put_ref, bf16[4,72,4096]{2,1,0:T(8,128)(2,1)} %bitcast.41, bf16[4,72,4096]{2,1,0:T(8,128)(2,1)} %collective-permute-done.12.r1, ...), custom_call_target="tpu_custom_call" | custom-call | flops 1000000 | bytes 1 | tf_op jit(solution)/shard_map/combine/pallas_call | solution.py:146
  235.7 2.7 collective-permute-start.15
  240.7 21.6 %collective-permute-done.15 = bf16[128,4096]{1,0:T(8,128)(2,1)S(1)} collective-permute-done((bf16[128,4096]{1,0:T(8,128)(2,1)}, bf16[128,4096]{1,0:T(8,128)(2,1)S(1)}, u32[]{:S(2)}, u32[]{:S(2)}) %collective-permute-start.15) | collective-permute-done | bytes 1048608 | tf_op jit(solution)/shard_map/r1/ppermute | solution.py:47
  262.3 3.6 %collective-permute-done.16 = bf16[128,4096]{1,0:T(8,128)(2,1)S(1)} collective-permute-done((bf16[128,4096]{1,0:T(8,128)(2,1)}, bf16[128,4096]{1,0:T(8,128)(2,1)S(1)}, u32[]{:S(2)}, u32[]{:S(2)}) %collective-permute-start.16) | collective-permute-done | bytes 1048608 | tf_op jit(solution)/shard_map/r1/ppermute | solution.py:47
  265.8 2.9 %add_convert_fusion = bf16[128,4096]{1,0:T(8,128)(2,1)} fusion(bf16[128,4096]{1,0:T(8,128)(2,1)S(1)} %collective-permute-done.17, bf16[128,4096]{1,0:T(8,128)(2,1)S(1)} %collective-permute-done.16, bf16[128,4096]{1,0:T(8,128)(2,1)S(1)} %collective-permute-done.15, bf16[128,4096]{1,0:T(8,128)(2,1)} %get-tuple-element.66), kind=kLoop, calls=%fused_computation | loop fusion | flops 4194304 | bytes 5242880 | tf_op jit(solution)/shard_map/convert_element_type | solution.py:360
  (50 shorter events, 33.2 us)
Async XLA Ops:
  7.2 220.3 %reduce-scatter.3.cloned.1.call-start = ((), (), s32[]{:S(2)}) async-start(), calls=%async_computation.2 | async-start | bytes 7077888 | tf_op jit(solution)/shard_map/reduce_scatter | solution.py:346
  9.9 34.3 %copy-start.1 = (bf16[136,4096]{1,0:T(8,128)(2,1)}, bf16[136,4096]{1,0:T(8,128)(2,1)S(1)}, u32[]{:S(2)}) copy-start(bf16[136,4096]{1,0:T(8,128)(2,1)S(1)} %pad_maximum_fusion.m0.b0) | copy-start | bytes 3342340
  9.9 17.2 %collective-permute-start.2 = (bf16[136,4096]{1,0:T(8,128)(2,1)S(1)}, bf16[136,4096]{1,0:T(8,128)(2,1)S(1)}, u32[]{:S(2)}, u32[]{:S(2)}) collective-permute-start(bf16[136,4096]{1,0:T(8,128)(2,1)S(1)} %pad_maximum_fusion.m0.b0), channel_id=1, source_target_pairs={{0,2},{1,3},{2,0},{3,1},{4,6},{5,7},{6,4},{7,5},{8,10},{9,11},{10,... | collective-permute-start | bytes 3342344 | tf_op jit(solution)/shard_map/p1x/ppermute | solution.py:47
  13.1 26.0 %collective-permute-start.1 = (bf16[136,4096]{1,0:T(8,128)(2,1)S(1)}, bf16[136,4096]{1,0:T(8,128)(2,1)S(1)}, u32[]{:S(2)}, u32[]{:S(2)}) collective-permute-start(bf16[136,4096]{1,0:T(8,128)(2,1)S(1)} %pad_maximum_fusion.m0.b0), channel_id=1, source_target_pairs={{0,3},{1,0},{2,1},{3,2},{4,7},{5,4},{6,5},{7,6},{8,11},{9,8},{10,9... | collective-permute-start | bytes 3342344 | tf_op jit(solution)/shard_map/p1x/ppermute | solution.py:47
  14.2 24.9 %collective-permute-start = (bf16[136,4096]{1,0:T(8,128)(2,1)S(1)}, bf16[136,4096]{1,0:T(8,128)(2,1)}, u32[]{:S(2)}, u32[]{:S(2)}) collective-permute-start(bf16[136,4096]{1,0:T(8,128)(2,1)S(1)} %pad_maximum_fusion.m0.b0), channel_id=1, source_target_pairs={{0,1},{1,2},{2,3},{3,0},{4,5},{5,6},{6,7},{7,4},{8,9},{9,10},{10,1... | collective-permute-start | bytes 3342344 | tf_op jit(solution)/shard_map/p1x/ppermute | solution.py:47
  27.1 17.1 %copy-start.3 = (bf16[136,4096]{1,0:T(8,128)(2,1)}, bf16[136,4096]{1,0:T(8,128)(2,1)S(1)}, u32[]{:S(2)}) copy-start(bf16[136,4096]{1,0:T(8,128)(2,1)S(1)} %collective-permute-done.2.m3.b3) | copy-start | bytes 3342340
  39.1 5.0 %copy-start.4 = (bf16[136,4096]{1,0:T(8,128)(2,1)}, bf16[136,4096]{1,0:T(8,128)(2,1)S(1)}, u32[]{:S(2)}) copy-start(bf16[136,4096]{1,0:T(8,128)(2,1)S(1)} %collective-permute-done.1.m2.b2) | copy-start | bytes 3342340
  39.2 18.0 %collective-permute-start.8 = (bf16[128,4096]{1,0:T(8,128)(2,1)}, bf16[128,4096]{1,0:T(8,128)(2,1)}, u32[]{:S(2)}, u32[]{:S(2)}) collective-permute-start(bf16[128,4096]{1,0:T(8,128)(2,1)} %b0), channel_id=1, source_target_pairs={{0,2},{1,3},{2,0},{3,1},{4,6},{5,7},{6,4},{7,5},{8,10},{9,11},{10,... | collective-permute-start | bytes 3145736 | tf_op jit(solution)/shard_map/p1g/ppermute | solution.py:47
  42.1 35.4 %collective-permute-start.7 = (bf16[128,4096]{1,0:T(8,128)(2,1)}, bf16[128,4096]{1,0:T(8,128)(2,1)}, u32[]{:S(2)}, u32[]{:S(2)}) collective-permute-start(bf16[128,4096]{1,0:T(8,128)(2,1)} %b0), channel_id=1, source_target_pairs={{0,3},{1,0},{2,1},{3,2},{4,7},{5,4},{6,5},{7,6},{8,11},{9,8},{10,9... | collective-permute-start | bytes 3145736 | tf_op jit(solution)/shard_map/p1g/ppermute | solution.py:47
  43.4 34.5 %collective-permute-start.6 = (bf16[128,4096]{1,0:T(8,128)(2,1)}, bf16[128,4096]{1,0:T(8,128)(2,1)}, u32[]{:S(2)}, u32[]{:S(2)}) collective-permute-start(bf16[128,4096]{1,0:T(8,128)(2,1)} %b0), channel_id=1, source_target_pairs={{0,1},{1,2},{2,3},{3,0},{4,5},{5,6},{6,7},{7,4},{8,9},{9,10},{10,1... | collective-permute-start | bytes 3145736 | tf_op jit(solution)/shard_map/p1g/ppermute | solution.py:47
  54.0 36.6 %collective-permute-start.3 = (bf16[4,72,4096]{2,1,0:T(8,128)(2,1)}, bf16[4,72,4096]{2,1,0:T(8,128)(2,1)S(1)}, u32[]{:S(2)}, u32[]{:S(2)}) collective-permute-start(bf16[4,72,4096]{2,1,0:T(8,128)(2,1)} %get-tuple-element.41), channel_id=1, source_target_pairs={{0,4},{1,5},{2,6},{3,7},{4,8},{5,9},{6,10},{7,11},{8,12},{9,13},{1... | collective-permute-start | bytes 7077896 | tf_op jit(solution)/shard_map/p2x/ppermute | solution.py:47
  55.5 35.1 %collective-permute-start.4 = (bf16[4,72,4096]{2,1,0:T(8,128)(2,1)}, bf16[4,72,4096]{2,1,0:T(8,128)(2,1)}, u32[]{:S(2)}, u32[]{:S(2)}) collective-permute-start(bf16[4,72,4096]{2,1,0:T(8,128)(2,1)} %get-tuple-element.42), channel_id=1, source_target_pairs={{0,12},{1,13},{2,14},{3,15},{4,0},{5,1},{6,2},{7,3},{8,4},{9,5},{1... | collective-permute-start | bytes 7077896 | tf_op jit(solution)/shard_map/p2x/ppermute | solution.py:47
  57.2 58.9 %collective-permute-start.5 = (bf16[4,72,4096]{2,1,0:T(8,128)(2,1)}, bf16[4,72,4096]{2,1,0:T(8,128)(2,1)}, u32[]{:S(2)}, u32[]{:S(2)}) collective-permute-start(bf16[4,72,4096]{2,1,0:T(8,128)(2,1)} %get-tuple-element.44), channel_id=1, source_target_pairs={{0,8},{1,9},{2,10},{3,11},{4,12},{5,13},{6,14},{7,15},{8,0},{9,1},... | collective-permute-start | bytes 7077896 | tf_op jit(solution)/shard_map/p2x/ppermute | solution.py:47
  85.6 60.2 %collective-permute-start.9 = (bf16[4,72,4096]{2,1,0:T(8,128)(2,1)}, bf16[4,72,4096]{2,1,0:T(8,128)(2,1)S(1)}, u32[]{:S(2)}, u32[]{:S(2)}) collective-permute-start(bf16[4,72,4096]{2,1,0:T(8,128)(2,1)} %get-tuple-element.46), channel_id=1, source_target_pairs={{0,4},{1,5},{2,6},{3,7},{4,8},{5,9},{6,10},{7,11},{8,12},{9,13},{1... | collective-permute-start | bytes 7077896 | tf_op jit(solution)/shard_map/p2g/ppermute | solution.py:47
  88.4 57.3 %collective-permute-start.10 = (bf16[4,72,4096]{2,1,0:T(8,128)(2,1)}, bf16[4,72,4096]{2,1,0:T(8,128)(2,1)}, u32[]{:S(2)}, u32[]{:S(2)}) collective-permute-start(bf16[4,72,4096]{2,1,0:T(8,128)(2,1)} %get-tuple-element.51), channel_id=1, source_target_pairs={{0,12},{1,13},{2,14},{3,15},{4,0},{5,1},{6,2},{7,3},{8,4},{9,5},{1... | collective-permute-start | bytes 7077896 | tf_op jit(solution)/shard_map/p2g/ppermute | solution.py:47
  90.6 25.5 %copy-start.6 = (bf16[4,72,4096]{2,1,0:T(8,128)(2,1)}, bf16[4,72,4096]{2,1,0:T(8,128)(2,1)S(1)}, u32[]{:S(2)}) copy-start(bf16[4,72,4096]{2,1,0:T(8,128)(2,1)S(1)} %collective-permute-done.3) | copy-start | bytes 7077892
  130.6 35.9 %collective-permute-start.11 = (bf16[4,72,4096]{2,1,0:T(8,128)(2,1)}, bf16[4,72,4096]{2,1,0:T(8,128)(2,1)S(1)}, u32[]{:S(2)}, u32[]{:S(2)}) collective-permute-start(bf16[4,72,4096]{2,1,0:T(8,128)(2,1)} %get-tuple-element.55), channel_id=1, source_target_pairs={{0,8},{1,9},{2,10},{3,11},{4,12},{5,13},{6,14},{7,15},{8,0},{9,1},... | collective-permute-start | bytes 7077896 | tf_op jit(solution)/shard_map/p2g2/ppermute | solution.py:47
  163.2 30.4 %collective-permute-start.13 = (bf16[4,72,4096]{2,1,0:T(8,128)(2,1)}, bf16[4,72,4096]{2,1,0:T(8,128)(2,1)}, u32[]{:S(2)}, u32[]{:S(2)}) collective-permute-start(bf16[4,72,4096]{2,1,0:T(8,128)(2,1)} %bitcast.45), channel_id=1, source_target_pairs={{0,4},{1,5},{2,6},{3,7},{4,8},{5,9},{6,10},{7,11},{8,12},{9,13},{1... | collective-permute-start | bytes 7077896 | tf_op jit(solution)/shard_map/r2/ppermute | solution.py:47
  163.8 29.7 %collective-permute-start.12 = (bf16[4,72,4096]{2,1,0:T(8,128)(2,1)}, bf16[4,72,4096]{2,1,0:T(8,128)(2,1)}, u32[]{:S(2)}, u32[]{:S(2)}) collective-permute-start(bf16[4,72,4096]{2,1,0:T(8,128)(2,1)} %bitcast.44), channel_id=1, source_target_pairs={{0,12},{1,13},{2,14},{3,15},{4,0},{5,1},{6,2},{7,3},{8,4},{9,5},{1... | collective-permute-start | bytes 7077896 | tf_op jit(solution)/shard_map/r2/ppermute | solution.py:47
  180.4 91.7 %reduce-scatter.5.cloned.1.call-start = ((), (), s32[]{:S(2)}) async-start(), calls=%async_computation.3 | async-start | bytes 7077888 | tf_op jit(solution)/shard_map/reduce_scatter | solution.py:355
  193.5 30.7 %collective-permute-start.14 = (bf16[4,72,4096]{2,1,0:T(8,128)(2,1)}, bf16[4,72,4096]{2,1,0:T(8,128)(2,1)}, u32[]{:S(2)}, u32[]{:S(2)}) collective-permute-start(bf16[4,72,4096]{2,1,0:T(8,128)(2,1)} %bitcast.46), channel_id=1, source_target_pairs={{0,8},{1,9},{2,10},{3,11},{4,12},{5,13},{6,14},{7,15},{8,0},{9,1},... | collective-permute-start | bytes 7077896 | tf_op jit(solution)/shard_map/r2/ppermute | solution.py:47
  235.7 26.6 %collective-permute-start.15 = (bf16[128,4096]{1,0:T(8,128)(2,1)}, bf16[128,4096]{1,0:T(8,128)(2,1)S(1)}, u32[]{:S(2)}, u32[]{:S(2)}) collective-permute-start(bf16[128,4096]{1,0:T(8,128)(2,1)} %get-tuple-element.67), channel_id=1, source_target_pairs={{0,3},{1,0},{2,1},{3,2},{4,7},{5,4},{6,5},{7,6},{8,11},{9,8},{10,9... | collective-permute-start | bytes 3145736 | tf_op jit(solution)/shard_map/r1/ppermute | solution.py:47
  238.4 27.5 %collective-permute-start.16 = (bf16[128,4096]{1,0:T(8,128)(2,1)}, bf16[128,4096]{1,0:T(8,128)(2,1)S(1)}, u32[]{:S(2)}, u32[]{:S(2)}) collective-permute-start(bf16[128,4096]{1,0:T(8,128)(2,1)} %get-tuple-element.68), channel_id=1, source_target_pairs={{0,1},{1,2},{2,3},{3,0},{4,5},{5,6},{6,7},{7,4},{8,9},{9,10},{10,1... | collective-permute-start | bytes 3145736 | tf_op jit(solution)/shard_map/r1/ppermute | solution.py:47
  238.4 27.5 %collective-permute-start.17 = (bf16[128,4096]{1,0:T(8,128)(2,1)}, bf16[128,4096]{1,0:T(8,128)(2,1)S(1)}, u32[]{:S(2)}, u32[]{:S(2)}) collective-permute-start(bf16[128,4096]{1,0:T(8,128)(2,1)} %get-tuple-element.69), channel_id=1, source_target_pairs={{0,2},{1,3},{2,0},{3,1},{4,6},{5,7},{6,4},{7,5},{8,10},{9,11},{10,... | collective-permute-start | bytes 3145736 | tf_op jit(solution)/shard_map/r1/ppermute | solution.py:47
  (3 other events, 5.8 us)
Sparse Core Ops, SparseCore 0:
  180.5 46.8 reduce-scatter.2
  229.8 42.1 reduce-scatter.4

commit v9 on v8

--- a/solution.py
+++ b/solution.py
@@ -232,20 +232,21 @@
 
 def expert_back(gs, pre, place, down, up):
     n, (width, hidden) = len(gs), up.shape
-    tiles = width // TILE
+    tile = 2 * TILE
+    tiles = width // tile
     out = pl.pallas_call(
         functools.partial(back_kernel, n),
         out_shape=(jax.ShapeDtypeStruct((n * ROWS, hidden), jnp.bfloat16),)
         + (jax.ShapeDtypeStruct((ROWS, width), jnp.bfloat16),) * n,
         grid=(2 * tiles,),
-        in_specs=[pl.BlockSpec((ROWS, TILE), lambda c: (0, jnp.minimum(c, tiles - 1)))] * n
+        in_specs=[pl.BlockSpec((ROWS, tile), lambda c: (0, jnp.minimum(c, tiles - 1)))] * n
         + [
             pl.BlockSpec((n * ROWS, hidden), lambda c: (place, 0)),
-            pl.BlockSpec((hidden, TILE), lambda c: (0, jnp.minimum(c, tiles - 1))),
-            pl.BlockSpec((TILE, hidden), lambda c: (jnp.maximum(c - tiles, 0), 0)),
+            pl.BlockSpec((hidden, tile), lambda c: (0, jnp.minimum(c, tiles - 1))),
+            pl.BlockSpec((tile, hidden), lambda c: (jnp.maximum(c - tiles, 0), 0)),
         ],
         out_specs=(pl.BlockSpec((n * ROWS, hidden), lambda c: (0, 0)),)
-        + (pl.BlockSpec((ROWS, TILE), lambda c: (0, jnp.maximum(c - tiles, 0))),) * n,
+        + (pl.BlockSpec((ROWS, tile), lambda c: (0, jnp.maximum(c - tiles, 0))),) * n,
         scratch_shapes=[pltpu.VMEM((n * ROWS, hidden), jnp.float32)],
         compiler_params=PARAMS,
         cost_estimate=cost(2 * n * ROWS, width, hidden) if n > 1 else LIGHT,

time: 282 us -> 282 us (level)
  Pallas kernels: 106 us -> 103 us
    pallas_call x3, Pallas kernels: 40.7 us -> 37.5 us  [expert_back(): pl.pallas_call(functools.partial(back_kernel, n), out_shape=(jax.ShapeDty...]
  transfers between devices with their start and end apart: 20 -> 20, of which waited for: 14 -> 14; matrix products, arithmetic and copies ran while one was open for 2% -> 2% of each run, Pallas kernels for 38% -> 37%
where the time goes in v9:
time: 282 us; the launch traced here: 281 us
  waiting for transfers between devices  116 us (41%)
  Pallas kernels  103 us (37%)
  starting transfers between devices  35 us (12%)
  between operations  14.1 us (5%)
  other arithmetic  10.5 us (4%)
  local copies, waits for them, and re-layouts  2.87 us (1%)
    ppermute x18, waiting for transfers between devices, send(): lax.ppermute(value, BOTH, ring(first, shift))  109 us
    pallas_call x3, Pallas kernels, expert_back(): pl.pallas_call(functools.partial(back_kernel, n), out_shape=(jax.ShapeDty...  37.5 us
    ppermute x18, starting transfers between devices, send(): lax.ppermute(value, BOTH, ring(first, shift))  34.7 us
    pallas_call x2, Pallas kernels, select(): pl.pallas_call(functools.partial(select_kernel, scaled), out_shape=(jax.S...  15.3 us
    pallas_call x1, Pallas kernels, expert_pre(): pl.pallas_call(pre_kernel, out_shape=(jax.ShapeDtypeStruct((WIDE + ROWS,...  14.5 us
    pallas_call x1, Pallas kernels, up_partial(): pl.pallas_call(up_kernel, out_shape=jax.ShapeDtypeStruct((width, hidden),...  12.7 us
    pallas_call x1, Pallas kernels, down_partial(): pl.pallas_call(down_kernel, out_shape=jax.ShapeDtypeStruct((hidden, width...  12.4 us
    pallas_call x1, Pallas kernels, combine(): pl.pallas_call(combine_kernel, out_shape=(jax.ShapeDtypeStruct((128, widt...  8.22 us
  transfers between devices with their start and end apart: 20, of which 14 were waited for; matrix products, arithmetic and copies ran while one was open for 2% of the time, Pallas kernels for 37%

profile of v9, /device:TPU:0, one launch (start us, length us, event | category | flops | bytes accessed | tf_op | source)
XLA Modules:
  0.0 281.1 jit_solution(17887948961797301379)
XLA Ops:
  9.9 3.2 %collective-permute-start.2 = (bf16[136,4096]{1,0:T(8,128)(2,1)S(1)}, bf16[136,4096]{1,0:T(8,128)(2,1)S(1)}, u32[]{:S(2)}, u32[]{:S(2)}) collective-permute-start(bf16[136,4096]{1,0:T(8,128)(2,1)S(1)} %pad_maximum_fusion.m0.b0), channel_id=1, source_target_pairs={{0,2},{1,3},{2,0},{3,1},{4,6},{5,7},{6,4},{7,5},{8,10},{9,11},{10,... | collective-permute-start | bytes 3342344 | tf_op jit(solution)/shard_map/p1x/ppermute | solution.py:47
  16.4 10.7 %collective-permute-done.2.m3.b3 = bf16[136,4096]{1,0:T(8,128)(2,1)S(1)} collective-permute-done((bf16[136,4096]{1,0:T(8,128)(2,1)S(1)}, bf16[136,4096]{1,0:T(8,128)(2,1)S(1)}, u32[]{:S(2)}, u32[]{:S(2)}) %collective-permute-start.2) | collective-permute-done | bytes 1114144 | tf_op jit(solution)/shard_map/p1x/ppermute | solution.py:47
  27.1 12.0 %collective-permute-done.1.m2.b2 = bf16[136,4096]{1,0:T(8,128)(2,1)S(1)} collective-permute-done((bf16[136,4096]{1,0:T(8,128)(2,1)S(1)}, bf16[136,4096]{1,0:T(8,128)(2,1)S(1)}, u32[]{:S(2)}, u32[]{:S(2)}) %collective-permute-start.1) | collective-permute-done | bytes 1114144 | tf_op jit(solution)/shard_map/p1x/ppermute | solution.py:47
  39.2 3.0 %collective-permute-start.8 = (bf16[128,4096]{1,0:T(8,128)(2,1)}, bf16[128,4096]{1,0:T(8,128)(2,1)}, u32[]{:S(2)}, u32[]{:S(2)}) collective-permute-start(bf16[128,4096]{1,0:T(8,128)(2,1)} %b0), channel_id=1, source_target_pairs={{0,2},{1,3},{2,0},{3,1},{4,6},{5,7},{6,4},{7,5},{8,10},{9,11},{10,... | collective-permute-start | bytes 3145736 | tf_op jit(solution)/shard_map/p1g/ppermute | solution.py:47
  46.3 7.6 %select.22 = (bf16[4,72,4096]{2,1,0:T(8,128)(2,1)}, bf16[4,72,4096]{2,1,0:T(8,128)(2,1)}, bf16[4,72,4096]{2,1,0:T(8,128)(2,1)}, bf16[4,72,4096]{2,1,0:T(8,128)(2,1)}) custom-call(bf16[4,288,128]{2,1,0:T(8,128)(2,1)} %get-tuple-element.39.pick_ref, f32[4,288,128]{2,1,0:T(8,128)} %get-tuple-element.40.weight_ref, bf16[136,4096]{1,0:T(8,128)(2,1)} %copy-done.1, ...), custom_call_target="tpu_custom_call" | custom-call | flops 30000001024 | bytes 1 | tf_op jit(solution)/shard_map/select/pallas_call | solution.py:118
  57.2 3.7 %collective-permute-start.5 = (bf16[4,72,4096]{2,1,0:T(8,128)(2,1)}, bf16[4,72,4096]{2,1,0:T(8,128)(2,1)}, u32[]{:S(2)}, u32[]{:S(2)}) collective-permute-start(bf16[4,72,4096]{2,1,0:T(8,128)(2,1)} %get-tuple-element.44), channel_id=1, source_target_pairs={{0,8},{1,9},{2,10},{3,11},{4,12},{5,13},{6,14},{7,15},{8,0},{9,1},... | collective-permute-start | bytes 7077896 | tf_op jit(solution)/shard_map/p2x/ppermute | solution.py:47
  60.9 16.7 %collective-permute-done.7.b2 = bf16[128,4096]{1,0:T(8,128)(2,1)} collective-permute-done((bf16[128,4096]{1,0:T(8,128)(2,1)}, bf16[128,4096]{1,0:T(8,128)(2,1)}, u32[]{:S(2)}, u32[]{:S(2)}) %collective-permute-start.7) | collective-permute-done | bytes 1048608 | tf_op jit(solution)/shard_map/p1g/ppermute | solution.py:47
  77.9 7.7 %select_scaled.1 = (bf16[4,72,4096]{2,1,0:T(8,128)(2,1)}, bf16[4,72,4096]{2,1,0:T(8,128)(2,1)}, bf16[4,72,4096]{2,1,0:T(8,128)(2,1)}, bf16[4,72,4096]{2,1,0:T(8,128)(2,1)}) custom-call(bf16[4,288,128]{2,1,0:T(8,128)(2,1)} %get-tuple-element.39.pick_ref, f32[4,288,128]{2,1,0:T(8,128)} %get-tuple-element.40.weight_ref, bf16[128,4096]{1,0:T(8,128)(2,1)} %b0, ...), custom_call_target="tpu_custom_call" | custom-call | flops 30000001024 | bytes 1 | tf_op jit(solution)/shard_map/select_scaled/pallas_call | solution.py:118
  85.6 2.9 %collective-permute-start.9 = (bf16[4,72,4096]{2,1,0:T(8,128)(2,1)}, bf16[4,72,4096]{2,1,0:T(8,128)(2,1)S(1)}, u32[]{:S(2)}, u32[]{:S(2)}) collective-permute-start(bf16[4,72,4096]{2,1,0:T(8,128)(2,1)} %get-tuple-element.46), channel_id=1, source_target_pairs={{0,4},{1,5},{2,6},{3,7},{4,8},{5,9},{6,10},{7,11},{8,12},{9,13},{1... | collective-permute-start | bytes 7077896 | tf_op jit(solution)/shard_map/p2g/ppermute | solution.py:47
  90.7 25.4 %collective-permute-done.5 = bf16[4,72,4096]{2,1,0:T(8,128)(2,1)} collective-permute-done((bf16[4,72,4096]{2,1,0:T(8,128)(2,1)}, bf16[4,72,4096]{2,1,0:T(8,128)(2,1)}, u32[]{:S(2)}, u32[]{:S(2)}) %collective-permute-start.5) | collective-permute-done | bytes 2359328 | tf_op jit(solution)/shard_map/p2x/ppermute | solution.py:47
  116.1 14.5 %expert_pre.1 = (f32[1152,768]{1,0:T(8,128)}, bf16[768,1152]{1,0:T(8,128)(2,1)}) custom-call(bf16[288,4096]{1,0:T(8,128)(2,1)} %bitcast.42, bf16[288,4096]{1,0:T(8,128)(2,1)} %bitcast.5.refs_1_.x1, bf16[288,4096]{1,0:T(8,128)(2,1)} %bitcast.47, bf16[288,4096]{1,0:T(8,128)(2,1)} %bitcast.7.refs_3_.x3, bf16[4096,768]{1,0:T(8,128)(2,1)} %bitcast.28), custom_call_target="tpu_custom_call" | custom-call | flops 7247757312 | bytes 17498112 | tf_op jit(solution)/shard_map/expert_pre/pallas_call | solution.py:188
  130.6 2.8 collective-permute-start.11
  133.4 11.1 %expert_back.3 = (bf16[288,768]{1,0:T(8,128)(2,1)}, bf16[288,4096]{1,0:T(8,128)(2,1)}) custom-call(bf16[288,4096]{1,0:T(8,128)(2,1)} %bitcast.35, f32[1152,768]{1,0:T(8,128)} %get-tuple-element.48.refs_1_.refs_2_, bf16[768,4096]{1,0:T(8,128)(2,1)} %bitcast.32, bf16[4096,768]{1,0:T(8,128)(2,1)} %bitcast.29), custom_call_target="tpu_custom_call" | custom-call | flops 1000000 | bytes 1 | tf_op jit(solution)/shard_map/expert_back/pallas_call | solution.py:237
  145.9 15.3 %expert_back.4 = (bf16[576,768]{1,0:T(8,128)(2,1)}, bf16[288,4096]{1,0:T(8,128)(2,1)}, bf16[288,4096]{1,0:T(8,128)(2,1)}) custom-call(bf16[288,4096]{1,0:T(8,128)(2,1)} %bitcast.39, bf16[288,4096]{1,0:T(8,128)(2,1)} %bitcast.12.refs_1_.g1, f32[1152,768]{1,0:T(8,128)} %get-tuple-element.48.refs_1_.refs_2_, bf16[768,4096]{1,0:T(8,128)(2,1)} %bitcast.33, ...), custom_call_target="tpu_custom_call" | custom-call | flops 7247757312 | bytes 17498112 | tf_op jit(solution)/shard_map/expert_back/pallas_call | solution.py:237
  168.0 12.4 %down_partial.1 = bf16[768,4096]{1,0:T(8,128)(2,1)} custom-call(bf16[768,1152]{1,0:T(8,128)(2,1)} %get-tuple-element.59.act, bf16[288,4096]{1,0:T(8,128)(2,1)} %bitcast.40, bf16[288,4096]{1,0:T(8,128)(2,1)} %bitcast.12.refs_1_.g1, bf16[288,4096]{1,0:T(8,128)(2,1)} %bitcast.36, bf16[288,4096]{1,0:T(8,128)(2,1)} %bitcast.37), custom_call_target="tpu_custom_call" | custom-call | flops 1000000 | bytes 1 | tf_op jit(solution)/shard_map/down_partial/pallas_call | solution.py:285
  180.7 11.1 %expert_back.5 = (bf16[288,768]{1,0:T(8,128)(2,1)}, bf16[288,4096]{1,0:T(8,128)(2,1)}) custom-call(bf16[288,4096]{1,0:T(8,128)(2,1)} %bitcast.38, f32[1152,768]{1,0:T(8,128)} %get-tuple-element.48.refs_1_.refs_2_, bf16[768,4096]{1,0:T(8,128)(2,1)} %bitcast.34, bf16[4096,768]{1,0:T(8,128)(2,1)} %bitcast.31), custom_call_target="tpu_custom_call" | custom-call | flops 1000000 | bytes 1 | tf_op jit(solution)/shard_map/expert_back/pallas_call | solution.py:237
  191.9 2.9 %collective-permute-start.14 = (bf16[4,72,4096]{2,1,0:T(8,128)(2,1)}, bf16[4,72,4096]{2,1,0:T(8,128)(2,1)}, u32[]{:S(2)}, u32[]{:S(2)}) collective-permute-start(bf16[4,72,4096]{2,1,0:T(8,128)(2,1)} %bitcast.46), channel_id=1, source_target_pairs={{0,8},{1,9},{2,10},{3,11},{4,12},{5,13},{6,14},{7,15},{8,0},{9,1},... | collective-permute-start | bytes 7077896 | tf_op jit(solution)/shard_map/r2/ppermute | solution.py:47
  194.7 12.7 %up_partial.1 = bf16[4096,768]{1,0:T(8,128)(2,1)} custom-call(bf16[288,4096]{1,0:T(8,128)(2,1)} %bitcast.43, bf16[288,4096]{1,0:T(8,128)(2,1)} %bitcast.5.refs_1_.x1, bf16[288,4096]{1,0:T(8,128)(2,1)} %bitcast.48, bf16[288,4096]{1,0:T(8,128)(2,1)} %bitcast.7.refs_3_.x3, bf16[576,768]{1,0:T(8,128)(2,1)} %get-tuple-element.52.p0, ...), custom_call_target="tpu_custom_call" | custom-call | flops 299999985664 | bytes 1 | tf_op jit(solution)/shard_map/up_partial/pallas_call | solution.py:265
  207.4 15.1 %collective-permute-done.14.r3 = bf16[4,72,4096]{2,1,0:T(8,128)(2,1)} collective-permute-done((bf16[4,72,4096]{2,1,0:T(8,128)(2,1)}, bf16[4,72,4096]{2,1,0:T(8,128)(2,1)}, u32[]{:S(2)}, u32[]{:S(2)}) %collective-permute-start.14) | collective-permute-done | bytes 2359328 | tf_op jit(solution)/shard_map/r2/ppermute | solution.py:47
  222.5 5.0 %reduce-scatter.3.cloned.1.call-done = bf16[96,4096]{1,0:T(8,128)(2,1)} async-done(((bf16[768,4096]{1,0:T(8,128)(2,1)}), bf16[96,4096]{1,0:T(8,128)(2,1)}) %reduce-scatter.3.cloned.1.call-update) | async-done | bytes 786448 | tf_op jit(solution)/shard_map/reduce_scatter | solution.py:347
  227.6 8.2 %combine.1 = (bf16[128,4096]{1,0:T(8,128)(2,1)}, bf16[128,4096]{1,0:T(8,128)(2,1)}, bf16[128,4096]{1,0:T(8,128)(2,1)}, bf16[128,4096]{1,0:T(8,128)(2,1)}) custom-call(bf16[4,4,128,72]{3,2,1,0:T(8,128)(2,1)} %get-tuple-element.63.put_ref, bf16[4,72,4096]{2,1,0:T(8,128)(2,1)} %bitcast.41, bf16[4,72,4096]{2,1,0:T(8,128)(2,1)} %collective-permute-done.12.r1, ...), custom_call_target="tpu_custom_call" | custom-call | flops 1000000 | bytes 1 | tf_op jit(solution)/shard_map/combine/pallas_call | solution.py:146
  240.8 21.6 %collective-permute-done.15 = bf16[128,4096]{1,0:T(8,128)(2,1)S(1)} collective-permute-done((bf16[128,4096]{1,0:T(8,128)(2,1)}, bf16[128,4096]{1,0:T(8,128)(2,1)S(1)}, u32[]{:S(2)}, u32[]{:S(2)}) %collective-permute-start.15) | collective-permute-done | bytes 1048608 | tf_op jit(solution)/shard_map/r1/ppermute | solution.py:47
  262.4 3.6 %collective-permute-done.16 = bf16[128,4096]{1,0:T(8,128)(2,1)S(1)} collective-permute-done((bf16[128,4096]{1,0:T(8,128)(2,1)}, bf16[128,4096]{1,0:T(8,128)(2,1)S(1)}, u32[]{:S(2)}, u32[]{:S(2)}) %collective-permute-start.16) | collective-permute-done | bytes 1048608 | tf_op jit(solution)/shard_map/r1/ppermute | solution.py:47
  266.0 3.0 %add_convert_fusion = bf16[128,4096]{1,0:T(8,128)(2,1)} fusion(bf16[128,4096]{1,0:T(8,128)(2,1)S(1)} %collective-permute-done.17, bf16[128,4096]{1,0:T(8,128)(2,1)S(1)} %collective-permute-done.16, bf16[128,4096]{1,0:T(8,128)(2,1)S(1)} %collective-permute-done.15, bf16[128,4096]{1,0:T(8,128)(2,1)} %get-tuple-element.66), kind=kLoop, calls=%fused_computation | loop fusion | flops 4194304 | bytes 5242880 | tf_op jit(solution)/shard_map/convert_element_type | solution.py:361
  (50 shorter events, 34.9 us)
Async XLA Ops:
  7.2 220.4 %reduce-scatter.3.cloned.1.call-start = ((), (), s32[]{:S(2)}) async-start(), calls=%async_computation.2 | async-start | bytes 7077888 | tf_op jit(solution)/shard_map/reduce_scatter | solution.py:347
  9.9 34.3 %copy-start.1 = (bf16[136,4096]{1,0:T(8,128)(2,1)}, bf16[136,4096]{1,0:T(8,128)(2,1)S(1)}, u32[]{:S(2)}) copy-start(bf16[136,4096]{1,0:T(8,128)(2,1)S(1)} %pad_maximum_fusion.m0.b0) | copy-start | bytes 3342340
  9.9 17.2 %collective-permute-start.2 = (bf16[136,4096]{1,0:T(8,128)(2,1)S(1)}, bf16[136,4096]{1,0:T(8,128)(2,1)S(1)}, u32[]{:S(2)}, u32[]{:S(2)}) collective-permute-start(bf16[136,4096]{1,0:T(8,128)(2,1)S(1)} %pad_maximum_fusion.m0.b0), channel_id=1, source_target_pairs={{0,2},{1,3},{2,0},{3,1},{4,6},{5,7},{6,4},{7,5},{8,10},{9,11},{10,... | collective-permute-start | bytes 3342344 | tf_op jit(solution)/shard_map/p1x/ppermute | solution.py:47
  13.1 26.0 %collective-permute-start.1 = (bf16[136,4096]{1,0:T(8,128)(2,1)S(1)}, bf16[136,4096]{1,0:T(8,128)(2,1)S(1)}, u32[]{:S(2)}, u32[]{:S(2)}) collective-permute-start(bf16[136,4096]{1,0:T(8,128)(2,1)S(1)} %pad_maximum_fusion.m0.b0), channel_id=1, source_target_pairs={{0,3},{1,0},{2,1},{3,2},{4,7},{5,4},{6,5},{7,6},{8,11},{9,8},{10,9... | collective-permute-start | bytes 3342344 | tf_op jit(solution)/shard_map/p1x/ppermute | solution.py:47
  14.2 24.9 %collective-permute-start = (bf16[136,4096]{1,0:T(8,128)(2,1)S(1)}, bf16[136,4096]{1,0:T(8,128)(2,1)}, u32[]{:S(2)}, u32[]{:S(2)}) collective-permute-start(bf16[136,4096]{1,0:T(8,128)(2,1)S(1)} %pad_maximum_fusion.m0.b0), channel_id=1, source_target_pairs={{0,1},{1,2},{2,3},{3,0},{4,5},{5,6},{6,7},{7,4},{8,9},{9,10},{10,1... | collective-permute-start | bytes 3342344 | tf_op jit(solution)/shard_map/p1x/ppermute | solution.py:47
  27.1 17.1 %copy-start.3 = (bf16[136,4096]{1,0:T(8,128)(2,1)}, bf16[136,4096]{1,0:T(8,128)(2,1)S(1)}, u32[]{:S(2)}) copy-start(bf16[136,4096]{1,0:T(8,128)(2,1)S(1)} %collective-permute-done.2.m3.b3) | copy-start | bytes 3342340
  39.1 5.0 %copy-start.4 = (bf16[136,4096]{1,0:T(8,128)(2,1)}, bf16[136,4096]{1,0:T(8,128)(2,1)S(1)}, u32[]{:S(2)}) copy-start(bf16[136,4096]{1,0:T(8,128)(2,1)S(1)} %collective-permute-done.1.m2.b2) | copy-start | bytes 3342340
  39.2 18.0 %collective-permute-start.8 = (bf16[128,4096]{1,0:T(8,128)(2,1)}, bf16[128,4096]{1,0:T(8,128)(2,1)}, u32[]{:S(2)}, u32[]{:S(2)}) collective-permute-start(bf16[128,4096]{1,0:T(8,128)(2,1)} %b0), channel_id=1, source_target_pairs={{0,2},{1,3},{2,0},{3,1},{4,6},{5,7},{6,4},{7,5},{8,10},{9,11},{10,... | collective-permute-start | bytes 3145736 | tf_op jit(solution)/shard_map/p1g/ppermute | solution.py:47
  42.1 35.4 %collective-permute-start.7 = (bf16[128,4096]{1,0:T(8,128)(2,1)}, bf16[128,4096]{1,0:T(8,128)(2,1)}, u32[]{:S(2)}, u32[]{:S(2)}) collective-permute-start(bf16[128,4096]{1,0:T(8,128)(2,1)} %b0), channel_id=1, source_target_pairs={{0,3},{1,0},{2,1},{3,2},{4,7},{5,4},{6,5},{7,6},{8,11},{9,8},{10,9... | collective-permute-start | bytes 3145736 | tf_op jit(solution)/shard_map/p1g/ppermute | solution.py:47
  43.4 34.5 %collective-permute-start.6 = (bf16[128,4096]{1,0:T(8,128)(2,1)}, bf16[128,4096]{1,0:T(8,128)(2,1)}, u32[]{:S(2)}, u32[]{:S(2)}) collective-permute-start(bf16[128,4096]{1,0:T(8,128)(2,1)} %b0), channel_id=1, source_target_pairs={{0,1},{1,2},{2,3},{3,0},{4,5},{5,6},{6,7},{7,4},{8,9},{9,10},{10,1... | collective-permute-start | bytes 3145736 | tf_op jit(solution)/shard_map/p1g/ppermute | solution.py:47
  54.0 36.6 %collective-permute-start.3 = (bf16[4,72,4096]{2,1,0:T(8,128)(2,1)}, bf16[4,72,4096]{2,1,0:T(8,128)(2,1)S(1)}, u32[]{:S(2)}, u32[]{:S(2)}) collective-permute-start(bf16[4,72,4096]{2,1,0:T(8,128)(2,1)} %get-tuple-element.41), channel_id=1, source_target_pairs={{0,4},{1,5},{2,6},{3,7},{4,8},{5,9},{6,10},{7,11},{8,12},{9,13},{1... | collective-permute-start | bytes 7077896 | tf_op jit(solution)/shard_map/p2x/ppermute | solution.py:47
  55.5 35.1 %collective-permute-start.4 = (bf16[4,72,4096]{2,1,0:T(8,128)(2,1)}, bf16[4,72,4096]{2,1,0:T(8,128)(2,1)}, u32[]{:S(2)}, u32[]{:S(2)}) collective-permute-start(bf16[4,72,4096]{2,1,0:T(8,128)(2,1)} %get-tuple-element.42), channel_id=1, source_target_pairs={{0,12},{1,13},{2,14},{3,15},{4,0},{5,1},{6,2},{7,3},{8,4},{9,5},{1... | collective-permute-start | bytes 7077896 | tf_op jit(solution)/shard_map/p2x/ppermute | solution.py:47
  57.2 58.9 %collective-permute-start.5 = (bf16[4,72,4096]{2,1,0:T(8,128)(2,1)}, bf16[4,72,4096]{2,1,0:T(8,128)(2,1)}, u32[]{:S(2)}, u32[]{:S(2)}) collective-permute-start(bf16[4,72,4096]{2,1,0:T(8,128)(2,1)} %get-tuple-element.44), channel_id=1, source_target_pairs={{0,8},{1,9},{2,10},{3,11},{4,12},{5,13},{6,14},{7,15},{8,0},{9,1},... | collective-permute-start | bytes 7077896 | tf_op jit(solution)/shard_map/p2x/ppermute | solution.py:47
  85.6 59.0 %collective-permute-start.9 = (bf16[4,72,4096]{2,1,0:T(8,128)(2,1)}, bf16[4,72,4096]{2,1,0:T(8,128)(2,1)S(1)}, u32[]{:S(2)}, u32[]{:S(2)}) collective-permute-start(bf16[4,72,4096]{2,1,0:T(8,128)(2,1)} %get-tuple-element.46), channel_id=1, source_target_pairs={{0,4},{1,5},{2,6},{3,7},{4,8},{5,9},{6,10},{7,11},{8,12},{9,13},{1... | collective-permute-start | bytes 7077896 | tf_op jit(solution)/shard_map/p2g/ppermute | solution.py:47
  88.4 56.1 %collective-permute-start.10 = (bf16[4,72,4096]{2,1,0:T(8,128)(2,1)}, bf16[4,72,4096]{2,1,0:T(8,128)(2,1)}, u32[]{:S(2)}, u32[]{:S(2)}) collective-permute-start(bf16[4,72,4096]{2,1,0:T(8,128)(2,1)} %get-tuple-element.51), channel_id=1, source_target_pairs={{0,12},{1,13},{2,14},{3,15},{4,0},{5,1},{6,2},{7,3},{8,4},{9,5},{1... | collective-permute-start | bytes 7077896 | tf_op jit(solution)/shard_map/p2g/ppermute | solution.py:47
  90.6 25.5 %copy-start.6 = (bf16[4,72,4096]{2,1,0:T(8,128)(2,1)}, bf16[4,72,4096]{2,1,0:T(8,128)(2,1)S(1)}, u32[]{:S(2)}) copy-start(bf16[4,72,4096]{2,1,0:T(8,128)(2,1)S(1)} %collective-permute-done.3) | copy-start | bytes 7077892
  130.6 35.9 %collective-permute-start.11 = (bf16[4,72,4096]{2,1,0:T(8,128)(2,1)}, bf16[4,72,4096]{2,1,0:T(8,128)(2,1)S(1)}, u32[]{:S(2)}, u32[]{:S(2)}) collective-permute-start(bf16[4,72,4096]{2,1,0:T(8,128)(2,1)} %get-tuple-element.55), channel_id=1, source_target_pairs={{0,8},{1,9},{2,10},{3,11},{4,12},{5,13},{6,14},{7,15},{8,0},{9,1},... | collective-permute-start | bytes 7077896 | tf_op jit(solution)/shard_map/p2g2/ppermute | solution.py:47
  161.2 30.7 %collective-permute-start.13 = (bf16[4,72,4096]{2,1,0:T(8,128)(2,1)}, bf16[4,72,4096]{2,1,0:T(8,128)(2,1)}, u32[]{:S(2)}, u32[]{:S(2)}) collective-permute-start(bf16[4,72,4096]{2,1,0:T(8,128)(2,1)} %bitcast.45), channel_id=1, source_target_pairs={{0,4},{1,5},{2,6},{3,7},{4,8},{5,9},{6,10},{7,11},{8,12},{9,13},{1... | collective-permute-start | bytes 7077896 | tf_op jit(solution)/shard_map/r2/ppermute | solution.py:47
  161.9 30.0 %collective-permute-start.12 = (bf16[4,72,4096]{2,1,0:T(8,128)(2,1)}, bf16[4,72,4096]{2,1,0:T(8,128)(2,1)}, u32[]{:S(2)}, u32[]{:S(2)}) collective-permute-start(bf16[4,72,4096]{2,1,0:T(8,128)(2,1)} %bitcast.44), channel_id=1, source_target_pairs={{0,12},{1,13},{2,14},{3,15},{4,0},{5,1},{6,2},{7,3},{8,4},{9,5},{1... | collective-permute-start | bytes 7077896 | tf_op jit(solution)/shard_map/r2/ppermute | solution.py:47
  180.4 91.5 %reduce-scatter.5.cloned.1.call-start = ((), (), s32[]{:S(2)}) async-start(), calls=%async_computation.3 | async-start | bytes 7077888 | tf_op jit(solution)/shard_map/reduce_scatter | solution.py:356
  191.9 30.7 %collective-permute-start.14 = (bf16[4,72,4096]{2,1,0:T(8,128)(2,1)}, bf16[4,72,4096]{2,1,0:T(8,128)(2,1)}, u32[]{:S(2)}, u32[]{:S(2)}) collective-permute-start(bf16[4,72,4096]{2,1,0:T(8,128)(2,1)} %bitcast.46), channel_id=1, source_target_pairs={{0,8},{1,9},{2,10},{3,11},{4,12},{5,13},{6,14},{7,15},{8,0},{9,1},... | collective-permute-start | bytes 7077896 | tf_op jit(solution)/shard_map/r2/ppermute | solution.py:47
  235.8 26.6 %collective-permute-start.15 = (bf16[128,4096]{1,0:T(8,128)(2,1)}, bf16[128,4096]{1,0:T(8,128)(2,1)S(1)}, u32[]{:S(2)}, u32[]{:S(2)}) collective-permute-start(bf16[128,4096]{1,0:T(8,128)(2,1)} %get-tuple-element.67), channel_id=1, source_target_pairs={{0,3},{1,0},{2,1},{3,2},{4,7},{5,4},{6,5},{7,6},{8,11},{9,8},{10,9... | collective-permute-start | bytes 3145736 | tf_op jit(solution)/shard_map/r1/ppermute | solution.py:47
  238.5 27.5 %collective-permute-start.16 = (bf16[128,4096]{1,0:T(8,128)(2,1)}, bf16[128,4096]{1,0:T(8,128)(2,1)S(1)}, u32[]{:S(2)}, u32[]{:S(2)}) collective-permute-start(bf16[128,4096]{1,0:T(8,128)(2,1)} %get-tuple-element.68), channel_id=1, source_target_pairs={{0,1},{1,2},{2,3},{3,0},{4,5},{5,6},{6,7},{7,4},{8,9},{9,10},{10,1... | collective-permute-start | bytes 3145736 | tf_op jit(solution)/shard_map/r1/ppermute | solution.py:47
  238.5 27.5 %collective-permute-start.17 = (bf16[128,4096]{1,0:T(8,128)(2,1)}, bf16[128,4096]{1,0:T(8,128)(2,1)S(1)}, u32[]{:S(2)}, u32[]{:S(2)}) collective-permute-start(bf16[128,4096]{1,0:T(8,128)(2,1)} %get-tuple-element.69), channel_id=1, source_target_pairs={{0,2},{1,3},{2,0},{3,1},{4,6},{5,7},{6,4},{7,5},{8,10},{9,11},{10,... | collective-permute-start | bytes 3145736 | tf_op jit(solution)/shard_map/r1/ppermute | solution.py:47
  (3 other events, 5.8 us)
Sparse Core Ops, SparseCore 0:
  180.5 46.9 reduce-scatter.2
  230.0 41.8 reduce-scatter.4
